TPU v7x, 32 devices: a whole 2x2x4 slice. The times are simulated.
32 devices in a mesh: seq: 8 (over z, x), head: 4 (over y, core).
Axes of the slice: x: 2, y: 2, z: 4, core: 2. Of those that a mesh axis runs over, the one named last changes fastest.
Arguments:
- block_input: bfloat16 [1024, 1024], P('seq', 'head'), may hold values from -6 to 6
- mixer_gain: bfloat16 [1024], P('head'), may hold values from 0.5 to 1.5
- proj_weight: bfloat16 [1024, 8, 512], P(None, 'head'), may hold values from -0.1875 to 0.1875
- rate_weight: bfloat16 [1024, 8, 2], P(None, 'head'), may hold values from -0.1875 to 0.1875
- conv_weight: float32 [4, 8, 384], P(None, 'head'), may hold values from -3 to 3
- decay_log: float32 [8], P('head'), may hold values from -13 to -3
- decay_bias: float32 [8], P('head'), may hold values from -2 to 1
- write_bias: float32 [8], P('head'), may hold values from -6 to -2
- output_gain: float32 [8, 128], P('head'), may hold values from 0.5 to 1.5
- merge_weight: bfloat16 [1024, 1024], P('head'), may hold values from -0.375 to 0.375
- feed_gain: bfloat16 [1024], P('head'), may hold values from 0.5 to 1.5
- gateup_weight: bfloat16 [1024, 2, 2816], P(None, None, 'head'), may hold values from -0.1875 to 0.1875
- down_weight: bfloat16 [2816, 1024], P('head'), may hold values from -0.21875 to 0.21875
- output_grad: bfloat16 [1024, 1024], P('seq', 'head'), may hold values from -6 to 6
Outputs:
- block_output: float32 [1024, 1024], P('seq', 'head')
- input_grad: float32 [1024, 1024], P('seq', 'head')
- mixer_gain_grad: float32 [1024], P('head')
- proj_weight_grad: float32 [1024, 8, 512], P('seq', 'head')
- rate_weight_grad: float32 [1024, 8, 2], P('seq', 'head')
- conv_weight_grad: float32 [4, 8, 384], P(None, 'head', 'seq')
- decay_log_grad: float32 [8], P('head')
- decay_bias_grad: float32 [8], P('head')
- write_bias_grad: float32 [8], P('head')
- output_gain_grad: float32 [8, 128], P('head', 'seq')
- merge_weight_grad: float32 [1024, 1024], P('head', 'seq')
- feed_gain_grad: float32 [1024], P('head')
- gateup_weight_grad: float32 [1024, 2, 2816], P('seq', None, 'head')
- down_weight_grad: float32 [2816, 1024], P('head', 'seq')
All inputs are finite; a program needn't handle non-finite values.
Results may differ from a plain program's by a relative error of at most 0.015.
Values may be sent and summed in bfloat16 or wider, within the bound.
No kernel may reach another device: no remote copies, remote signals or barrier semaphores. Data moves between devices by JAX's collectives and lax.ppermute only.
A program may use at most 128 MiB of HBM per device.

v0:
```python
import jax
import jax.numpy as jnp
from jax import lax
from jax.sharding import PartitionSpec as P

CONV = 4
GROUP = 64
SEQS = 1


EPSILON = 1e-06
HIGH = lax.Precision.HIGHEST


def passed_along(value, axis, steps):
    count = lax.axis_size(axis)
    first, last = (max(0, -steps), min(count, count - steps))
    return lax.ppermute(value, axis, [(source, source + steps) for source in range(first, last)])


def rms_scale(rows):
    return lax.rsqrt(jnp.mean(rows * rows, axis=-1, keepdims=True) + EPSILON)


def lower_solve(system, target):
    return jax.scipy.linalg.solve_triangular(system, target, lower=True, unit_diagonal=True)


def group_setup(key_rows, value_rows, write_rate, log_decay):
    length = log_decay.shape[-1]
    position = jnp.arange(length)
    causal = position[None, :] <= position[:, None]
    strict = position[None, :] < position[:, None]
    cum_decay = jnp.cumsum(log_decay, axis=-1)
    decay_gap = cum_decay[:, :, None] - cum_decay[:, None, :]
    decays = jnp.where(causal, jnp.exp(jnp.where(causal, decay_gap, 0.0)), 0.0)
    key_inner = jnp.einsum("hcd,hsd->hcs", key_rows, key_rows, precision=HIGH)
    system = jnp.eye(length, dtype=jnp.float32) + jnp.where(
        strict, write_rate[:, :, None] * decays * key_inner, 0.0
    )
    growth = jnp.exp(cum_decay)
    weights = lower_solve(system, (write_rate * growth)[:, :, None] * key_rows)
    values = lower_solve(system, write_rate[:, :, None] * value_rows)
    remain = jnp.exp(cum_decay[:, -1:] - cum_decay)
    return (cum_decay, decays, growth, weights, values, remain)


def group_outputs(queries, key_rows, value_rows, write_rate, log_decay, memory):
    cum_decay, decays, growth, weights, values, remain = group_setup(
        key_rows, value_rows, write_rate, log_decay
    )
    updates = values - jnp.einsum("hck,hvk->hcv", weights, memory, precision=HIGH)
    scores = decays * jnp.einsum("hcd,hsd->hcs", queries, key_rows, precision=HIGH)
    outputs = growth[:, :, None] * jnp.einsum("hck,hvk->hcv", queries, memory, precision=HIGH)
    outputs = outputs + jnp.einsum("hcs,hsv->hcv", scores, updates, precision=HIGH)
    memory_next = jnp.exp(cum_decay[:, -1])[:, None, None] * memory
    memory_next = memory_next + jnp.einsum(
        "hcv,hc,hck->hvk", updates, remain, key_rows, precision=HIGH
    )
    return (outputs, memory_next)


def group_effect(key_rows, value_rows, write_rate, log_decay):
    cum_decay, decays, growth, weights, values, remain = group_setup(
        key_rows, value_rows, write_rate, log_decay
    )
    identity = jnp.eye(key_rows.shape[-1], dtype=jnp.float32)
    carried = jnp.exp(cum_decay[:, -1])[:, None, None] * identity
    carried = carried - jnp.einsum("hck,hc,hce->hke", weights, remain, key_rows, precision=HIGH)
    added = jnp.einsum("hcv,hc,hck->hvk", values, remain, key_rows, precision=HIGH)
    return (carried, added)


def to_blocks(array):
    number = array.shape[0] // GROUP
    shaped = array.reshape((number, GROUP) + array.shape[1:])
    return jnp.moveaxis(shaped, 1, 2)


def run_memory(queries, key_rows, value_rows, write_rate, log_decay, memory):

    def advance(memory, pieces):
        outputs, memory_next = group_outputs(*pieces, memory)
        return (memory_next, outputs)

    blocks = tuple(
        (to_blocks(element) for element in (queries, key_rows, value_rows, write_rate, log_decay))
    )
    memory_end, outputs = lax.scan(advance, memory, blocks)
    outputs = jnp.moveaxis(outputs, 2, 1).reshape(value_rows.shape)
    return (outputs, memory_end)


def front_part(extended, rates, conv_weight, decay_log, decay_bias, write_bias):
    length = rates.shape[0]
    kernel_taps = conv_weight.shape[0]
    mixed = extended[:length] * conv_weight[0]
    for offset in range(1, kernel_taps):
        mixed = mixed + extended[offset : offset + length] * conv_weight[offset]
    mixed = jax.nn.silu(mixed)
    head_dim = conv_weight.shape[-1] // 3
    queries = mixed[..., :head_dim]
    key_rows = mixed[..., head_dim : 2 * head_dim]
    value_rows = mixed[..., 2 * head_dim :]
    queries = (
        queries
        * lax.rsqrt(jnp.sum(queries * queries, axis=-1, keepdims=True) + EPSILON)
        * head_dim ** (-0.5)
    )
    key_rows = key_rows * lax.rsqrt(jnp.sum(key_rows * key_rows, axis=-1, keepdims=True) + EPSILON)
    write_rate = jax.nn.sigmoid(rates[..., 0] + write_bias)
    log_decay = -jnp.exp(decay_log) * jax.nn.softplus(rates[..., 1] + decay_bias)
    return (queries, key_rows, value_rows, write_rate, log_decay)


def back_part(queries, key_rows, value_rows, write_rate, log_decay, gate_rows, output_gain, memory):
    outputs, memory_end = run_memory(queries, key_rows, value_rows, write_rate, log_decay, memory)
    normed = outputs * rms_scale(outputs) * output_gain * jax.nn.silu(gate_rows)
    return (normed, memory_end)


def compose(earlier, later):
    joined = jnp.einsum("hij,hjk->hik", earlier[0], later[0], precision=HIGH)
    shifted = jnp.einsum("hij,hjk->hik", earlier[1], later[0], precision=HIGH) + later[1]
    return (joined, shifted)


def on_device(
    block_input,
    mixer_gain,
    proj_weight,
    rate_weight,
    conv_weight,
    decay_log,
    decay_bias,
    write_bias,
    output_gain,
    merge_weight,
    feed_gain,
    gateup_weight,
    down_weight,
    output_grad,
):
    inputs_full, gain_one, gain_two, grads_full = (
        lax.all_gather(block_input, "head", axis=1, tiled=True),
        lax.all_gather(mixer_gain, "head", axis=0, tiled=True),
        lax.all_gather(feed_gain, "head", axis=0, tiled=True),
        lax.all_gather(output_grad, "head", axis=1, tiled=True),
    )
    local_width = block_input.shape[1]
    part = lax.axis_index("head")
    ranks = lax.axis_size("seq")
    rank = lax.axis_index("seq")
    span = ranks // SEQS
    opening = rank % span == 0
    closing = rank % span == span - 1
    model_width = inputs_full.shape[1]
    inputs = inputs_full.astype(jnp.float32)
    scale_one = rms_scale(inputs)
    gain_one = gain_one.astype(jnp.float32)
    gain_two = gain_two.astype(jnp.float32)
    normed_in = (inputs * scale_one * gain_one).astype(jnp.bfloat16)
    projected = jnp.einsum(
        "td,dhe->the", normed_in, proj_weight, preferred_element_type=jnp.float32
    )
    head_dim = proj_weight.shape[2] // 4
    local_heads = proj_weight.shape[1]
    conv_rows = projected[..., : 3 * head_dim].astype(jnp.bfloat16)
    gate_rows = projected[..., 3 * head_dim :]
    rates = jnp.einsum("td,dhe->the", normed_in, rate_weight, preferred_element_type=jnp.float32)
    edge_rows = passed_along(conv_rows[-(CONV - 1) :], "seq", 1)
    edge_rows = jnp.where(opening, jnp.zeros_like(edge_rows), edge_rows)
    extended = jnp.concatenate([edge_rows, conv_rows], axis=0).astype(jnp.float32)
    features, front_pull = jax.vjp(
        front_part, extended, rates, conv_weight, decay_log, decay_bias, write_bias
    )
    identity_stack = jnp.broadcast_to(
        jnp.eye(head_dim, dtype=jnp.float32), (local_heads, head_dim, head_dim)
    )
    zero_stack = jnp.zeros((local_heads, head_dim, head_dim), jnp.float32)

    def summarize(carry, pieces):
        carried, added = group_effect(*pieces)
        transfer, offset = carry
        return (compose((transfer, offset), (carried, added)), 0)

    blocks_in = tuple((to_blocks(element) for element in features[1:]))
    (transfer_raw, offset), unused = lax.scan(summarize, (identity_stack, zero_stack), blocks_in)
    transfer = jnp.where(opening, 0.0, transfer_raw)
    all_transfer, all_offset = (
        lax.all_gather(transfer[None], "seq", axis=0, tiled=True),
        lax.all_gather(offset[None], "seq", axis=0, tiled=True),
    )

    def absorb(index, memory):
        return (
            jnp.einsum("hij,hjk->hik", memory, all_transfer[index], precision=HIGH)
            + all_offset[index]
        )

    incoming = lax.fori_loop(0, rank, absorb, zero_stack)
    incoming = jnp.where(opening, 0.0, incoming)
    (normed, memory_end), back_pull = jax.vjp(
        back_part, *features, gate_rows, output_gain, incoming
    )
    mixed_rows = normed.astype(jnp.bfloat16).reshape(normed.shape[0], local_heads * head_dim)
    all_rows, all_weight = (
        lax.all_gather(mixed_rows, "head", axis=1, tiled=True),
        lax.all_gather(merge_weight, "head", axis=0, tiled=True),
    )
    mixer_out = jnp.dot(all_rows, all_weight, preferred_element_type=jnp.float32)
    resid = inputs + mixer_out
    scale_two = rms_scale(resid)
    feed_in = (resid * scale_two * gain_two).astype(jnp.bfloat16)
    gateup = jnp.einsum("td,dcf->tcf", feed_in, gateup_weight, preferred_element_type=jnp.float32)
    gate_part = gateup[:, 0]
    up_part = gateup[:, 1]
    hidden = (jax.nn.silu(gate_part) * up_part).astype(jnp.bfloat16)
    feed_part = jnp.dot(hidden, down_weight, preferred_element_type=jnp.float32)
    feed_out = lax.psum_scatter(
        feed_part.astype(jnp.bfloat16), "head", scatter_dimension=1, tiled=True
    ).astype(jnp.float32)
    mine_resid = lax.dynamic_slice_in_dim(resid, part * local_width, local_width, 1)
    block_output = mine_resid + feed_out
    grad_hidden = jnp.einsum(
        "td,fd->tf", grads_full, down_weight, preferred_element_type=jnp.float32
    )
    grad_down = jnp.einsum("tf,td->fd", hidden, grads_full, preferred_element_type=jnp.float32)
    sigma = jax.nn.sigmoid(gate_part)
    grad_gate = grad_hidden * up_part * sigma * (1.0 + gate_part * (1.0 - sigma))
    grad_up = grad_hidden * gate_part * sigma
    grad_gateup_rows = jnp.stack([grad_gate, grad_up], axis=1).astype(jnp.bfloat16)
    grad_gateup = jnp.einsum(
        "td,tcf->dcf", feed_in, grad_gateup_rows, preferred_element_type=jnp.float32
    )
    grad_feed_part = jnp.einsum(
        "tcf,dcf->td", grad_gateup_rows, gateup_weight, preferred_element_type=jnp.float32
    )
    grad_feed_in = lax.psum(grad_feed_part, "head")
    mine_feed_grad = lax.dynamic_slice_in_dim(grad_feed_in, part * local_width, local_width, 1)
    grad_gain_two = jnp.sum(mine_feed_grad * mine_resid * scale_two, axis=0)
    weighted = grad_feed_in * gain_two
    grad_resid = (
        grads_full.astype(jnp.float32)
        + scale_two * weighted
        - resid * scale_two**3 * jnp.mean(weighted * resid, axis=-1, keepdims=True)
    )
    grad_resid_half = grad_resid.astype(jnp.bfloat16)
    grad_merge = jnp.einsum(
        "tk,td->kd", mixed_rows, grad_resid_half, preferred_element_type=jnp.float32
    )
    grad_mixed = jnp.einsum(
        "td,kd->tk", grad_resid_half, merge_weight, preferred_element_type=jnp.float32
    )
    grad_mixed = grad_mixed.reshape(normed.shape)
    first_pass = back_pull((grad_mixed, jnp.zeros_like(memory_end)))
    local_state = first_pass[7]
    reverse_transfer = jnp.where(closing, 0.0, jnp.swapaxes(transfer_raw, 1, 2))
    all_reverse, all_state = (
        lax.all_gather(
            reverse_transfer[None].astype(jnp.bfloat16), "seq", axis=0, tiled=True
        ).astype(jnp.float32),
        lax.all_gather(local_state[None].astype(jnp.bfloat16), "seq", axis=0, tiled=True).astype(
            jnp.float32
        ),
    )

    def absorb_back(index, memory):
        source = ranks - 1 - index
        return (
            jnp.einsum("hij,hjk->hik", memory, all_reverse[source], precision=HIGH)
            + all_state[source]
        )

    outgoing = lax.fori_loop(0, ranks - 1 - rank, absorb_back, zero_stack)
    outgoing = jnp.where(closing, 0.0, outgoing)
    second_pass = back_pull((jnp.zeros_like(grad_mixed), outgoing))
    totals = jax.tree.map(jnp.add, first_pass, second_pass)
    grad_extended, grad_rates, grad_conv, grad_decay_log, grad_decay_bias, grad_write_bias = (
        front_pull(tuple(totals[:5]))
    )
    grad_gate_rows = totals[5]
    grad_output_gain = totals[6]
    edge_grads = passed_along(grad_extended[: CONV - 1], "seq", -1)
    edge_grads = jnp.where(closing, jnp.zeros_like(edge_grads), edge_grads)
    own_rows = grad_extended[CONV - 1 :]
    grad_conv_rows = jnp.concatenate(
        [own_rows[: -(CONV - 1)], own_rows[-(CONV - 1) :] + edge_grads], axis=0
    )
    grad_proj_rows = jnp.concatenate([grad_conv_rows, grad_gate_rows], axis=-1).astype(jnp.bfloat16)
    grad_rates_half = grad_rates.astype(jnp.bfloat16)
    grad_proj = jnp.einsum(
        "td,the->dhe", normed_in, grad_proj_rows, preferred_element_type=jnp.float32
    )
    grad_rate = jnp.einsum(
        "td,the->dhe", normed_in, grad_rates_half, preferred_element_type=jnp.float32
    )
    grad_normed_part = jnp.einsum(
        "the,dhe->td", grad_proj_rows, proj_weight, preferred_element_type=jnp.float32
    )
    grad_normed_part = grad_normed_part + jnp.einsum(
        "the,dhe->td", grad_rates_half, rate_weight, preferred_element_type=jnp.float32
    )
    stat_part = jnp.sum(grad_normed_part * gain_one * inputs, axis=-1)
    stat_rows = jnp.broadcast_to(stat_part[None, :], (lax.axis_size("head"), stat_part.shape[0]))
    grad_normed, stat_total = (
        lax.psum_scatter(
            grad_normed_part.astype(jnp.bfloat16), "head", scatter_dimension=1, tiled=True
        ).astype(jnp.float32),
        lax.psum_scatter(
            stat_rows.astype(jnp.bfloat16), "head", scatter_dimension=0, tiled=True
        ).astype(jnp.float32),
    )
    mine_inputs = lax.dynamic_slice_in_dim(inputs, part * local_width, local_width, 1)
    mine_gain = lax.dynamic_slice_in_dim(gain_one, part * local_width, local_width, 0)
    mine_resid_grad = lax.dynamic_slice_in_dim(grad_resid, part * local_width, local_width, 1)
    grad_gain_one = jnp.sum(grad_normed * mine_inputs * scale_one, axis=0)
    input_grad = (
        mine_resid_grad
        + scale_one * grad_normed * mine_gain
        - mine_inputs * scale_one**3 * (stat_total[0][:, None] / model_width)
    )
    summed = (
        lax.psum_scatter(
            grad_proj.astype(jnp.bfloat16), "seq", scatter_dimension=0, tiled=True
        ).astype(jnp.float32),
        lax.psum_scatter(
            grad_rate.astype(jnp.bfloat16), "seq", scatter_dimension=0, tiled=True
        ).astype(jnp.float32),
        lax.psum_scatter(
            grad_conv.astype(jnp.bfloat16), "seq", scatter_dimension=2, tiled=True
        ).astype(jnp.float32),
        lax.psum_scatter(
            grad_output_gain.astype(jnp.bfloat16), "seq", scatter_dimension=1, tiled=True
        ).astype(jnp.float32),
        lax.psum_scatter(
            grad_merge.astype(jnp.bfloat16), "seq", scatter_dimension=1, tiled=True
        ).astype(jnp.float32),
        lax.psum_scatter(
            grad_gateup.astype(jnp.bfloat16), "seq", scatter_dimension=0, tiled=True
        ).astype(jnp.float32),
        lax.psum_scatter(
            grad_down.astype(jnp.bfloat16), "seq", scatter_dimension=1, tiled=True
        ).astype(jnp.float32),
    )
    small_sums = lax.psum(
        (grad_gain_one, grad_gain_two, grad_decay_log, grad_decay_bias, grad_write_bias), "seq"
    )
    return (
        block_output,
        input_grad,
        small_sums[0],
        summed[0],
        summed[1],
        summed[2],
        small_sums[2],
        small_sums[3],
        small_sums[4],
        summed[3],
        summed[4],
        small_sums[1],
        summed[5],
        summed[6],
    )


def solution(mesh):
    return jax.shard_map(
        on_device,
        mesh=mesh,
        in_specs=(
            P("seq", "head"),
            P("head"),
            P(None, "head", None),
            P(None, "head", None),
            P(None, "head", None),
            P("head"),
            P("head"),
            P("head"),
            P("head", None),
            P("head", None),
            P("head"),
            P(None, None, "head"),
            P("head", None),
            P("seq", "head"),
        ),
        out_specs=(
            P("seq", "head"),
            P("seq", "head"),
            P("head"),
            P("seq", "head", None),
            P("seq", "head", None),
            P(None, "head", "seq"),
            P("head"),
            P("head"),
            P("head"),
            P("head", "seq"),
            P("head", "seq"),
            P("head"),
            P("seq", None, "head"),
            P("head", "seq"),
        ),
        check_vma=False,
    )
```

profile of v0, /device:TPU:0, one launch (start us, length us, event | category | flops | bytes accessed | tf_op | source)
XLA Modules:
  0.0 1080.6 jit_solution(13610740234095488584)
XLA Ops:
  7.3 7.6 all_gather.30
  15.6 5.1 all-gather.4
  21.4 2.9 fusion.378
  24.9 3.4 collective-permute-start
  34.7 32.9 %while.153 = (s32[]{:T(128)}, f32[2,128,128]{1,2,0:T(8,128)}, f32[2,128,128]{1,2,0:T(8,128)}, f32[2,2,64]{2,1,0:T(2,128)}, f32[2,2,64]{2,1,0:T(2,128)S(1)}, /*in...) while((s32[]{:T(128)}, f32[2,128,128]{1,2,0:T(8,128)}, ...), condition=%wide.region_4.6_spmd.clone, body=%wide.region_2.5_spmd.clone.sunk | while | flops 189083840 | bytes 2474687 | solution.py:188
  36.3 9.8 custom-call.43
  52.3 9.8 custom-call.43
  73.3 5.1 all-gather.5
  79.0 7.7 all_gather.37
  89.6 20.8 %all-gather.12.cloned.1.call-done = f32[16,128,128]{2,1,0:T(8,128)} async-done(((f32[2,128,128]{2,1,0:T(8,128)}), f32[16,128,128]{2,1,0:T(8,128)}) %all-gather.12.cloned.1.call-update) | async-done | bytes 1048592 | tf_op jit(solution)/shard_map/all_gather | solution.py:191
  110.4 41.7 %all-gather.14.cloned.1.call-done = f32[16,128,128]{2,1,0:T(8,128)} async-done(((f32[2,128,128]{2,1,0:T(8,128)}), f32[16,128,128]{2,1,0:T(8,128)}) %all-gather.14.cloned.1.call-update) | async-done | bytes 1048592 | tf_op jit(solution)/shard_map/all_gather | solution.py:192
  159.6 76.7 %while.151 = (s32[]{:T(128)}, f32[2,128,128]{2,1,0:T(8,128)S(1)}, f32[2,2,64,128]{3,2,1,0:T(8,128)}, f32[2,2,64,64]{3,2,1,0:T(8,128)}, f32[2,2,64,64]{3,2,1,0:T(...) while((s32[]{:T(128)}, f32[2,128,128]{2,1,0:T(8,128)S(1)}, ...), condition=%wide.region_10.12_spmd.clone.clone, body=%wide.region_8.11_spmd.clone.clone.sunk | while | flops 138826176 | bytes 3589617 | solution.py:89
  169.3 11.2 %custom-call.41 = f32[2,1,64,64]{2,3,1,0:T(8,128)} custom-call(f32[2,1,64,64]{3,2,1,0:T(8,128)} %get-tuple-element.4352), custom_call_target="InvertDiagBlocksLowerTriangular" | custom-call | tf_op jit(solution)/shard_map/jvp()/while/body/eval_jaxpr/jit(_solve_triangular)/vmap()/triangular_solve/custom-call.1 | solution.py:26
  207.7 11.2 %custom-call.41 = f32[2,1,64,64]{2,3,1,0:T(8,128)} custom-call(f32[2,1,64,64]{3,2,1,0:T(8,128)} %get-tuple-element.4352), custom_call_target="InvertDiagBlocksLowerTriangular" | custom-call | tf_op jit(solution)/shard_map/jvp()/while/body/eval_jaxpr/jit(_solve_triangular)/vmap()/triangular_solve/custom-call.1 | solution.py:26
  243.4 7.5 all_gather.34
  250.9 2.2 multiply_reduce_fusion.4
  261.8 71.8 %all-gather.2 = bf16[16,128,128]{2,1,0:T(8,128)(2,1)S(1)} all-gather(bf16[2,128,128]{2,1,0:T(8,128)(2,1)} %copy.265), channel_id=4, replica_groups=mesh['seq'=8,'head'=4] {'seq'}, dimensions={0}, use_global_device_ids=true | all-gather | bytes 589824 | tf_op jit(solution)/shard_map/all_gather | solution.py:260
  341.1 2.4 multiply_reduce_fusion.12
  349.8 68.1 %while.154 = (s32[]{:T(128)}, f32[2,128,128]{2,1,0:T(8,128)S(1)}, f32[2,2,64,128]{3,2,1,0:T(8,128)}, f32[2,2,64,128]{3,2,1,0:T(8,128)}, f32[2,2,64,128]{3,2,1,0:...) while((s32[]{:T(128)}, f32[2,128,128]{2,1,0:T(8,128)S(1)}, ...), condition=%wide.region_27.30_spmd.clone.clone, body=%wide.region_17.29_spmd.clone.clone.sunk | while | flops 290255936 | bytes 13738772 | solution.py:89
  355.1 10.6 custom-call.44
  389.2 10.6 custom-call.44
  417.8 31.5 %all-gather.3 = bf16[16,128,128]{2,1,0:T(8,128)(2,1)S(1)} all-gather(bf16[2,128,128]{2,1,0:T(8,128)(2,1)S(1)} %convert_element_type.163), channel_id=5, replica_groups=mesh['seq'=8,'head'=4] {'seq'}, dimensions={0}, use_global_device_ids=true | all-gather | bytes 589824 | tf_op jit(solution)/shard_map/all_gather | solution.py:263
  451.1 38.0 %while.150 = (s32[]{:T(128)}, f32[2,128,128]{1,2,0:T(8,128)}, s32[]{:T(128)}, f32[8,2,128,128]{3,2,1,0:T(8,128)}, f32[8,2,128,128]{3,2,1,0:T(8,128)}, /*index=5*/s32[]{:T(128)}, s32[]{:T(128)}, s32[]{:T(128)}, s32[]{:T(128)}) while((s32[]{:T(128)}, f32[2,128,128]{1,2,0:T(8,128)}, s32[]{:T(128)}, f32[8,2,128,128]{3,2,1,0:T(8,128)}, ...), condition=%wide.region_29.32_spmd, body=%wide.region_28.31_spmd.sunk | while | flops 50364420 | bytes 1310875 | solution.py:275
  465.4 2.0 fusion.552
  494.8 67.9 %while.152 = (s32[]{:T(128)}, f32[2,128,128]{2,1,0:T(8,128)S(1)}, f32[2,2,64,128]{3,2,1,0:T(8,128)}, f32[2,2,64,128]{3,2,1,0:T(8,128)}, f32[2,2,64,128]{3,2,1,0:...) while((s32[]{:T(128)}, f32[2,128,128]{2,1,0:T(8,128)S(1)}, ...), condition=%wide.region_41.44_spmd.clone.clone, body=%wide.region_31.43_spmd.clone.clone.sunk | while | flops 290124864 | bytes 13737729 | solution.py:89
  500.1 10.6 custom-call.42
  534.1 10.6 custom-call.42
  572.9 2.1 multiply_reduce_fusion.9
  578.6 2.5 convolution_convert_fusion.4
  584.3 4.1 collective-permute-done.1
  590.1 2.2 convolution_convert_fusion.3
  592.3 2.0 copy.325
  596.1 2.6 copy.329
  598.8 3.2 convolution_convert_fusion.1
  602.2 3.6 convolution_convert_fusion
  605.8 4.6 copy.333
  612.9 8.8 reduce-scatter.32.cloned.1.call-done
  623.0 5.6 all-reduce.17
  629.3 53.8 %reduce-scatter.30.cloned.1.call-done = bf16[48,8]{1,0:T(8,128)(2,1)} async-done(((bf16[384,8]{1,0:T(8,128)(2,1)}), bf16[48,8]{1,0:T(8,128)(2,1)}) %reduce-scatter.30.cloned.1.call-update) | async-done | bytes 784
  684.6 62.9 %reduce-scatter.28.cloned.1.call-done = bf16[128,4]{1,0:T(8,128)(2,1)} async-done(((bf16[1024,4]{1,0:T(8,128)(2,1)}), bf16[128,4]{1,0:T(8,128)(2,1)}) %reduce-scatter.28.cloned.1.call-update) | async-done | bytes 1040
  749.0 20.7 %reduce-scatter.22.cloned.1.call-done = bf16[128,256]{1,0:T(8,128)(2,1)} async-done(((bf16[128,1024]{1,0:T(8,128)(2,1)}), bf16[128,256]{1,0:T(8,128)(2,1)}) %reduce-scatter.22.cloned.1.call-update) | async-done | bytes 65552 | tf_op jit(solution)/shard_map/reduce_scatter | solution.py:220
  771.3 21.0 %reduce-scatter.24.cloned.1.call-done = bf16[128,256]{1,0:T(8,128)(2,1)} async-done(((bf16[128,1024]{1,0:T(8,128)(2,1)}), bf16[128,256]{1,0:T(8,128)(2,1)}) %reduce-scatter.24.cloned.1.call-update) | async-done | bytes 65552 | tf_op jit(solution)/shard_map/reduce_scatter | solution.py:307
  794.1 21.9 %all-reduce.18 = (f32[256]{0:T(256)}, f32[2]{0:T(128)}, f32[2]{0:T(128)}, f32[2]{0:T(128)}, f32[256]{0:T(256)}) all-reduce(f32[256]{0:T(256)S(1)} %get-tuple-element.3605, f32[2]{0:T(128)S(1)} %negate_multiply_fusion, f32[2]{0:T(128)S(1)} %copy-done.123, f32[2]{0:T(128)S(1)} %copy-done.122, ...), channel_id=1, replica_groups=mesh['seq'=8,'head'=4] {'seq'}, use_global_device_ids=true, to_apply=%region_48.51 | all-reduce | flops 518 | bytes 4144 | tf_op jit(solution)/shard_map/psum | solution.py:346
  816.0 42.2 %reduce-scatter.34.cloned.1.call-done = bf16[128,256]{1,0:T(8,128)(2,1)} async-done(((bf16[1024,256]{1,0:T(8,128)(2,1)}), bf16[128,256]{1,0:T(8,128)(2,1)}) %reduce-scatter.34.cloned.1.call-update) | async-done | bytes 65552
  859.8 66.4 %reduce-scatter.38.cloned.1.call-done = bf16[128,704]{1,0:T(8,128)(2,1)} async-done(((bf16[1024,704]{1,0:T(8,128)(2,1)}), bf16[128,704]{1,0:T(8,128)(2,1)}) %reduce-scatter.38.cloned.1.call-update) | async-done | bytes 180240
  928.0 68.8 %reduce-scatter.26.cloned.1.call-done = bf16[128,2,512]{2,0,1:T(8,128)(2,1)} async-done(((bf16[1024,2,512]{2,0,1:T(8,128)(2,1)}), bf16[128,2,512]{2,0,1:T(8,128)(2,1)}) %reduce-scatter.26.cloned.1.call-update) | async-done | bytes 262160 | tf_op jit(solution)/shard_map/reduce_scatter | solution.py:324
  996.8 2.0 copy.280
  998.9 73.2 %reduce-scatter.36.cloned.1.call-done = bf16[128,1408]{1,0:T(8,128)(2,1)} async-done(((bf16[1024,1408]{1,0:T(8,128)(2,1)}), bf16[128,1408]{1,0:T(8,128)(2,1)}) %reduce-scatter.36.cloned.1.call-update) | async-done | bytes 360464
  (817 shorter events, 293.1 us)
Async XLA Ops:
  7.2 247.0 %copy-start = (bf16[1024,2,704]{0,2,1:T(8,128)(2,1)S(1)}, bf16[1024,2,704]{0,2,1:T(8,128)(2,1)}, u32[]{:S(2)}) copy-start(bf16[1024,2,704]{0,2,1:T(8,128)(2,1)} %param.43) | copy-start | bytes 8650756
  7.2 21.1 %copy-start.127 = (f32[2]{0:T(128)S(1)}, f32[2]{0:T(128)}, u32[]{:S(2)}) copy-start(f32[2]{0:T(128)} %param.37) | copy-start | bytes 28
  7.2 21.1 %copy-start.102 = (bf16[1024,2,2]{0,2,1:T(2,128)(2,1)S(1)}, bf16[1024,2,2]{0,2,1:T(2,128)(2,1)}, u32[]{:S(2)}) copy-start(bf16[1024,2,2]{0,2,1:T(2,128)(2,1)} %param.35) | copy-start | bytes 24580
  7.2 103.2 %all-gather.12.cloned.1.call-start = ((), (), s32[]{:S(2)}) async-start(), calls=%async_computation.14 | async-start | bytes 1179648 | tf_op jit(solution)/shard_map/all_gather | solution.py:191
  14.9 14.0 %copy-start.23 = (bf16[128,1024]{1,0:T(8,128)(2,1)}, bf16[128,1024]{1,0:T(8,128)(2,1)S(1)}, u32[]{:S(2)}) copy-start(bf16[128,1024]{1,0:T(8,128)(2,1)S(1)} %all_gather.30) | copy-start | bytes 786436
  14.9 13.9 %copy-start.94 = (f32[4,2,384]{2,1,0:T(2,128)S(1)}, f32[4,2,384]{2,1,0:T(2,128)}, u32[]{:S(2)}) copy-start(f32[4,2,384]{2,1,0:T(2,128)} %param.36) | copy-start | bytes 36868
  24.9 6.4 collective-permute-start
  34.7 52.1 %copy-start.92 = (f32[2,128]{1,0:T(2,128)S(1)}, f32[2,128]{1,0:T(2,128)}, u32[]{:S(2)}) copy-start(f32[2,128]{1,0:T(2,128)} %param.40) | copy-start | bytes 3076
  69.4 82.7 %all-gather.14.cloned.1.call-start = ((), (), s32[]{:S(2)}) async-start(), calls=%async_computation.15 | async-start | bytes 1179648 | tf_op jit(solution)/shard_map/all_gather | solution.py:192
  71.1 179.7 %all-gather.10.cloned.1.call-start = ((), (), s32[]{:S(2)}) async-start(), calls=%async_computation.9 | async-start | bytes 2621440 | tf_op jit(solution)/shard_map/all_gather | solution.py:209
  71.9 262.8 %all-reduce.21.cloned.1.call-start = ((), (), s32[]{:S(2)}) async-start(), calls=%async_computation.11 | async-start | bytes 1048576 | tf_op jit(solution)/shard_map/psum | solution.py:239
  237.2 17.0 %copy-start.75 = (f32[4,1,256]{2,1,0:T(1,128)S(1)}, f32[4,1,256]{2,1,0:T(1,128)}, u32[]{:S(2)}) copy-start(f32[4,1,256]{2,1,0:T(1,128)} %convert_element_type.188) | copy-start | bytes 12292
  239.6 15.6 %copy-start.101 = (f32[128,2]{0,1:T(2,128)}, f32[128,2]{0,1:T(2,128)S(1)}, u32[]{:S(2)}) copy-start(f32[128,2]{0,1:T(2,128)S(1)} %add.469) | copy-start | bytes 3076
  258.6 77.6 %copy-start.111 = (f32[128]{0:T(128)S(1)}, f32[128]{0:T(128)}, u32[]{:S(2)}) copy-start(f32[128]{0:T(128)} %copy-done.110) | copy-start | bytes 1540
  258.6 363.1 %reduce-scatter.32.cloned.1.call-start = ((), (), s32[]{:S(2)}) async-start(), calls=%async_computation.18 | async-start | bytes 36864
  338.4 11.3 %copy-start.29 = (pred[64,64]{1,0:T(8,128)(4,1)S(1)}, pred[64,64]{1,0:T(8,128)(4,1)}, u32[]{:S(2)}) copy-start(pred[64,64]{1,0:T(8,128)(4,1)} %get-tuple-element.4935) | copy-start | bytes 12292
  365.8 11.4 %copy-start.77 = (f32[2,2,64]{2,1,0:T(2,128)S(1)}, f32[2,2,64]{2,1,0:T(2,128)}, u32[]{:S(2)}) copy-start(f32[2,2,64]{2,1,0:T(2,128)} %get-tuple-element.4740) | copy-start | bytes 3076 | tf_op jit(solution)/shard_map/transpose(jvp())/while
  365.8 12.0 %copy-start.1 = (f32[2,2,64,128]{3,2,1,0:T(8,128)S(1)}, f32[2,2,64,128]{3,2,1,0:T(8,128)}, u32[]{:S(2)}) copy-start(f32[2,2,64,128]{3,2,1,0:T(8,128)} %get-tuple-element.4732) | copy-start | bytes 393220 | tf_op jit(solution)/shard_map/transpose(jvp())/while
  365.8 12.3 %copy-start.21 = (f32[2,2,64,64]{3,2,1,0:T(8,128)S(1)}, f32[2,2,64,64]{3,2,1,0:T(8,128)}, u32[]{:S(2)}) copy-start(f32[2,2,64,64]{3,2,1,0:T(8,128)} %get-tuple-element.4743) | copy-start | bytes 196612 | tf_op jit(solution)/shard_map/transpose(jvp())/while
  365.8 12.6 %copy-start.51 = (f32[2,2,64,128]{3,2,1,0:T(8,128)S(1)}, f32[2,2,64,128]{3,2,1,0:T(8,128)}, u32[]{:S(2)}) copy-start(f32[2,2,64,128]{3,2,1,0:T(8,128)} %get-tuple-element.4687) | copy-start | bytes 393220 | tf_op jit(solution)/shard_map/transpose(jvp())/while
  367.1 11.6 %copy-start.53 = (f32[2,2,64,128]{3,2,1,0:T(8,128)S(1)}, f32[2,2,64,128]{3,2,1,0:T(8,128)}, u32[]{:S(2)}) copy-start(f32[2,2,64,128]{3,2,1,0:T(8,128)} %get-tuple-element.4688) | copy-start | bytes 393220 | tf_op jit(solution)/shard_map/transpose(jvp())/while
  399.8 11.4 %copy-start.77 = (f32[2,2,64]{2,1,0:T(2,128)S(1)}, f32[2,2,64]{2,1,0:T(2,128)}, u32[]{:S(2)}) copy-start(f32[2,2,64]{2,1,0:T(2,128)} %get-tuple-element.4740) | copy-start | bytes 3076 | tf_op jit(solution)/shard_map/transpose(jvp())/while
  399.9 12.0 %copy-start.1 = (f32[2,2,64,128]{3,2,1,0:T(8,128)S(1)}, f32[2,2,64,128]{3,2,1,0:T(8,128)}, u32[]{:S(2)}) copy-start(f32[2,2,64,128]{3,2,1,0:T(8,128)} %get-tuple-element.4732) | copy-start | bytes 393220 | tf_op jit(solution)/shard_map/transpose(jvp())/while
  399.9 12.3 %copy-start.21 = (f32[2,2,64,64]{3,2,1,0:T(8,128)S(1)}, f32[2,2,64,64]{3,2,1,0:T(8,128)}, u32[]{:S(2)}) copy-start(f32[2,2,64,64]{3,2,1,0:T(8,128)} %get-tuple-element.4743) | copy-start | bytes 196612 | tf_op jit(solution)/shard_map/transpose(jvp())/while
  399.9 12.6 %copy-start.51 = (f32[2,2,64,128]{3,2,1,0:T(8,128)S(1)}, f32[2,2,64,128]{3,2,1,0:T(8,128)}, u32[]{:S(2)}) copy-start(f32[2,2,64,128]{3,2,1,0:T(8,128)} %get-tuple-element.4687) | copy-start | bytes 393220 | tf_op jit(solution)/shard_map/transpose(jvp())/while
  401.1 11.6 %copy-start.53 = (f32[2,2,64,128]{3,2,1,0:T(8,128)S(1)}, f32[2,2,64,128]{3,2,1,0:T(8,128)}, u32[]{:S(2)}) copy-start(f32[2,2,64,128]{3,2,1,0:T(8,128)} %get-tuple-element.4688) | copy-start | bytes 393220 | tf_op jit(solution)/shard_map/transpose(jvp())/while
  510.8 11.4 %copy-start.78 = (f32[2,2,64]{2,1,0:T(2,128)S(1)}, f32[2,2,64]{2,1,0:T(2,128)}, u32[]{:S(2)}) copy-start(f32[2,2,64]{2,1,0:T(2,128)} %get-tuple-element.4879) | copy-start | bytes 3076 | tf_op jit(solution)/shard_map/transpose(jvp())/while
  510.8 12.0 %copy-start.2 = (f32[2,2,64,128]{3,2,1,0:T(8,128)S(1)}, f32[2,2,64,128]{3,2,1,0:T(8,128)}, u32[]{:S(2)}) copy-start(f32[2,2,64,128]{3,2,1,0:T(8,128)} %get-tuple-element.4871) | copy-start | bytes 393220 | tf_op jit(solution)/shard_map/transpose(jvp())/while
  510.8 12.3 %copy-start.22 = (f32[2,2,64,64]{3,2,1,0:T(8,128)S(1)}, f32[2,2,64,64]{3,2,1,0:T(8,128)}, u32[]{:S(2)}) copy-start(f32[2,2,64,64]{3,2,1,0:T(8,128)} %get-tuple-element.4882) | copy-start | bytes 196612 | tf_op jit(solution)/shard_map/transpose(jvp())/while
  510.8 12.6 %copy-start.57 = (f32[2,2,64,128]{3,2,1,0:T(8,128)S(1)}, f32[2,2,64,128]{3,2,1,0:T(8,128)}, u32[]{:S(2)}) copy-start(f32[2,2,64,128]{3,2,1,0:T(8,128)} %get-tuple-element.4827) | copy-start | bytes 393220 | tf_op jit(solution)/shard_map/transpose(jvp())/while
  512.1 11.6 %copy-start.59 = (f32[2,2,64,128]{3,2,1,0:T(8,128)S(1)}, f32[2,2,64,128]{3,2,1,0:T(8,128)}, u32[]{:S(2)}) copy-start(f32[2,2,64,128]{3,2,1,0:T(8,128)} %get-tuple-element.4828) | copy-start | bytes 393220 | tf_op jit(solution)/shard_map/transpose(jvp())/while
  544.8 11.4 %copy-start.78 = (f32[2,2,64]{2,1,0:T(2,128)S(1)}, f32[2,2,64]{2,1,0:T(2,128)}, u32[]{:S(2)}) copy-start(f32[2,2,64]{2,1,0:T(2,128)} %get-tuple-element.4879) | copy-start | bytes 3076 | tf_op jit(solution)/shard_map/transpose(jvp())/while
  544.8 12.0 %copy-start.2 = (f32[2,2,64,128]{3,2,1,0:T(8,128)S(1)}, f32[2,2,64,128]{3,2,1,0:T(8,128)}, u32[]{:S(2)}) copy-start(f32[2,2,64,128]{3,2,1,0:T(8,128)} %get-tuple-element.4871) | copy-start | bytes 393220 | tf_op jit(solution)/shard_map/transpose(jvp())/while
  544.8 12.3 %copy-start.22 = (f32[2,2,64,64]{3,2,1,0:T(8,128)S(1)}, f32[2,2,64,64]{3,2,1,0:T(8,128)}, u32[]{:S(2)}) copy-start(f32[2,2,64,64]{3,2,1,0:T(8,128)} %get-tuple-element.4882) | copy-start | bytes 196612 | tf_op jit(solution)/shard_map/transpose(jvp())/while
  544.8 12.6 %copy-start.57 = (f32[2,2,64,128]{3,2,1,0:T(8,128)S(1)}, f32[2,2,64,128]{3,2,1,0:T(8,128)}, u32[]{:S(2)}) copy-start(f32[2,2,64,128]{3,2,1,0:T(8,128)} %get-tuple-element.4827) | copy-start | bytes 393220 | tf_op jit(solution)/shard_map/transpose(jvp())/while
  546.1 11.6 %copy-start.59 = (f32[2,2,64,128]{3,2,1,0:T(8,128)S(1)}, f32[2,2,64,128]{3,2,1,0:T(8,128)}, u32[]{:S(2)}) copy-start(f32[2,2,64,128]{3,2,1,0:T(8,128)} %get-tuple-element.4828) | copy-start | bytes 393220 | tf_op jit(solution)/shard_map/transpose(jvp())/while
  570.2 112.9 %reduce-scatter.30.cloned.1.call-start = ((), (), s32[]{:S(2)}) async-start(), calls=%async_computation.17 | async-start | bytes 110592
  576.3 171.2 %reduce-scatter.28.cloned.1.call-start = ((), (), s32[]{:S(2)}) async-start(), calls=%async_computation.16 | async-start | bytes 294912
  578.5 191.2 %reduce-scatter.22.cloned.1.call-start = ((), (), s32[]{:S(2)}) async-start(), calls=%async_computation.10 | async-start | bytes 327680 | tf_op jit(solution)/shard_map/reduce_scatter | solution.py:220
  581.1 211.2 %reduce-scatter.24.cloned.1.call-start = ((), (), s32[]{:S(2)}) async-start(), calls=%async_computation.12 | async-start | bytes 327680 | tf_op jit(solution)/shard_map/reduce_scatter | solution.py:307
  582.6 5.7 collective-permute-start.1
  590.0 268.1 %reduce-scatter.34.cloned.1.call-start = ((), (), s32[]{:S(2)}) async-start(), calls=%async_computation.19 | async-start | bytes 589824
  594.3 331.8 %reduce-scatter.38.cloned.1.call-start = ((), (), s32[]{:S(2)}) async-start(), calls=%async_computation.21 | async-start | bytes 1769472
  598.8 398.1 %reduce-scatter.26.cloned.1.call-start = ((), (), s32[]{:S(2)}) async-start(), calls=%async_computation.13 | async-start | bytes 2359296 | tf_op jit(solution)/shard_map/reduce_scatter | solution.py:324
  602.1 469.9 %reduce-scatter.36.cloned.1.call-start = ((), (), s32[]{:S(2)}) async-start(), calls=%async_computation.20 | async-start | bytes 3244032
  610.3 182.0 %copy-start.124 = (f32[128]{0:T(128)S(1)}, f32[128]{0:T(128)}, u32[]{:S(2)}) copy-start(f32[128]{0:T(128)} %get-tuple-element.3630) | copy-start | bytes 1540
  610.3 183.7 %copy-start.122 = (f32[2]{0:T(128)S(1)}, f32[2]{0:T(128)}, u32[]{:S(2)}) copy-start(f32[2]{0:T(128)} %get-tuple-element.3538) | copy-start | bytes 28
  610.3 183.7 %copy-start.123 = (f32[2]{0:T(128)S(1)}, f32[2]{0:T(128)}, u32[]{:S(2)}) copy-start(f32[2]{0:T(128)} %get-tuple-element.3641) | copy-start | bytes 28
  (151 other events, 964.0 us)
Sparse Core Ops, SparseCore 0:
  69.5 40.8 all-gather.11
  113.1 38.9 all-gather.13
  153.7 21.3 all-gather.9
  258.7 75.1 all-reduce.20
  570.4 51.2 reduce-scatter.31
  625.4 57.7 reduce-scatter.29
  686.4 61.0 reduce-scatter.27
  750.6 19.1 reduce-scatter.21
  772.2 20.0 reduce-scatter.23
  795.5 62.6 reduce-scatter.33
  861.6 64.5 reduce-scatter.37
  929.6 67.2 reduce-scatter.25
  1000.4 71.5 reduce-scatter.35
where the time goes:
time: 1090 us; the launch traced here: 1080 us
  waiting for transfers between devices  485 us (44%)
  blocking collectives  164 us (15%)
  other arithmetic  159 us (15%)
  matrix products  127 us (12%)
  local copies, waits for them, and re-layouts  123 us (11%)
  between operations  15.1 us (1%)
    unnamed x19, waiting for transfers between devices  308 us
    another operation x34, other arithmetic, lower_solve(): jax.scipy.linalg.solve_triangular(system, target, lower=True, unit_diagon...  90.9 us
    all_gather x1, blocking collectives, on_device(): lax.all_gather(reverse_transfer[None].astype(jnp.bfloat16), 'seq', axis=0...  71.8 us
    reduce_scatter x1, waiting for transfers between devices, on_device(): lax.psum_scatter(grad_proj.astype(jnp.bfloat16), 'seq', scatter_dimension...  68.8 us
    all_gather x1, waiting for transfers between devices, on_device(): lax.all_gather(offset[None], 'seq', axis=0, tiled=True)  41.7 us
    all_gather x1, blocking collectives, on_device(): lax.all_gather(local_state[None].astype(jnp.bfloat16), 'seq', axis=0, til...  31.5 us
    unnamed x171, local copies, waits for them, and re-layouts  25.2 us
    psum x1, blocking collectives, on_device(): lax.psum((grad_gain_one, grad_gain_two, grad_decay_log, grad_decay_bias,...  21.9 us
  transfers between devices with their start and end apart: 15, of which 12 were waited for; matrix products, arithmetic and copies ran while one was open for 14% of the time, Pallas kernels for 0%

commit v1 on v0

v1 whole, which is shorter than its diff:
```python
import functools

import jax
import jax.numpy as jnp
from jax import lax
from jax.experimental import pallas as pl
from jax.experimental.pallas import tpu as pltpu
from jax.sharding import PartitionSpec as P


EPSILON = 1e-06
EDGE = 8
BF = jnp.bfloat16
F32 = jnp.float32
NN = (((1,), (0,)), ((), ()))
NT = (((1,), (1,)), ((), ()))
TN = (((0,), (0,)), ((), ()))


def shifted(value, axis, steps):
    count = lax.axis_size(axis)
    pairs = [(i, i + steps) for i in range(count) if 0 <= i + steps < count]
    return lax.ppermute(value, axis, pairs)


def plane(ranks):
    inner = 1
    while inner * inner * 4 <= ranks:
        inner *= 2
    return ranks // inner, inner


def turned(value, axis, steps, group):
    count = lax.axis_size(axis)
    pairs = [(i, i // group * group + (i % group + steps) % group) for i in range(count)]
    return lax.ppermute(value, axis, pairs)


def in_group(value, ranks):
    _, inner = plane(ranks)
    return [value] + [turned(value, "seq", i, inner) for i in range(1, inner)]


def summed_over(value, axis):
    count = lax.axis_size(axis)
    step = 1
    while step < count:
        value = value + lax.ppermute(value, axis, [(i, i ^ step) for i in range(count)])
        step *= 2
    return value


def outer_sum(blocks, ranks):
    outer, inner = plane(ranks)
    total = blocks[0].astype(F32)
    for steps in range(1, outer):
        pairs = [(r, (r + steps * inner) % ranks) for r in range(ranks)]
        total = total + lax.ppermute(blocks[steps], "seq", pairs).astype(F32)
    return total


def rms_scale(rows):
    return lax.rsqrt(jnp.mean(rows * rows, axis=-1, keepdims=True) + EPSILON)


def halves(x):
    high = x.astype(BF)
    low = (x - high.astype(F32)).astype(BF)
    return high, low


def dot(a, b, dims=NN):
    ah, al = halves(a)
    bh, bl = halves(b)
    one = functools.partial(lax.dot_general, dimension_numbers=dims, preferred_element_type=F32)
    return one(ah, bh) + (one(ah, bl) + one(al, bh))


def grids(length):
    row = lax.broadcasted_iota(jnp.int32, (length, length), 0)
    col = lax.broadcasted_iota(jnp.int32, (length, length), 1)
    return row, col


def to_row(column, row, col):
    return jnp.sum(jnp.where(row == col, column, 0.0), axis=0, keepdims=True)


def to_column(line, row, col):
    return jnp.sum(jnp.where(row == col, line, 0.0), axis=1, keepdims=True)


def decay_matrix(cum, row, col):
    causal = col <= row
    gap = cum - to_row(cum, row, col)
    return jnp.where(causal, jnp.exp(jnp.where(causal, gap, 0.0)), 0.0)


def unit_lower_inverse(lower, row, col):
    length = lower.shape[0]
    identity = jnp.where(row == col, 1.0, 0.0)
    pair = (row // 2 == col // 2) & (col < row)
    inverse = identity - jnp.where(pair, lower, 0.0)
    size = 2
    while size < length:
        off = (row // (2 * size) == col // (2 * size)) & (row // size != col // size) & (col < row)
        inverse = inverse - dot(dot(inverse, jnp.where(off, lower, 0.0)), inverse)
        size *= 2
    return inverse


def setup_kernel(
    proj_ref, rates_ref, taps_ref, params_ref,
    pre_ref, q_ref, k_ref, inv_ref, w_ref, vals_ref, score_ref, inner_ref, cols_ref, map_ref,
    ext_ref,
):
    heads, rows, width = proj_ref.shape
    length = rows - EDGE
    dim = width // 4
    taps = taps_ref.shape[0]
    row, col = grids(length)
    for h in range(heads):
        ext_ref[...] = proj_ref[h, :, : 3 * dim].astype(BF).astype(F32)
        start = EDGE - taps + 1
        pre = ext_ref[start : start + length, :] * taps_ref[0, h : h + 1, :]
        for j in range(1, taps):
            pre = pre + ext_ref[start + j : start + j + length, :] * taps_ref[j, h : h + 1, :]
        pre_ref[h] = pre
        mixed = pre * jax.nn.sigmoid(pre)
        q = mixed[:, :dim]
        k = mixed[:, dim : 2 * dim]
        v = mixed[:, 2 * dim :]
        q = q * lax.rsqrt(jnp.sum(q * q, axis=1, keepdims=True) + EPSILON) * dim ** (-0.5)
        k = k * lax.rsqrt(jnp.sum(k * k, axis=1, keepdims=True) + EPSILON)
        beta = jax.nn.sigmoid(rates_ref[h, :, 0:1] + params_ref[2:3, h : h + 1])
        shift = rates_ref[h, :, 1:2] + params_ref[1:2, h : h + 1]
        soft = jnp.maximum(shift, 0.0) + jnp.log1p(jnp.exp(-jnp.abs(shift)))
        decay = -jnp.exp(params_ref[0:1, h : h + 1]) * soft
        cum = jnp.sum(jnp.where(col <= row, to_row(decay, row, col), 0.0), axis=1, keepdims=True)
        decays = decay_matrix(cum, row, col)
        growth = jnp.exp(cum)
        last = cum[length - 1 : length, :]
        remain = jnp.exp(last - cum)
        inner = jnp.where(col < row, decays * dot(k, k, NT), 0.0)
        inverse = unit_lower_inverse(beta * inner, row, col)
        weights = dot(inverse, (beta * growth) * k)
        values = dot(inverse, beta * v)
        kept = remain * k
        identity = jnp.where(row[:dim, :dim] == col[:dim, :dim], jnp.exp(last), 0.0)
        map_ref[0, h] = identity - dot(weights, kept, TN)
        map_ref[1, h] = dot(values, kept, TN)
        q_ref[h] = q
        k_ref[h] = k
        inv_ref[h] = inverse
        w_ref[h] = weights
        vals_ref[h] = values
        score_ref[h] = decays * dot(q, k, NT)
        inner_ref[h] = inner
        cols_ref[h] = jnp.concatenate(
            [cum, beta, decay, jax.nn.sigmoid(shift), jnp.zeros((length, 4), F32)], axis=1
        )


def outputs_kernel(
    q_ref, w_ref, vals_ref, score_ref, cols_ref, state_ref, gate_ref, gain_ref,
    mixed_ref, upd_ref, out_ref,
):
    heads, _, dim = q_ref.shape
    for h in range(heads):
        state = state_ref[h]
        upd = vals_ref[h] - dot(w_ref[h], state, NT)
        out = jnp.exp(cols_ref[h, :, 0:1]) * dot(q_ref[h], state, NT) + dot(score_ref[h], upd)
        gate = gate_ref[h, EDGE:, 3 * dim :]
        normed = out * lax.rsqrt(jnp.mean(out * out, axis=1, keepdims=True) + EPSILON)
        normed = normed * gain_ref[h : h + 1, :] * (gate * jax.nn.sigmoid(gate))
        mixed_ref[:, h * dim : (h + 1) * dim] = normed.astype(BF)
        upd_ref[h] = upd
        out_ref[h] = out


def local_back_kernel(
    grad_ref, out_ref, gate_ref, gain_ref, score_ref, q_ref, w_ref, cols_ref,
    dout_ref, dupd_ref, dstate_ref, dgate_ref, dgain_ref,
):
    heads, _, dim = q_ref.shape
    for h in range(heads):
        grad = grad_ref[:, h * dim : (h + 1) * dim]
        out = out_ref[h]
        scale = lax.rsqrt(jnp.mean(out * out, axis=1, keepdims=True) + EPSILON)
        normed = out * scale
        gate = gate_ref[h, EDGE:, 3 * dim :]
        sigma = jax.nn.sigmoid(gate)
        gain = gain_ref[h : h + 1, :]
        silu = gate * sigma
        dgain_ref[h : h + 1, :] = jnp.sum(grad * normed * silu, axis=0, keepdims=True)
        dgate_ref[h] = grad * normed * gain * (sigma * (1.0 + gate * (1.0 - sigma)))
        inside = grad * gain * silu
        dout = scale * (inside - normed * jnp.mean(inside * normed, axis=1, keepdims=True))
        dupd = dot(score_ref[h], dout, TN)
        grown = jnp.exp(cols_ref[h, :, 0:1]) * dout
        dstate_ref[h] = dot(grown, q_ref[h], TN) - dot(dupd, w_ref[h], TN)
        dout_ref[h] = dout
        dupd_ref[h] = dupd


def score_back_kernel(
    dout_ref, upd_ref, score_ref, q_ref, k_ref, cols_ref, state_ref,
    dq_ref, dk_ref, dcum_ref,
):
    heads, length, _ = q_ref.shape
    row, col = grids(length)
    for h in range(heads):
        dout = dout_ref[h]
        q = q_ref[h]
        cum = cols_ref[h, :, 0:1]
        dscore = jnp.where(col <= row, dot(dout, upd_ref[h], NT), 0.0)
        dinner = dscore * decay_matrix(cum, row, col)
        grown = dot(jnp.exp(cum) * dout, state_ref[h])
        dq_ref[h] = grown + dot(dinner, k_ref[h])
        dk_ref[h] = dot(dinner, q, TN)
        both = dscore * score_ref[h]
        dcum = jnp.sum(both, axis=1, keepdims=True) + jnp.sum(q * grown, axis=1, keepdims=True)
        dcum = dcum - to_column(jnp.sum(both, axis=0, keepdims=True), row, col)
        dcum_ref[h] = jnp.broadcast_to(dcum, (length, 8))


def final_back_kernel(
    dend_ref, dupd_ref, state_ref, upd_ref, inv_ref, inner_ref, k_ref, q_ref, cols_ref,
    dq_ref, dk_ref, dcum_ref, pre_ref, proj_ref, taps_ref, params_ref, dgate_ref,
    rows_ref, dtaps_ref, dparams_ref,
    ext_ref, pad_ref,
):
    heads, length, dim = q_ref.shape
    taps = taps_ref.shape[0]
    rows = length + EDGE
    row, col = grids(length)
    width = 4 * dim
    pad_ref[...] = jnp.zeros_like(pad_ref)
    rows_ref[:, heads * width :] = jnp.zeros((rows, rows_ref.shape[1] - heads * width), BF)
    lane = lax.broadcasted_iota(jnp.int32, (1, 128), 1)
    for h in range(heads):
        dend = dend_ref[h]
        state = state_ref[h]
        upd = upd_ref[h]
        k = k_ref[h]
        inner = inner_ref[h]
        cum = cols_ref[h, :, 0:1]
        beta = cols_ref[h, :, 1:2]
        decay = cols_ref[h, :, 2:3]
        soft_slope = cols_ref[h, :, 3:4]
        growth = jnp.exp(cum)
        last = cum[length - 1 : length, :]
        remain = jnp.exp(last - cum)
        kept = remain * k
        pre = pre_ref[h]
        sigma = jax.nn.sigmoid(pre)
        mixed = pre * sigma
        v = mixed[:, 2 * dim :]
        dupd = dupd_ref[h] + dot(kept, dend, NT)
        solved = dot(inv_ref[h], dupd, TN)
        dkept = dot(upd, dend)
        dright = -dot(solved, state)
        dlower = jnp.where(col < row, -dot(solved, upd, NT), 0.0)
        across = jnp.sum(dright * k, axis=1, keepdims=True)
        dlow_inner = dlower * inner
        dbeta_inner = jnp.sum(dlow_inner, axis=1, keepdims=True)
        dbeta = dbeta_inner + growth * across + jnp.sum(solved * v, axis=1, keepdims=True)
        both = beta * dlow_inner
        dinner = (dlower * beta) * decay_matrix(cum, row, col)
        dk = dk_ref[h] + dot(dinner, k) + dot(dinner, k, TN)
        dk = dk + (beta * growth) * dright + remain * dkept
        tail = jnp.sum(dkept * kept, axis=1, keepdims=True)
        dcum = dcum_ref[h, :, 0:1] + beta * dbeta_inner
        dcum = dcum - to_column(jnp.sum(both, axis=0, keepdims=True), row, col)
        dcum = dcum + (beta * growth) * across - tail
        dlast = jnp.sum(tail, axis=0, keepdims=True)
        held = jnp.sum(jnp.sum(state * dend, axis=1, keepdims=True), axis=0, keepdims=True)
        dlast = dlast + jnp.exp(last) * held
        ddecay = jnp.sum(jnp.where(col >= row, to_row(dcum, row, col), 0.0), axis=1, keepdims=True)
        ddecay = ddecay + dlast
        dv = beta * solved
        dshift = ddecay * (-jnp.exp(params_ref[0:1, h : h + 1])) * soft_slope
        dwrite = dbeta * beta * (1.0 - beta)
        total_log = jnp.sum(ddecay * decay, axis=0, keepdims=True)
        total_bias = jnp.sum(dshift, axis=0, keepdims=True)
        total_write = jnp.sum(dwrite, axis=0, keepdims=True)
        line = jnp.where(lane == 0, total_log, 0.0) + jnp.where(lane == 1, total_bias, 0.0)
        dparams_ref[h : h + 1, :] = line + jnp.where(lane == 2, total_write, 0.0)
        place = heads * width
        rate_lanes = jnp.where(lane == 2 * h, dwrite, 0.0) + jnp.where(lane == 2 * h + 1, dshift, 0.0)
        rows_ref[EDGE:, place : place + 128] += rate_lanes.astype(BF)
        q_raw = mixed[:, :dim]
        k_raw = mixed[:, dim : 2 * dim]
        q_scale = lax.rsqrt(jnp.sum(q_raw * q_raw, axis=1, keepdims=True) + EPSILON)
        k_scale = lax.rsqrt(jnp.sum(k_raw * k_raw, axis=1, keepdims=True) + EPSILON)
        q_unit = q_raw * q_scale
        dq = dq_ref[h] * dim ** (-0.5)
        dq = q_scale * (dq - q_unit * jnp.sum(dq * q_unit, axis=1, keepdims=True))
        dk = k_scale * (dk - k * jnp.sum(dk * k, axis=1, keepdims=True))
        slope = sigma * (1.0 + pre * (1.0 - sigma))
        dpre = jnp.concatenate([dq, dk, dv], axis=1) * slope
        pad_ref[EDGE : EDGE + length, :] = dpre
        ext_ref[...] = proj_ref[h, :, : 3 * dim].astype(BF).astype(F32)
        start = EDGE - taps + 1
        total = jnp.zeros((rows, 3 * dim), F32)
        for j in range(taps):
            dtaps_ref[j, h : h + 1, :] = jnp.sum(
                dpre * ext_ref[start + j : start + j + length, :], axis=0, keepdims=True
            )
            total = total + pad_ref[taps - 1 - j : taps - 1 - j + rows, :] * taps_ref[j, h : h + 1, :]
        rows_ref[:, h * width : h * width + 3 * dim] = total.astype(BF)
        rows_ref[:EDGE, h * width + 3 * dim : (h + 1) * width] = jnp.zeros((EDGE, dim), BF)
        rows_ref[EDGE:, h * width + 3 * dim : (h + 1) * width] = dgate_ref[h].astype(BF)


def picked(left, places, share):
    if share % 128 == 0:
        return left
    starts = [places[z] * share for z in range(places.shape[0])]
    return jnp.stack([lax.dynamic_slice_in_dim(left, start, share, 1) for start in starts])


def columns_of(left_ref, place_ref, z, share):
    if len(left_ref.shape) == 3:
        return left_ref[z]
    return left_ref[:, pl.ds(pl.multiple_of(place_ref[z] * share, share), share)]


def feature_minor_kernel(parts, lefts, which, place_ref, *refs):
    outer = place_ref.shape[0]
    rights = (len(refs) - outer) // parts - lefts
    for z in range(outer):
        out_ref = refs[len(refs) - outer + z]
        share = out_ref.shape[1]
        at = 0
        for a, b, i in which:
            total = None
            for p in range(parts):
                left = columns_of(refs[p * (lefts + rights) + a], place_ref, z, share)
                right = refs[p * (lefts + rights) + lefts + b][i]
                one = lax.dot_general(right, left, TN, preferred_element_type=F32)
                total = one if total is None else total + one
            out_ref[at : at + total.shape[0], :] = total.astype(BF)
            at += total.shape[0]


def feature_major_kernel(parts, place_ref, *refs):
    for z in range(place_ref.shape[0]):
        out_ref = refs[2 * parts + z]
        share = out_ref.shape[0]
        total = None
        for p in range(parts):
            left = columns_of(refs[2 * p], place_ref, z, share)
            one = lax.dot_general(left, refs[2 * p + 1][...], TN, preferred_element_type=F32)
            total = one if total is None else total + one
        out_ref[...] = total.astype(BF)


def input_back_kernel(rows_ref, weight_ref, inputs_ref, gain_ref, sent_ref):
    sides, rows, wide = sent_ref.shape
    local = wide - 128
    grad = lax.dot_general(rows_ref[...], weight_ref[...], NT, preferred_element_type=F32)
    stat = jnp.sum(grad * gain_ref[...] * inputs_ref[...], axis=1, keepdims=True)
    high, low = halves(stat)
    lane = lax.broadcasted_iota(jnp.int32, (rows, 128), 1)
    stats = jnp.where(lane == 0, high.astype(F32), 0.0) + jnp.where(lane == 1, low.astype(F32), 0.0)
    for side in range(sides):
        sent_ref[side, :, :local] = grad[:, side * local : (side + 1) * local].astype(BF)
        sent_ref[side, :, local:] = stats.astype(BF)


def compose_kernel(early_ref, late_ref, both_ref):
    for h in range(early_ref.shape[1]):
        later = late_ref[0, h]
        both_ref[0, h] = dot(early_ref[0, h], later)
        both_ref[1, h] = dot(early_ref[1, h], later) + late_ref[1, h]


def carry_kernel(first_ref, map_ref, second_ref, sum_ref):
    for h in range(first_ref.shape[0]):
        sum_ref[h] = dot(first_ref[h], map_ref[h]) + second_ref[h]


def carry_back_kernel(first_ref, map_ref, second_ref, sum_ref):
    for h in range(first_ref.shape[0]):
        sum_ref[h] = dot(first_ref[h], map_ref[h], NT) + second_ref[h]


def kernel_call(body, outs, args, dots, scratch=(), scalars=0):
    vmem = pl.BlockSpec(memory_space=pltpu.VMEM)
    smem = pl.BlockSpec(memory_space=pltpu.SMEM)
    shapes = [jax.ShapeDtypeStruct(shape, kind) for shape, kind in outs]
    total = sum(a.size * a.dtype.itemsize for a in args)
    return pl.pallas_call(
        body,
        out_shape=shapes,
        in_specs=[smem] * scalars + [vmem] * (len(args) - scalars),
        out_specs=[vmem] * len(outs),
        scratch_shapes=list(scratch),
        cost_estimate=pl.CostEstimate(
            flops=dots * 6 * 128**3, bytes_accessed=total, transcendentals=0
        ),
    )(*args)


def scan_states(pair, ranks, extras):
    heads = pair.shape[1]
    shape = pair.shape[1:]
    maps = []
    done = []
    span = 1
    while 2 * span < ranks:
        early = shifted(pair, "seq", span)
        joined = shifted(pair[0], "seq", 1 - span) if span > 1 else pair[0]
        if extras:
            early, joined, ready = lax.optimization_barrier((early, joined, extras[0]))
            extras = extras[1:]
            done.append(ready)
        else:
            early, joined = lax.optimization_barrier((early, joined))
        maps.append(joined)
        (pair,) = kernel_call(compose_kernel, [(pair.shape, F32)], (early, pair), 4 * heads)
        span *= 2
    near = shifted(pair, "seq", 1)
    if span + 1 >= ranks:
        return near[1], maps + [pair[0]], done + list(extras)
    far = shifted(pair[1], "seq", span + 1)
    joined = shifted(pair[0], "seq", -span)
    near, far, joined = lax.optimization_barrier((near, far, joined))
    (incoming,) = kernel_call(carry_kernel, [(shape, F32)], (far, near[0], near[1]), 2 * heads)
    return incoming, maps + [joined], done + list(extras)


def scan_back(local, maps, ranks, extra):
    heads = local.shape[0]
    total = local
    span = 1
    for level in range(len(maps) - 1):
        later = shifted(total, "seq", -span)
        if level == len(maps) - 2:
            later, extra = lax.optimization_barrier((later, extra))
        (total,) = kernel_call(
            carry_back_kernel, [(local.shape, F32)], (later, maps[level], total), 2 * heads
        )
        span *= 2
    near = shifted(total, "seq", -1)
    if span + 1 < ranks:
        far = shifted(total, "seq", -(span + 1))
        (near,) = kernel_call(
            carry_back_kernel, [(local.shape, F32)], (far, maps[-1], near), 2 * heads
        )
    return near, extra


def layer(
    block_input,
    mixer_gain,
    proj_weight,
    rate_weight,
    conv_weight,
    decay_log,
    decay_bias,
    write_bias,
    output_gain,
    merge_weight,
    feed_gain,
    gateup_weight,
    down_weight,
    output_grad,
):
    length, local_width = block_input.shape
    model_width, heads, width = proj_weight.shape
    dim = width // 4
    hidden_width = down_weight.shape[0]
    taps = conv_weight.shape[0]
    ranks = lax.axis_size("seq")
    sides = lax.axis_size("head")
    rank = lax.axis_index("seq")
    part = lax.axis_index("head")
    rows = length + EDGE

    edge = shifted(block_input[length - EDGE :], "seq", 1)
    gains = [jnp.broadcast_to(gain[None], (EDGE, local_width)) for gain in (mixer_gain, feed_gain)]
    packed = jnp.concatenate([edge, block_input, *gains, output_grad], axis=0)
    whole = lax.all_gather(packed, "head", axis=1, tiled=True)
    whole, merge_sent = lax.optimization_barrier((whole, merge_weight))
    inputs_ext = whole[:rows].astype(F32)
    inputs = inputs_ext[EDGE:]
    gain_one = whole[rows].astype(F32)
    gain_two = whole[rows + EDGE].astype(F32)
    grads_full = whole[rows + 2 * EDGE :]
    all_weight = jnp.concatenate(
        [merge_weight] + [turned(merge_sent, "head", i, sides) for i in range(1, sides)], axis=0
    )

    scale_ext = rms_scale(inputs_ext)
    normed_ext = (inputs_ext * scale_ext * gain_one).astype(BF)
    projected = jnp.einsum("td,dhe->hte", normed_ext, proj_weight, preferred_element_type=F32)
    rates = jnp.einsum(
        "td,dhe->hte", normed_ext[EDGE:], rate_weight, preferred_element_type=F32
    )
    params = jnp.stack([decay_log, decay_bias, write_bias])

    cube = (heads, length, dim)
    square = (heads, length, length)
    pre, q, k, inverse, weights, values, scores, inner, cols, pair = kernel_call(
        setup_kernel,
        [
            ((heads, length, 3 * dim), F32), (cube, F32), (cube, F32), (square, F32), (cube, F32),
            (cube, F32), (square, F32), (square, F32), ((heads, length, 8), F32),
            ((2, heads, dim, dim), F32),
        ],
        (projected, rates, conv_weight, params),
        18 * heads,
        [pltpu.VMEM((rows, 3 * dim), F32)],
    )
    rate_columns = jnp.moveaxis(rate_weight, 0, 2).reshape(2 * heads, model_width).T
    wide_weight = jnp.concatenate(
        [
            proj_weight.reshape(model_width, heads * width),
            jnp.pad(rate_columns, ((0, 0), (0, 128 - 2 * heads))),
        ],
        axis=1,
    )
    incoming, maps, (wide_weight, all_weight) = scan_states(pair, ranks, [wide_weight, all_weight])
    mixed_rows, updates, outs = kernel_call(
        outputs_kernel,
        [((length, heads * dim), BF), (cube, F32), (cube, F32)],
        (q, weights, values, scores, cols, incoming, projected, output_gain),
        3 * heads,
    )
    all_rows = jnp.concatenate(
        [mixed_rows] + [turned(mixed_rows, "head", i, sides) for i in range(1, sides)], axis=1
    )
    mixer_out = jnp.dot(all_rows, all_weight, preferred_element_type=F32)
    resid = inputs + mixer_out
    scale_two = rms_scale(resid)
    feed_in = (resid * scale_two * gain_two).astype(BF)
    gateup = jnp.einsum("td,dcf->tcf", feed_in, gateup_weight, preferred_element_type=F32)
    gate_part = gateup[:, 0]
    up_part = gateup[:, 1]
    sigma = jax.nn.sigmoid(gate_part)
    hidden = (gate_part * sigma * up_part).astype(BF)
    feed_part = jnp.dot(hidden, down_weight, preferred_element_type=F32)
    grad_hidden = jnp.einsum("td,fd->tf", grads_full, down_weight, preferred_element_type=F32)
    grad_gate = grad_hidden * up_part * sigma * (1.0 + gate_part * (1.0 - sigma))
    grad_up = grad_hidden * gate_part * sigma
    grad_gateup_rows = jnp.stack([grad_gate, grad_up], axis=0).astype(BF)
    grad_feed_part = jnp.einsum(
        "ctf,dcf->td", grad_gateup_rows, gateup_weight, preferred_element_type=F32
    )

    def by_side(value):
        return jnp.moveaxis(value.reshape(value.shape[0], sides, local_width), 1, 0)

    def by_part(values):
        return list(zip(*[in_group(value, ranks) for value in values]))

    feed_parts = by_part(
        [feed_in, grads_full, jnp.concatenate([grad_gateup_rows, hidden[None]], axis=0)]
    )
    got = lax.all_to_all(by_side(grad_feed_part.astype(BF)), "head", 0, 0, tiled=True)
    mine_feed_grad = jnp.sum(got.astype(F32), axis=0)
    got = lax.all_to_all(by_side(feed_part.astype(BF)), "head", 0, 0, tiled=True)
    feed_out = jnp.sum(got.astype(F32), axis=0)
    mine_resid = lax.dynamic_slice_in_dim(resid, part * local_width, local_width, 1)
    block_output = mine_resid + feed_out
    grad_feed_in = lax.all_gather(mine_feed_grad.astype(BF), "head", axis=1, tiled=True)
    grad_feed_in, feed_parts = lax.optimization_barrier((grad_feed_in, feed_parts))
    grad_feed_in = grad_feed_in.astype(F32)
    grad_gain_two = jnp.sum(mine_feed_grad * mine_resid * scale_two, axis=0)
    weighted = grad_feed_in * gain_two
    grad_resid = (
        grads_full.astype(F32)
        + scale_two * weighted
        - resid * scale_two**3 * jnp.mean(weighted * resid, axis=-1, keepdims=True)
    )
    grad_resid_half = grad_resid.astype(BF)
    grad_mixed = jnp.einsum("td,kd->tk", grad_resid_half, merge_weight, preferred_element_type=F32)

    douts, dupdates, dstate, dgate, grad_output_gain = kernel_call(
        local_back_kernel,
        [(cube, F32), (cube, F32), ((heads, dim, dim), F32), (cube, F32), ((heads, dim), F32)],
        (grad_mixed, outs, projected, output_gain, scores, q, weights, cols),
        3 * heads,
    )
    dq, dk, dcum = kernel_call(
        score_back_kernel,
        [(cube, F32), (cube, F32), ((heads, length, 8), F32)],
        (douts, updates, scores, q, k, cols, incoming),
        4 * heads,
    )

    share = model_width // ranks
    outer, group = plane(ranks)
    places = (rank // group + jnp.arange(outer)) % outer * group + rank % group

    merge_parts = by_part([grad_resid_half, mixed_rows[None]])
    parts = [
        [picked(left, places, share) for left in (feed[0], feed[1], merge[0])] + [feed[2], merge[1]]
        for feed, merge in zip(feed_parts, merge_parts)
    ]
    feed_rows = 3 * hidden_width
    late_blocks = kernel_call(
        functools.partial(
            feature_minor_kernel, len(parts), 3, ((0, 0, 0), (0, 0, 1), (1, 0, 2), (2, 1, 0))
        ),
        [((feed_rows + heads * dim, share), BF)] * outer,
        [places] + [ref for part_refs in parts for ref in part_refs],
        256,
        scalars=1,
    )
    grad_end, late_blocks = scan_back(dstate, maps, ranks, late_blocks)
    late_sum = outer_sum(late_blocks, ranks)
    feed_sum = late_sum[:feed_rows]
    grad_merge = late_sum[feed_rows:]
    grad_gateup = jnp.moveaxis(
        feed_sum[: 2 * hidden_width].reshape(2, hidden_width, share), 2, 0
    )
    grad_down = feed_sum[2 * hidden_width :]

    span_width = heads * width + 128
    grad_rows, grad_conv, grad_params = kernel_call(
        final_back_kernel,
        [((rows, span_width), BF), ((taps, heads, 3 * dim), F32), ((heads, 128), F32)],
        (
            grad_end, dupdates, incoming, updates, inverse, inner, k, q, cols, dq, dk, dcum,
            pre, projected, conv_weight, params, dgate,
        ),
        7 * heads,
        [pltpu.VMEM((rows, 3 * dim), F32), pltpu.VMEM((rows + EDGE, 3 * dim), F32)],
    )
    right_parts = in_group(grad_rows, ranks)
    left_parts = [picked(left, places, share) for left in in_group(normed_ext, ranks)]
    parts = list(zip(left_parts, right_parts))
    blocks = kernel_call(
        functools.partial(feature_major_kernel, len(parts)),
        [((share, span_width), BF)] * outer,
        [places] + [ref for part_refs in parts for ref in part_refs],
        100,
        scalars=1,
    )
    summed_rows = outer_sum(blocks, ranks)
    (sent,) = kernel_call(
        input_back_kernel,
        [((sides, rows, local_width + 128), BF)],
        (grad_rows, wide_weight, inputs_ext, gain_one[None]),
        64,
    )
    got = lax.all_to_all(sent, "head", 0, 0, tiled=True)
    got = jnp.sum(got.astype(F32), axis=0)
    mine_normed = got[:, :local_width]
    stat_total = got[:, local_width : local_width + 1] + got[:, local_width + 1 : local_width + 2]
    mine_ext = lax.dynamic_slice_in_dim(inputs_ext, part * local_width, local_width, 1)
    mine_gain = lax.dynamic_slice_in_dim(gain_one, part * local_width, local_width, 0)
    grad_gain_one = jnp.sum(mine_normed * mine_ext * scale_ext, axis=0)
    input_part = (
        scale_ext * mine_normed * mine_gain
        - mine_ext * scale_ext**3 * (stat_total / model_width)
    )
    from_next = shifted(input_part[:EDGE], "seq", -1)
    mine_resid_grad = lax.dynamic_slice_in_dim(grad_resid, part * local_width, local_width, 1)
    input_grad = mine_resid_grad + input_part[EDGE:]
    input_grad = jnp.concatenate(
        [input_grad[: length - EDGE], input_grad[length - EDGE :] + from_next], axis=0
    )

    small = [
        grad_conv.reshape(-1, 128),
        grad_output_gain.reshape(-1, 128),
        grad_params,
        grad_gain_two.reshape(-1, 128),
        grad_gain_one.reshape(-1, 128),
    ]
    ends = [0]
    for piece in small:
        ends.append(ends[-1] + piece.shape[0])
    total = summed_over(jnp.concatenate(small, axis=0), "seq")
    small = [total[start:end] for start, end in zip(ends, ends[1:])]
    conv_split = 3 * dim // ranks
    gain_split = dim // ranks
    grad_conv_mine = lax.dynamic_slice_in_dim(
        small[0].reshape(taps, heads, 3 * dim), rank * conv_split, conv_split, 2
    )
    grad_output_gain_mine = lax.dynamic_slice_in_dim(
        small[1].reshape(heads, dim), rank * gain_split, gain_split, 1
    )
    grad_params = small[2]
    grad_gain_two = small[3].reshape(-1)
    grad_gain_one = small[4].reshape(-1)
    grad_proj_mine = summed_rows[:, : heads * width].reshape(share, heads, width)
    grad_rate_mine = summed_rows[:, heads * width : heads * (width + 2)].reshape(share, heads, 2)
    return (
        block_output,
        input_grad,
        grad_gain_one,
        grad_proj_mine,
        grad_rate_mine,
        grad_conv_mine,
        grad_params[:, 0],
        grad_params[:, 1],
        grad_params[:, 2],
        grad_output_gain_mine,
        grad_merge,
        grad_gain_two,
        grad_gateup,
        grad_down,
    )


def solution(mesh):
    return jax.shard_map(
        layer,
        mesh=mesh,
        in_specs=(
            P("seq", "head"),
            P("head"),
            P(None, "head", None),
            P(None, "head", None),
            P(None, "head", None),
            P("head"),
            P("head"),
            P("head"),
            P("head", None),
            P("head", None),
            P("head"),
            P(None, None, "head"),
            P("head", None),
            P("seq", "head"),
        ),
        out_specs=(
            P("seq", "head"),
            P("seq", "head"),
            P("head"),
            P("seq", "head", None),
            P("seq", "head", None),
            P(None, "head", "seq"),
            P("head"),
            P("head"),
            P("head"),
            P("head", "seq"),
            P("head", "seq"),
            P("head"),
            P("seq", None, "head"),
            P("head", "seq"),
        ),
        check_vma=False,
    )
```

time: 1090 us -> 282 us (0.26)
  waiting for transfers between devices: 485 us -> 55.9 us
  blocking collectives: 164 us -> 13.9 us
  other arithmetic: 159 us -> 26.5 us
  matrix products: 127 us -> 13.7 us
  local copies, waits for them, and re-layouts: 123 us -> 30.3 us
  starting transfers between devices: 5.35 us -> 94.6 us
  Pallas kernels: 0 us -> 42.3 us
  between operations: 15.1 us -> 1.24 us
    unnamed x19 -> x0, waiting for transfers between devices: 308 us -> none
    all_gather x7 -> x2, blocking collectives: 136 us -> 13.9 us  [the longest x1 7.47 us: layer(): whole = lax.all_gather(packed, 'head', axis=1, tiled=True)]
    reduce_scatter x3 -> x0, waiting for transfers between devices: 111 us -> none  [the longest x1 68.8 us: on_device(): lax.psum_scatter(grad_proj.astype(jnp.bfloat16), 'seq', scatter_dimension...]
    another operation x59 -> x1, other arithmetic: 96.8 us -> 1.28 us  [layer(): params = jnp.stack([decay_log, decay_bias, write_bias])]
    dot_general x100 -> x8, matrix products: 108 us -> 13.7 us  [the longest x1 2.96 us: layer(): jnp.einsum('td,dhe->hte', normed_ext, proj_weight, preferred_element_type...]
    ppermute x2 -> x34, starting transfers between devices: 4.82 us -> 83.1 us  [the longest x12 30.8 us: shifted(): return lax.ppermute(value, axis, pairs)]
    all_gather x3 -> x0, waiting for transfers between devices: 62.5 us -> none  [the longest x1 41.7 us: on_device(): lax.all_gather(offset[None], 'seq', axis=0, tiled=True)]
    ppermute x2 -> x34, waiting for transfers between devices: 4.08 us -> 53.4 us  [the longest x3 19.5 us: summed_over(): lax.ppermute(value, axis, [(i, i ^ step) for i in range(count)])]
  transfers between devices with their start and end apart: 15 -> 37, of which waited for: 12 -> 16; matrix products, arithmetic and copies ran while one was open for 14% -> 20% of each run, Pallas kernels for 0% -> 9%
where the time goes in v1:
time: 282 us; the launch traced here: 278 us
  starting transfers between devices  94.6 us (34%)
  waiting for transfers between devices  55.9 us (20%)
  Pallas kernels  42.3 us (15%)
  local copies, waits for them, and re-layouts  30.3 us (11%)
  other arithmetic  26.5 us (9%)
  blocking collectives  13.9 us (5%)
  matrix products  13.7 us (5%)
    pallas_call x14, Pallas kernels, kernel_call(): pl.pallas_call(body, out_shape=shapes, in_specs=[smem] * scalars + [vmem]...  42.3 us
    ppermute x12, starting transfers between devices, shifted(): return lax.ppermute(value, axis, pairs)  30.8 us
    ppermute x3, starting transfers between devices, summed_over(): lax.ppermute(value, axis, [(i, i ^ step) for i in range(count)])  26.7 us
    ppermute x3, waiting for transfers between devices, summed_over(): lax.ppermute(value, axis, [(i, i ^ step) for i in range(count)])  19.5 us
    ppermute x12, waiting for transfers between devices, shifted(): return lax.ppermute(value, axis, pairs)  16.2 us
    ppermute x13, starting transfers between devices, turned(): return lax.ppermute(value, axis, pairs)  14.1 us
    ppermute x6, starting transfers between devices, outer_sum(): total = total + lax.ppermute(blocks[steps], 'seq', pairs).astype(F32)  11.5 us
    ppermute x13, waiting for transfers between devices, turned(): return lax.ppermute(value, axis, pairs)  9.19 us
  transfers between devices with their start and end apart: 37, of which 16 were waited for; matrix products, arithmetic and copies ran while one was open for 20% of the time, Pallas kernels for 9%

profile of v1, /device:TPU:0, one launch (start us, length us, event | category | flops | bytes accessed | tf_op | source)
XLA Modules:
  0.0 278.4 jit_solution(3311429182693660173)
XLA Ops:
  1.5 5.0 %collective-permute-start = (bf16[8,256]{1,0:T(8,128)(2,1)S(1)}, bf16[8,256]{1,0:T(8,128)(2,1)S(1)}, u32[]{:S(2)}, u32[]{:S(2)}) collective-permute-start(bf16[8,256]{1,0:T(8,128)(2,1)S(1)} %slice.109), channel_id=1, source_target_pairs={{0,4},{4,8},{8,12},{12,16},{16,20},{20,24},{24,28},{1,5},{5,9},{9,... | collective-permute-start | bytes 12296 | tf_op jit(solution)/shard_map/ppermute | solution.py:23
  7.8 3.6 %copy.65 = bf16[128,8,2,512]{3,1,2,0:T(8,128)(2,1)} copy(bf16[128,8,2,512]{3,2,1,0:T(2,128)(2,1)} %bitcast.140) | data formatting | bytes 4194304
  12.4 7.5 %all_gather.6 = bf16[280,1024]{1,0:T(8,128)(2,1)S(1)} all-gather(bf16[280,256]{1,0:T(8,128)(2,1)S(1)} %constant_dynamic-update-slice_fusion), channel_id=1, replica_groups=mesh['seq'=8,'head'=4] {'head'}, dimensions={1}, use_global_device_ids=true | all-gather | bytes 716800 | tf_op jit(solution)/shard_map/all_gather | solution.py:485
  20.2 3.0 %fusion.4.proj_ref.gate_ref = f32[2,136,512]{2,1,0:T(8,128)} fusion(bf16[1024,2,512]{2,1,0:T(2,128)(2,1)} %param.16, bf16[136,1024]{1,0:T(8,128)(2,1)S(1)} %multiply_convert_fusion.refs_0_), kind=kOutput, calls=%fused_computation.6 | convolution fusion | flops 285212672 | bytes 2932736 | tf_op jit(solution)/shard_map/td,dhe->hte/dot_general | solution.py:498
  26.3 7.3 %shard_map.245 = (f32[2,128,384]{2,1,0:T(8,128)}, f32[2,128,128]{2,1,0:T(8,128)}, f32[2,128,128]{2,1,0:T(8,128)}, f32[2,128,128]{2,1,0:T(8,128)}, f32[2,128,128]...) custom-call(f32[2,136,512]{2,1,0:T(8,128)} %fusion.4.proj_ref.gate_r, ...), custom_call_target="tpu_custom_call" | custom-call | flops 452984832 | bytes 571416 | tf_op jit(solution)/shard_map/pallas_call | solution.py:394
  33.7 4.2 %collective-permute-start.1 = (f32[2,2,128,128]{3,2,1,0:T(8,128)}, f32[2,2,128,128]{3,2,1,0:T(8,128)}, u32[]{:S(2)}, u32[]{:S(2)}) collective-permute-start(f32[2,2,128,128]{3,2,1,0:T(8,128)} %get-tuple-element.75.late_ref), channel_id=1, source_target_pairs={{0,4},{4,8},{8,12},{12,16},{16,20},{20,24},{24,28},{1,5},{5,9},{9,... | collective-permute-start | bytes 786440 | tf_op jit(solution)/shard_map/ppermute | solution.py:23
  37.8 3.3 %fusion.1.weight_ref = bf16[1024,1152]{1,0:T(8,128)(2,1)} fusion(bf16[1024,4]{1,0:T(8,128)(2,1)} %bitcast.141, bf16[1024,1024]{1,0:T(8,128)(2,1)} %bitcast.139), kind=kLoop, calls=%fused_computation.2 | loop fusion | flops 7077888 | bytes 4464640 | tf_op jit(solution)/shard_map/concatenate | solution.py:518
  42.8 2.0 shard_map.246.late_ref
  44.7 6.0 %collective-permute-start.2 = (f32[2,2,128,128]{3,2,1,0:T(8,128)}, f32[2,2,128,128]{3,2,1,0:T(8,128)}, u32[]{:S(2)}, u32[]{:S(2)}) collective-permute-start(f32[2,2,128,128]{3,2,1,0:T(8,128)} %shard_map.246.late_ref), channel_id=1, source_target_pairs={{0,8},{4,12},{8,16},{12,20},{16,24},{20,28},{1,9},{5,13},{9,17},{1... | collective-permute-start | bytes 786440 | tf_op jit(solution)/shard_map/ppermute | solution.py:23
  53.0 3.1 %pad_maximum_fusion = bf16[1024,1024]{1,0:T(8,128)(2,1)} fusion(bf16[256,1024]{1,0:T(8,128)(2,1)} %collective-permute-done.6, bf16[256,1024]{1,0:T(8,128)(2,1)} %collective-permute-done.5, bf16[256,1024]{1,0:T(8,128)(2,1)} %collective-permute-done.4, bf16[256,1024]{1,0:T(8,128)(2,1)} %param.23), kind=kLoop, calls=%fused_computation.3 | loop fusion | flops 8388608 | bytes 4194304 | tf_op jit(solution)/shard_map/concatenate | solution.py:492
  56.1 2.5 collective-permute-done.3.map_ref
  59.2 2.0 shard_map.247
  61.2 4.2 %collective-permute-start.7 = (f32[2,2,128,128]{3,2,1,0:T(8,128)}, f32[2,2,128,128]{3,2,1,0:T(8,128)}, u32[]{:S(2)}, u32[]{:S(2)}) collective-permute-start(f32[2,2,128,128]{3,2,1,0:T(8,128)} %shard_map.247), channel_id=1, source_target_pairs={{0,4},{4,8},{8,12},{12,16},{16,20},{20,24},{24,28},{1,5},{5,9},{9,... | collective-permute-start | bytes 786440 | tf_op jit(solution)/shard_map/ppermute | solution.py:23
  67.0 2.5 collective-permute-start.8
  71.7 6.4 %collective-permute-done.9.map_ref = f32[2,128,128]{2,1,0:T(8,128)} collective-permute-done((f32[2,128,128]{2,1,0:T(8,128)}, f32[2,128,128]{2,1,0:T(8,128)}, u32[]{:S(2)}, u32[]{:S(2)}) %collective-permute-start.9) | collective-permute-done | bytes 131104 | tf_op jit(solution)/shard_map/ppermute | solution.py:23
  81.6 2.7 shard_map.249
  89.5 2.2 multiply_reduce_fusion.2
  93.0 2.1 fusion.33
  100.2 4.0 %all-to-all-start.1 = ((bf16[4,128,256]{2,1,0:T(8,128)(2,1)}), bf16[4,128,256]{2,1,0:T(8,128)(2,1)}, u32[]{:S(2)}, u32[]{:S(2)}) async-start(bf16[4,128,256]{2,1,0:T(8,128)(2,1)} %bitcast.143), calls=%async_computation.1 | async-start | bytes 524288 | tf_op jit(solution)/shard_map/all_to_all | solution.py:562
  107.9 2.5 all-to-all-done.1
  110.4 4.0 %all-to-all-start = ((bf16[4,128,256]{2,1,0:T(8,128)(2,1)}), bf16[4,128,256]{2,1,0:T(8,128)(2,1)}, u32[]{:S(2)}, u32[]{:S(2)}) async-start(bf16[4,128,256]{2,1,0:T(8,128)(2,1)} %bitcast.142), calls=%async_computation | async-start | bytes 524288 | tf_op jit(solution)/shard_map/all_to_all | solution.py:564
  114.4 2.1 pad_maximum_fusion.1.refs_3_
  116.5 2.1 copy.56
  123.0 6.4 %all_gather.7 = bf16[128,1024]{1,0:T(8,128)(2,1)S(1)} all-gather(bf16[128,256]{1,0:T(8,128)(2,1)S(1)} %get-tuple-element.155), channel_id=1, replica_groups=mesh['seq'=8,'head'=4] {'head'}, dimensions={1}, use_global_device_ids=true | all-gather | bytes 327680 | tf_op jit(solution)/shard_map/all_gather | solution.py:568
  129.4 4.1 %collective-permute-done.15 = bf16[3,128,704]{1,2,0:T(8,128)(2,1)} collective-permute-done((bf16[3,128,704]{1,2,0:T(8,128)(2,1)}, bf16[3,128,704]{1,2,0:T(8,128)(2,1)}, u32[]{:S(2)}, u32[]{:S(2)}) %collective-permute-start.15) | collective-permute-done | bytes 540704 | tf_op jit(solution)/shard_map/ppermute | solution.py:36
  133.7 2.1 fusion.49
  137.0 2.1 fusion.52.grad_ref
  139.1 2.7 shard_map.250
  143.1 2.7 collective-permute-start.19
  146.3 2.1 copy.57.refs_8_
  154.5 4.2 %shard_map.252 = (bf16[2368,128]{1,0:T(8,128)(2,1)}, bf16[2368,128]{1,0:T(8,128)(2,1)}, bf16[2368,128]{1,0:T(8,128)(2,1)}, bf16[2368,128]{1,0:T(8,128)(2,1)}) custom-call(s32[4]{0:T(128)} %fusion.42.place_ref, bf16[128,1024]{1,0:T(8,128)(2,1)} %multiply_convert_fusion.1.refs_0_, bf16[128,1024]{1,0:T(8,128)(2,1)} %slice.123.refs_1_, ...), custom_call_target="tpu_custom_call" | custom-call | flops 3221225472 | bytes 2785296 | tf_op jit(solution)/shard_map/pallas_call | solution.py:394
  164.1 2.7 shard_map.255
  166.9 3.7 %collective-permute-done.20.first_ref = f32[2,128,128]{2,1,0:T(8,128)S(1)} collective-permute-done((f32[2,128,128]{2,1,0:T(8,128)}, f32[2,128,128]{2,1,0:T(8,128)S(1)}, u32[]{:S(2)}, u32[]{:S(2)}) %collective-permute-start.20) | collective-permute-done | bytes 131104 | tf_op jit(solution)/shard_map/ppermute | solution.py:23
  173.9 4.5 %shard_map.256 = (bf16[136,1152]{1,0:T(8,128)(2,1)}, f32[4,2,384]{2,1,0:T(2,128)}, f32[2,128]{1,0:T(2,128)}) custom-call(f32[2,128,128]{2,1,0:T(8,128)} %shard_map.254.dend_ref, f32[2,128,128]{2,1,0:T(8,128)} %get-tuple-element.100.dupd_ref, f32[2,128,128]{2,1,0:T(8,128)} %shard_map.248.state_ref, f32[2,128,128]{2,1,0:T(8,128)} %get-tuple-element.101.upd_ref, ...), custom_call_target="tpu_custom_call" | custom-call | flops 176160768 | bytes 2420760 | tf_op jit(solution)/shard_map/pallas_call | solution.py:394
  178.5 3.6 %shard_map.257 = bf16[4,136,384]{2,1,0:T(8,128)(2,1)} custom-call(bf16[136,1152]{1,0:T(8,128)(2,1)} %get-tuple-element.111.rows_ref.refs_1_, bf16[1024,1152]{1,0:T(8,128)(2,1)} %fusion.1.weight_ref, f32[136,1024]{1,0:T(8,128)} %copy-done.2, f32[1,1024]{1,0:T(1,128)} %copy-done.18), custom_call_target="tpu_custom_call" | custom-call | flops 805306368 | bytes 3233792 | tf_op jit(solution)/shard_map/pallas_call | solution.py:394
  182.1 3.5 %all-to-all-start.2 = ((bf16[4,136,384]{2,1,0:T(8,128)(2,1)}), bf16[4,136,384]{2,1,0:T(8,128)(2,1)S(1)}, u32[]{:S(2)}, u32[]{:S(2)}) async-start(bf16[4,136,384]{2,1,0:T(8,128)(2,1)} %shard_map.257), calls=%async_computation.2 | async-start | bytes 835584 | tf_op jit(solution)/shard_map/all_to_all | solution.py:650
  185.6 2.6 collective-permute-start.26
  190.9 2.8 %collective-permute-start.33 = (bf16[2368,128]{1,0:T(8,128)(2,1)}, bf16[2368,128]{1,0:T(8,128)(2,1)}, u32[]{:S(2)}, u32[]{:S(2)}) collective-permute-start(bf16[2368,128]{1,0:T(8,128)(2,1)} %get-tuple-element.123), channel_id=1, source_target_pairs={{0,24},{4,28},{8,0},{12,4},{16,8},{20,12},{24,16},{28,20},{1,25},{... | collective-permute-start | bytes 1818632 | tf_op jit(solution)/shard_map/ppermute | solution.py:58
  196.7 2.0 collective-permute-start.23
  198.7 4.1 %collective-permute-done.27.refs_3_ = bf16[136,1152]{1,0:T(8,128)(2,1)} collective-permute-done((bf16[136,1152]{1,0:T(8,128)(2,1)}, bf16[136,1152]{1,0:T(8,128)(2,1)}, u32[]{:S(2)}, u32[]{:S(2)}) %collective-permute-start.27) | collective-permute-done | bytes 313376 | tf_op jit(solution)/shard_map/ppermute | solution.py:36
  204.1 2.9 %shard_map.258 = (bf16[128,1152]{1,0:T(8,128)(2,1)}, bf16[128,1152]{1,0:T(8,128)(2,1)}, bf16[128,1152]{1,0:T(8,128)(2,1)}, bf16[128,1152]{1,0:T(8,128)(2,1)}) custom-call(s32[4]{0:T(128)} %fusion.42.place_ref, bf16[136,1024]{1,0:T(8,128)(2,1)} %copy-done.7, bf16[136,1152]{1,0:T(8,128)(2,1)} %get-tuple-element.111.rows_ref.refs_1_, ...), custom_call_target="tpu_custom_call" | custom-call | flops 1258291200 | bytes 1183760 | tf_op jit(solution)/shard_map/pallas_call | solution.py:394
  207.9 3.6 %collective-permute-start.28 = (bf16[128,1152]{1,0:T(8,128)(2,1)}, bf16[128,1152]{1,0:T(8,128)(2,1)}, u32[]{:S(2)}, u32[]{:S(2)}) collective-permute-start(bf16[128,1152]{1,0:T(8,128)(2,1)} %get-tuple-element.117), channel_id=1, source_target_pairs={{0,8},{4,12},{8,16},{12,20},{16,24},{20,28},{24,0},{28,4},{1,9},{5... | collective-permute-start | bytes 884744 | tf_op jit(solution)/shard_map/ppermute | solution.py:58
  211.5 8.6 %collective-permute-start.24 = (f32[32,128]{1,0:T(8,128)S(1)}, f32[32,128]{1,0:T(8,128)S(1)}, u32[]{:S(2)}, u32[]{:S(2)}) collective-permute-start(f32[32,128]{1,0:T(8,128)S(1)} %add.145), channel_id=1, source_target_pairs={{0,8},{4,12},{8,0},{12,4},{16,24},{20,28},{24,16},{28,20},{1,9},{5... | collective-permute-start | bytes 49160 | tf_op jit(solution)/shard_map/ppermute | solution.py:48
  220.8 18.5 %collective-permute-done.24 = f32[32,128]{1,0:T(8,128)S(1)} collective-permute-done((f32[32,128]{1,0:T(8,128)S(1)}, f32[32,128]{1,0:T(8,128)S(1)}, u32[]{:S(2)}, u32[]{:S(2)}) %collective-permute-start.24) | collective-permute-done | bytes 16416 | tf_op jit(solution)/shard_map/ppermute | solution.py:48
  239.3 16.1 %collective-permute-start.25 = (f32[32,128]{1,0:T(8,128)S(1)}, f32[32,128]{1,0:T(8,128)S(1)}, u32[]{:S(2)}, u32[]{:S(2)}) collective-permute-start(f32[32,128]{1,0:T(8,128)S(1)} %add.146), channel_id=1, source_target_pairs={{0,16},{4,20},{8,24},{12,28},{16,0},{20,4},{24,8},{28,12},{1,17},{... | collective-permute-start | bytes 49160 | tf_op jit(solution)/shard_map/ppermute | solution.py:48
  257.1 2.9 %collective-permute-start.29 = (bf16[128,1152]{1,0:T(8,128)(2,1)}, bf16[128,1152]{1,0:T(8,128)(2,1)}, u32[]{:S(2)}, u32[]{:S(2)}) collective-permute-start(bf16[128,1152]{1,0:T(8,128)(2,1)} %get-tuple-element.118), channel_id=1, source_target_pairs={{0,16},{4,20},{8,24},{12,28},{16,0},{20,4},{24,8},{28,12},{1,17},{... | collective-permute-start | bytes 884744 | tf_op jit(solution)/shard_map/ppermute | solution.py:58
  266.8 4.6 %collective-permute-done.29 = bf16[128,1152]{1,0:T(8,128)(2,1)} collective-permute-done((bf16[128,1152]{1,0:T(8,128)(2,1)}, bf16[128,1152]{1,0:T(8,128)(2,1)}, u32[]{:S(2)}, u32[]{:S(2)}) %collective-permute-start.29) | collective-permute-done | bytes 294944 | tf_op jit(solution)/shard_map/ppermute | solution.py:58
  271.4 3.9 %collective-permute-done.30 = bf16[128,1152]{1,0:T(8,128)(2,1)S(1)} collective-permute-done((bf16[128,1152]{1,0:T(8,128)(2,1)}, bf16[128,1152]{1,0:T(8,128)(2,1)S(1)}, u32[]{:S(2)}, u32[]{:S(2)}) %collective-permute-start.30) | collective-permute-done | bytes 294944 | tf_op jit(solution)/shard_map/ppermute | solution.py:58
  (174 shorter events, 76.2 us)
Async XLA Ops:
  0.6 92.4 %copy-start = (bf16[1024,2,704]{0,2,1:T(8,128)(2,1)S(1)}, bf16[1024,2,704]{0,2,1:T(8,128)(2,1)}, u32[]{:S(2)}) copy-start(bf16[1024,2,704]{0,2,1:T(8,128)(2,1)} %param.25) | copy-start | bytes 8650756
  1.5 10.8 %collective-permute-start = (bf16[8,256]{1,0:T(8,128)(2,1)S(1)}, bf16[8,256]{1,0:T(8,128)(2,1)S(1)}, u32[]{:S(2)}, u32[]{:S(2)}) collective-permute-start(bf16[8,256]{1,0:T(8,128)(2,1)S(1)} %slice.109), channel_id=1, source_target_pairs={{0,4},{4,8},{8,12},{12,16},{16,20},{20,24},{24,28},{1,5},{5,9},{9,... | collective-permute-start | bytes 12296 | tf_op jit(solution)/shard_map/ppermute | solution.py:23
  7.8 4.6 %copy-start.25 = (bf16[256]{0:T(256)(128)(2,1)S(1)}, bf16[256]{0:T(256)(128)(2,1)}, u32[]{:S(2)}) copy-start(bf16[256]{0:T(256)(128)(2,1)} %param.24) | copy-start | bytes 1540
  7.8 4.6 %copy-start.17 = (bf16[128,256]{1,0:T(8,128)(2,1)S(1)}, bf16[128,256]{1,0:T(8,128)(2,1)}, u32[]{:S(2)}) copy-start(bf16[128,256]{1,0:T(8,128)(2,1)} %param.27) | copy-start | bytes 196612
  19.9 67.0 %copy-start.1 = (bf16[280,1024]{1,0:T(8,128)(2,1)}, bf16[280,1024]{1,0:T(8,128)(2,1)S(1)}, u32[]{:S(2)}) copy-start(bf16[280,1024]{1,0:T(8,128)(2,1)S(1)} %all_gather.6) | copy-start | bytes 1720324
  24.1 28.9 %collective-permute-start.4 = (bf16[256,1024]{1,0:T(8,128)(2,1)}, bf16[256,1024]{1,0:T(8,128)(2,1)}, u32[]{:S(2)}, u32[]{:S(2)}) collective-permute-start(bf16[256,1024]{1,0:T(8,128)(2,1)} %param.23), channel_id=1, source_target_pairs={{0,1},{1,2},{2,3},{3,0},{4,5},{5,6},{6,7},{7,4},{8,9},{9,10},{10,1... | collective-permute-start | bytes 1572872 | tf_op jit(solution)/shard_map/ppermute | solution.py:36
  24.4 28.6 %collective-permute-start.5 = (bf16[256,1024]{1,0:T(8,128)(2,1)}, bf16[256,1024]{1,0:T(8,128)(2,1)}, u32[]{:S(2)}, u32[]{:S(2)}) collective-permute-start(bf16[256,1024]{1,0:T(8,128)(2,1)} %param.23), channel_id=1, source_target_pairs={{0,2},{1,3},{2,0},{3,1},{4,6},{5,7},{6,4},{7,5},{8,10},{9,11},{10,... | collective-permute-start | bytes 1572872 | tf_op jit(solution)/shard_map/ppermute | solution.py:36
  25.2 27.8 %collective-permute-start.6 = (bf16[256,1024]{1,0:T(8,128)(2,1)}, bf16[256,1024]{1,0:T(8,128)(2,1)}, u32[]{:S(2)}, u32[]{:S(2)}) collective-permute-start(bf16[256,1024]{1,0:T(8,128)(2,1)} %param.23), channel_id=1, source_target_pairs={{0,3},{1,0},{2,1},{3,2},{4,7},{5,4},{6,5},{7,6},{8,11},{9,8},{10,9... | collective-permute-start | bytes 1572872 | tf_op jit(solution)/shard_map/ppermute | solution.py:36
  33.7 9.1 %collective-permute-start.1 = (f32[2,2,128,128]{3,2,1,0:T(8,128)}, f32[2,2,128,128]{3,2,1,0:T(8,128)}, u32[]{:S(2)}, u32[]{:S(2)}) collective-permute-start(f32[2,2,128,128]{3,2,1,0:T(8,128)} %get-tuple-element.75.late_ref), channel_id=1, source_target_pairs={{0,4},{4,8},{8,12},{12,16},{16,20},{20,24},{24,28},{1,5},{5,9},{9,... | collective-permute-start | bytes 786440 | tf_op jit(solution)/shard_map/ppermute | solution.py:23
  44.7 14.5 %collective-permute-start.2 = (f32[2,2,128,128]{3,2,1,0:T(8,128)}, f32[2,2,128,128]{3,2,1,0:T(8,128)}, u32[]{:S(2)}, u32[]{:S(2)}) collective-permute-start(f32[2,2,128,128]{3,2,1,0:T(8,128)} %shard_map.246.late_ref), channel_id=1, source_target_pairs={{0,8},{4,12},{8,16},{12,20},{16,24},{20,28},{1,9},{5,13},{9,17},{1... | collective-permute-start | bytes 786440 | tf_op jit(solution)/shard_map/ppermute | solution.py:23
  51.7 6.9 %collective-permute-start.3 = (f32[2,128,128]{2,1,0:T(8,128)S(1)}, f32[2,128,128]{2,1,0:T(8,128)S(1)}, u32[]{:S(2)}, u32[]{:S(2)}) collective-permute-start(f32[2,128,128]{2,1,0:T(8,128)S(1)} %slice_bitcast_fusion.4), channel_id=1, source_target_pairs={{4,0},{8,4},{12,8},{16,12},{20,16},{24,20},{28,24},{5,1},{9,5},{13... | collective-permute-start | bytes 393224 | tf_op jit(solution)/shard_map/ppermute | solution.py:23
  61.2 16.9 %collective-permute-start.7 = (f32[2,2,128,128]{3,2,1,0:T(8,128)}, f32[2,2,128,128]{3,2,1,0:T(8,128)}, u32[]{:S(2)}, u32[]{:S(2)}) collective-permute-start(f32[2,2,128,128]{3,2,1,0:T(8,128)} %shard_map.247), channel_id=1, source_target_pairs={{0,4},{4,8},{8,12},{12,16},{16,20},{20,24},{24,28},{1,5},{5,9},{9,... | collective-permute-start | bytes 786440 | tf_op jit(solution)/shard_map/ppermute | solution.py:23
  67.0 4.6 %collective-permute-start.8 = (f32[2,128,128]{2,1,0:T(8,128)}, f32[2,128,128]{2,1,0:T(8,128)}, u32[]{:S(2)}, u32[]{:S(2)}) collective-permute-start(f32[2,128,128]{2,1,0:T(8,128)} %get-tuple-element.154), channel_id=1, source_target_pairs={{0,20},{4,24},{8,28},{1,21},{5,25},{9,29},{2,22},{6,26},{10,30},{3... | collective-permute-start | bytes 393224 | tf_op jit(solution)/shard_map/ppermute | solution.py:23
  69.5 8.6 %collective-permute-start.9 = (f32[2,128,128]{2,1,0:T(8,128)}, f32[2,128,128]{2,1,0:T(8,128)}, u32[]{:S(2)}, u32[]{:S(2)}) collective-permute-start(f32[2,128,128]{2,1,0:T(8,128)} %get-tuple-element.153), channel_id=1, source_target_pairs={{16,0},{20,4},{24,8},{28,12},{17,1},{21,5},{25,9},{29,13},{18,2},{... | collective-permute-start | bytes 393224 | tf_op jit(solution)/shard_map/ppermute | solution.py:23
  84.3 4.2 %collective-permute-start.10 = (bf16[128,256]{1,0:T(8,128)(2,1)}, bf16[128,256]{1,0:T(8,128)(2,1)S(1)}, u32[]{:S(2)}, u32[]{:S(2)}) collective-permute-start(bf16[128,256]{1,0:T(8,128)(2,1)} %get-tuple-element.81), channel_id=1, source_target_pairs={{0,1},{1,2},{2,3},{3,0},{4,5},{5,6},{6,7},{7,4},{8,9},{9,10},{10,1... | collective-permute-start | bytes 196616 | tf_op jit(solution)/shard_map/ppermute | solution.py:36
  84.3 5.2 %collective-permute-start.11 = (bf16[128,256]{1,0:T(8,128)(2,1)}, bf16[128,256]{1,0:T(8,128)(2,1)S(1)}, u32[]{:S(2)}, u32[]{:S(2)}) collective-permute-start(bf16[128,256]{1,0:T(8,128)(2,1)} %get-tuple-element.81), channel_id=1, source_target_pairs={{0,2},{1,3},{2,0},{3,1},{4,6},{5,7},{6,4},{7,5},{8,10},{9,11},{10,... | collective-permute-start | bytes 196616 | tf_op jit(solution)/shard_map/ppermute | solution.py:36
  85.3 4.2 %collective-permute-start.12 = (bf16[128,256]{1,0:T(8,128)(2,1)}, bf16[128,256]{1,0:T(8,128)(2,1)S(1)}, u32[]{:S(2)}, u32[]{:S(2)}) collective-permute-start(bf16[128,256]{1,0:T(8,128)(2,1)} %get-tuple-element.81), channel_id=1, source_target_pairs={{0,3},{1,0},{2,1},{3,2},{4,7},{5,4},{6,5},{7,6},{8,11},{9,8},{10,9... | collective-permute-start | bytes 196616 | tf_op jit(solution)/shard_map/ppermute | solution.py:36
  87.7 41.7 %collective-permute-start.14 = (bf16[128,1024]{1,0:T(8,128)(2,1)}, bf16[128,1024]{1,0:T(8,128)(2,1)}, u32[]{:S(2)}, u32[]{:S(2)}) collective-permute-start(bf16[128,1024]{1,0:T(8,128)(2,1)} %slice.123.refs_1_), channel_id=1, source_target_pairs={{0,4},{4,0},{8,12},{12,8},{16,20},{20,16},{24,28},{28,24},{1,5},{5... | collective-permute-start | bytes 786440 | tf_op jit(solution)/shard_map/ppermute | solution.py:36
  98.0 31.4 %collective-permute-start.13 = (bf16[128,1024]{1,0:T(8,128)(2,1)}, bf16[128,1024]{1,0:T(8,128)(2,1)}, u32[]{:S(2)}, u32[]{:S(2)}) collective-permute-start(bf16[128,1024]{1,0:T(8,128)(2,1)} %multiply_convert_fusion.1.refs_0_), channel_id=1, source_target_pairs={{0,4},{4,0},{8,12},{12,8},{16,20},{20,16},{24,28},{28,24},{1,5},{5... | collective-permute-start | bytes 786440 | tf_op jit(solution)/shard_map/ppermute | solution.py:36
  100.2 10.1 %all-to-all-start.1 = ((bf16[4,128,256]{2,1,0:T(8,128)(2,1)}), bf16[4,128,256]{2,1,0:T(8,128)(2,1)}, u32[]{:S(2)}, u32[]{:S(2)}) async-start(bf16[4,128,256]{2,1,0:T(8,128)(2,1)} %bitcast.143), calls=%async_computation.1 | async-start | bytes 524288 | tf_op jit(solution)/shard_map/all_to_all | solution.py:562
  110.4 10.4 %all-to-all-start = ((bf16[4,128,256]{2,1,0:T(8,128)(2,1)}), bf16[4,128,256]{2,1,0:T(8,128)(2,1)}, u32[]{:S(2)}, u32[]{:S(2)}) async-start(bf16[4,128,256]{2,1,0:T(8,128)(2,1)} %bitcast.142), calls=%async_computation | async-start | bytes 524288 | tf_op jit(solution)/shard_map/all_to_all | solution.py:564
  118.6 15.0 %collective-permute-start.15 = (bf16[3,128,704]{1,2,0:T(8,128)(2,1)}, bf16[3,128,704]{1,2,0:T(8,128)(2,1)}, u32[]{:S(2)}, u32[]{:S(2)}) collective-permute-start(bf16[3,128,704]{1,2,0:T(8,128)(2,1)} %copy.56), channel_id=1, source_target_pairs={{0,4},{4,0},{8,12},{12,8},{16,20},{20,16},{24,28},{28,24},{1,5},{5... | collective-permute-start | bytes 1622024 | tf_op jit(solution)/shard_map/ppermute | solution.py:36
  133.7 9.4 %copy-start.16 = (bf16[128,256]{1,0:T(8,128)(2,1)S(1)}, bf16[128,256]{1,0:T(8,128)(2,1)}, u32[]{:S(2)}) copy-start(bf16[128,256]{1,0:T(8,128)(2,1)} %get-tuple-element.81) | copy-start | bytes 196612
  135.8 17.4 %collective-permute-start.18 = (bf16[128,1024]{1,0:T(8,128)(2,1)}, bf16[128,1024]{1,0:T(8,128)(2,1)S(1)}, u32[]{:S(2)}, u32[]{:S(2)}) collective-permute-start(bf16[128,1024]{1,0:T(8,128)(2,1)} %get-tuple-element.141.refs_2_), channel_id=1, source_target_pairs={{0,4},{4,0},{8,12},{12,8},{16,20},{20,16},{24,28},{28,24},{1,5},{5... | collective-permute-start | bytes 786440 | tf_op jit(solution)/shard_map/ppermute | solution.py:36
  141.8 7.5 %collective-permute-start.16 = (f32[2,128,128]{2,1,0:T(8,128)}, f32[2,128,128]{2,1,0:T(8,128)S(1)}, u32[]{:S(2)}, u32[]{:S(2)}) collective-permute-start(f32[2,128,128]{2,1,0:T(8,128)} %get-tuple-element.85.second_ref), channel_id=1, source_target_pairs={{4,0},{8,4},{12,8},{16,12},{20,16},{24,20},{28,24},{5,1},{9,5},{13... | collective-permute-start | bytes 393224 | tf_op jit(solution)/shard_map/ppermute | solution.py:23
  143.1 10.1 %collective-permute-start.19 = (bf16[1,128,256]{2,1,0:T(8,128)(2,1)S(1)}, bf16[1,128,256]{2,1,0:T(8,128)(2,1)S(1)}, u32[]{:S(2)}, u32[]{:S(2)}) collective-permute-start(bf16[1,128,256]{2,1,0:T(8,128)(2,1)S(1)} %bitcast.151), channel_id=1, source_target_pairs={{0,4},{4,0},{8,12},{12,8},{16,20},{20,16},{24,28},{28,24},{1,5},{5... | collective-permute-start | bytes 196616 | tf_op jit(solution)/shard_map/ppermute | solution.py:36
  151.9 7.1 %collective-permute-start.17 = (f32[2,128,128]{2,1,0:T(8,128)}, f32[2,128,128]{2,1,0:T(8,128)S(1)}, u32[]{:S(2)}, u32[]{:S(2)}) collective-permute-start(f32[2,128,128]{2,1,0:T(8,128)} %shard_map.251.second_ref), channel_id=1, source_target_pairs={{8,0},{12,4},{16,8},{20,12},{24,16},{28,20},{9,1},{13,5},{17,9},{2... | collective-permute-start | bytes 393224 | tf_op jit(solution)/shard_map/ppermute | solution.py:23
  161.6 9.0 %collective-permute-start.20 = (f32[2,128,128]{2,1,0:T(8,128)}, f32[2,128,128]{2,1,0:T(8,128)S(1)}, u32[]{:S(2)}, u32[]{:S(2)}) collective-permute-start(f32[2,128,128]{2,1,0:T(8,128)} %shard_map.253), channel_id=1, source_target_pairs={{20,0},{24,4},{28,8},{21,1},{25,5},{29,9},{22,2},{26,6},{30,10},{2... | collective-permute-start | bytes 393224 | tf_op jit(solution)/shard_map/ppermute | solution.py:23
  162.8 8.5 %collective-permute-start.21 = (f32[2,128,128]{2,1,0:T(8,128)}, f32[2,128,128]{2,1,0:T(8,128)S(1)}, u32[]{:S(2)}, u32[]{:S(2)}) collective-permute-start(f32[2,128,128]{2,1,0:T(8,128)} %shard_map.253), channel_id=1, source_target_pairs={{4,0},{8,4},{12,8},{16,12},{20,16},{24,20},{28,24},{5,1},{9,5},{13... | collective-permute-start | bytes 393224 | tf_op jit(solution)/shard_map/ppermute | solution.py:23
  178.4 15.3 %copy-start.19 = (f32[4,2,384]{2,1,0:T(2,128)S(1)}, f32[4,2,384]{2,1,0:T(2,128)}, u32[]{:S(2)}) copy-start(f32[4,2,384]{2,1,0:T(2,128)} %get-tuple-element.113) | copy-start | bytes 36868
  178.4 16.7 %copy-start.21 = (f32[256]{0:T(256)S(1)}, f32[256]{0:T(256)}, u32[]{:S(2)}) copy-start(f32[256]{0:T(256)} %get-tuple-element.149) | copy-start | bytes 3076
  178.5 16.6 %copy-start.22 = (f32[2,128]{1,0:T(2,128)S(1)}, f32[2,128]{1,0:T(2,128)}, u32[]{:S(2)}) copy-start(f32[2,128]{1,0:T(2,128)} %get-tuple-element.114) | copy-start | bytes 3076
  178.5 16.6 %copy-start.23 = (f32[2,128]{1,0:T(2,128)S(1)}, f32[2,128]{1,0:T(2,128)}, u32[]{:S(2)}) copy-start(f32[2,128]{1,0:T(2,128)} %get-tuple-element.115) | copy-start | bytes 3076
  182.1 11.7 %all-to-all-start.2 = ((bf16[4,136,384]{2,1,0:T(8,128)(2,1)}), bf16[4,136,384]{2,1,0:T(8,128)(2,1)S(1)}, u32[]{:S(2)}, u32[]{:S(2)}) async-start(bf16[4,136,384]{2,1,0:T(8,128)(2,1)} %shard_map.257), calls=%async_computation.2 | async-start | bytes 835584 | tf_op jit(solution)/shard_map/all_to_all | solution.py:650
  185.6 11.2 %collective-permute-start.26 = (bf16[136,1024]{1,0:T(8,128)(2,1)}, bf16[136,1024]{1,0:T(8,128)(2,1)}, u32[]{:S(2)}, u32[]{:S(2)}) collective-permute-start(bf16[136,1024]{1,0:T(8,128)(2,1)} %copy-done.7), channel_id=1, source_target_pairs={{0,4},{4,0},{8,12},{12,8},{16,20},{20,16},{24,28},{28,24},{1,5},{5... | collective-permute-start | bytes 835592 | tf_op jit(solution)/shard_map/ppermute | solution.py:36
  188.8 73.9 %collective-permute-start.31 = (bf16[2368,128]{1,0:T(8,128)(2,1)}, bf16[2368,128]{1,0:T(8,128)(2,1)}, u32[]{:S(2)}, u32[]{:S(2)}) collective-permute-start(bf16[2368,128]{1,0:T(8,128)(2,1)} %get-tuple-element.121), channel_id=1, source_target_pairs={{0,8},{4,12},{8,16},{12,20},{16,24},{20,28},{24,0},{28,4},{1,9},{5... | collective-permute-start | bytes 1818632 | tf_op jit(solution)/shard_map/ppermute | solution.py:58
  189.9 72.7 %collective-permute-start.32 = (bf16[2368,128]{1,0:T(8,128)(2,1)}, bf16[2368,128]{1,0:T(8,128)(2,1)}, u32[]{:S(2)}, u32[]{:S(2)}) collective-permute-start(bf16[2368,128]{1,0:T(8,128)(2,1)} %get-tuple-element.122), channel_id=1, source_target_pairs={{0,16},{4,20},{8,24},{12,28},{16,0},{20,4},{24,8},{28,12},{1,17},{... | collective-permute-start | bytes 1818632 | tf_op jit(solution)/shard_map/ppermute | solution.py:58
  190.9 71.8 %collective-permute-start.33 = (bf16[2368,128]{1,0:T(8,128)(2,1)}, bf16[2368,128]{1,0:T(8,128)(2,1)}, u32[]{:S(2)}, u32[]{:S(2)}) collective-permute-start(bf16[2368,128]{1,0:T(8,128)(2,1)} %get-tuple-element.123), channel_id=1, source_target_pairs={{0,24},{4,28},{8,0},{12,4},{16,8},{20,12},{24,16},{28,20},{1,25},{... | collective-permute-start | bytes 1818632 | tf_op jit(solution)/shard_map/ppermute | solution.py:58
  193.8 9.1 %collective-permute-start.27 = (bf16[136,1152]{1,0:T(8,128)(2,1)}, bf16[136,1152]{1,0:T(8,128)(2,1)}, u32[]{:S(2)}, u32[]{:S(2)}) collective-permute-start(bf16[136,1152]{1,0:T(8,128)(2,1)} %get-tuple-element.111.rows_ref.refs_1_), channel_id=1, source_target_pairs={{0,4},{4,0},{8,12},{12,8},{16,20},{20,16},{24,28},{28,24},{1,5},{5... | collective-permute-start | bytes 940040 | tf_op jit(solution)/shard_map/ppermute | solution.py:36
  196.7 66.0 %copy-start.4 = (bf16[2368,128]{1,0:T(8,128)(2,1)S(1)}, bf16[2368,128]{1,0:T(8,128)(2,1)}, u32[]{:S(2)}) copy-start(bf16[2368,128]{1,0:T(8,128)(2,1)} %get-tuple-element.120) | copy-start | bytes 1818628
  196.7 11.2 %collective-permute-start.23 = (f32[32,128]{1,0:T(8,128)S(1)}, f32[32,128]{1,0:T(8,128)S(1)}, u32[]{:S(2)}, u32[]{:S(2)}) collective-permute-start(f32[32,128]{1,0:T(8,128)S(1)} %concatenate.28), channel_id=1, source_target_pairs={{0,4},{4,0},{8,12},{12,8},{16,20},{20,16},{24,28},{28,24},{1,5},{5... | collective-permute-start | bytes 49160 | tf_op jit(solution)/shard_map/ppermute | solution.py:48
  202.8 8.7 %collective-permute-start.22 = (f32[8,256]{1,0:T(8,128)S(1)}, f32[8,256]{1,0:T(8,128)S(1)}, u32[]{:S(2)}, u32[]{:S(2)}) collective-permute-start(f32[8,256]{1,0:T(8,128)S(1)} %slice.156), channel_id=1, source_target_pairs={{4,0},{8,4},{12,8},{16,12},{20,16},{24,20},{28,24},{5,1},{9,5},{13... | collective-permute-start | bytes 24584 | tf_op jit(solution)/shard_map/ppermute | solution.py:23
  207.9 58.9 %collective-permute-start.28 = (bf16[128,1152]{1,0:T(8,128)(2,1)}, bf16[128,1152]{1,0:T(8,128)(2,1)}, u32[]{:S(2)}, u32[]{:S(2)}) collective-permute-start(bf16[128,1152]{1,0:T(8,128)(2,1)} %get-tuple-element.117), channel_id=1, source_target_pairs={{0,8},{4,12},{8,16},{12,20},{16,24},{20,28},{24,0},{28,4},{1,9},{5... | collective-permute-start | bytes 884744 | tf_op jit(solution)/shard_map/ppermute | solution.py:58
  211.5 27.8 %collective-permute-start.24 = (f32[32,128]{1,0:T(8,128)S(1)}, f32[32,128]{1,0:T(8,128)S(1)}, u32[]{:S(2)}, u32[]{:S(2)}) collective-permute-start(f32[32,128]{1,0:T(8,128)S(1)} %add.145), channel_id=1, source_target_pairs={{0,8},{4,12},{8,0},{12,4},{16,24},{20,28},{24,16},{28,20},{1,9},{5... | collective-permute-start | bytes 49160 | tf_op jit(solution)/shard_map/ppermute | solution.py:48
  239.3 17.8 %collective-permute-start.25 = (f32[32,128]{1,0:T(8,128)S(1)}, f32[32,128]{1,0:T(8,128)S(1)}, u32[]{:S(2)}, u32[]{:S(2)}) collective-permute-start(f32[32,128]{1,0:T(8,128)S(1)} %add.146), channel_id=1, source_target_pairs={{0,16},{4,20},{8,24},{12,28},{16,0},{20,4},{24,8},{28,12},{1,17},{... | collective-permute-start | bytes 49160 | tf_op jit(solution)/shard_map/ppermute | solution.py:48
  257.1 14.2 %collective-permute-start.29 = (bf16[128,1152]{1,0:T(8,128)(2,1)}, bf16[128,1152]{1,0:T(8,128)(2,1)}, u32[]{:S(2)}, u32[]{:S(2)}) collective-permute-start(bf16[128,1152]{1,0:T(8,128)(2,1)} %get-tuple-element.118), channel_id=1, source_target_pairs={{0,16},{4,20},{8,24},{12,28},{16,0},{20,4},{24,8},{28,12},{1,17},{... | collective-permute-start | bytes 884744 | tf_op jit(solution)/shard_map/ppermute | solution.py:58
  262.7 12.6 %collective-permute-start.30 = (bf16[128,1152]{1,0:T(8,128)(2,1)}, bf16[128,1152]{1,0:T(8,128)(2,1)S(1)}, u32[]{:S(2)}, u32[]{:S(2)}) collective-permute-start(bf16[128,1152]{1,0:T(8,128)(2,1)} %get-tuple-element.119), channel_id=1, source_target_pairs={{0,24},{4,28},{8,0},{12,4},{16,8},{20,12},{24,16},{28,20},{1,25},{... | collective-permute-start | bytes 884744 | tf_op jit(solution)/shard_map/ppermute | solution.py:58
  264.4 10.8 %copy-start.6 = (bf16[128,1152]{1,0:T(8,128)(2,1)S(1)}, bf16[128,1152]{1,0:T(8,128)(2,1)}, u32[]{:S(2)}) copy-start(bf16[128,1152]{1,0:T(8,128)(2,1)} %get-tuple-element.116) | copy-start | bytes 884740
  (18 other events, 40.9 us)

commit v2 on v1

--- a/solution.py
+++ b/solution.py
@@ -41,21 +41,36 @@
     return [value] + [turned(value, "seq", i, inner) for i in range(1, inner)]
 
 
-def summed_over(value, axis):
-    count = lax.axis_size(axis)
+def shared_sum(value, ranks):
+    outer, inner = plane(ranks)
     step = 1
-    while step < count:
-        value = value + lax.ppermute(value, axis, [(i, i ^ step) for i in range(count)])
+    while step < inner:
+        other = lax.ppermute(value, "seq", [(i, i ^ step) for i in range(ranks)])
+        value = value + other
         step *= 2
-    return value
-
-
-def outer_sum(blocks, ranks):
-    outer, inner = plane(ranks)
+    return [value] + [outward(value, ranks, steps) for steps in range(1, outer)]
+
+
+def ordered_sum(parts, place):
+    stacked = jnp.stack(parts)
+    count = len(parts)
+    return sum(
+        lax.dynamic_index_in_dim(stacked, (place - i) % count, 0, keepdims=False)
+        for i in range(count)
+    )
+
+
+def outward(value, ranks, steps):
+    _, inner = plane(ranks)
+    pairs = [(r, (r + steps * inner) % ranks) for r in range(ranks)]
+    return lax.ppermute(value, "seq", pairs)
+
+
+def inner_sum(blocks, ranks):
+    _, inner = plane(ranks)
     total = blocks[0].astype(F32)
-    for steps in range(1, outer):
-        pairs = [(r, (r + steps * inner) % ranks) for r in range(ranks)]
-        total = total + lax.ppermute(blocks[steps], "seq", pairs).astype(F32)
+    for steps in range(1, inner):
+        total = total + turned(blocks[steps], "seq", steps, inner).astype(F32)
     return total
 
 
@@ -109,9 +124,18 @@
     return inverse
 
 
+def pack_kernel(edge_ref, input_ref, gains_ref, grad_ref, packed_ref):
+    length, _ = input_ref.shape
+    rows = length + EDGE
+    packed_ref[:EDGE, :] = edge_ref[...]
+    packed_ref[EDGE:rows, :] = input_ref[...]
+    packed_ref[rows : rows + 2 * EDGE, :] = gains_ref[...]
+    packed_ref[rows + 2 * EDGE :, :] = grad_ref[...]
+
+
 def setup_kernel(
     proj_ref, rates_ref, taps_ref, params_ref,
-    pre_ref, q_ref, k_ref, inv_ref, w_ref, vals_ref, score_ref, inner_ref, cols_ref, map_ref,
+    pre_ref, q_ref, k_ref, inv_ref, w_ref, vals_ref, score_ref, inner_ref, cols_ref, map_ref, alone_ref, offset_ref,
     ext_ref,
 ):
     heads, rows, width = proj_ref.shape
@@ -147,8 +171,12 @@
         values = dot(inverse, beta * v)
         kept = remain * k
         identity = jnp.where(row[:dim, :dim] == col[:dim, :dim], jnp.exp(last), 0.0)
-        map_ref[0, h] = identity - dot(weights, kept, TN)
-        map_ref[1, h] = dot(values, kept, TN)
+        alone = identity - dot(weights, kept, TN)
+        offset = dot(values, kept, TN)
+        map_ref[0, h] = alone
+        map_ref[1, h] = offset
+        alone_ref[h] = alone
+        offset_ref[h] = offset
         q_ref[h] = q
         k_ref[h] = k
         inv_ref[h] = inverse
@@ -178,13 +206,68 @@
         out_ref[h] = out
 
 
-def local_back_kernel(
-    grad_ref, out_ref, gate_ref, gain_ref, score_ref, q_ref, w_ref, cols_ref,
-    dout_ref, dupd_ref, dstate_ref, dgate_ref, dgain_ref,
+def feed_kernel(sides, place_ref, whole_ref, gateup_ref, down_ref, *refs):
+    rows_refs, merge_refs = refs[:sides], refs[sides : 2 * sides]
+    resid_ref, right_ref, sent_ref, back_ref, back_half_ref, *feed_refs = refs[2 * sides :]
+    feed_ref = feed_refs.pop()
+    length = resid_ref.shape[0]
+    rows = length + EDGE
+    hidden = down_ref.shape[0]
+    resid = whole_ref[EDGE:rows, :].astype(F32)
+    for row_ref, merge_ref in zip(rows_refs, merge_refs):
+        resid = resid + jnp.dot(row_ref[...], merge_ref[...], preferred_element_type=F32)
+    resid_ref[...] = resid
+    gain = whole_ref[rows + EDGE : rows + EDGE + 1, :].astype(F32)
+    feed_in = (resid * rms_scale(resid) * gain).astype(BF)
+    feed_ref[...] = feed_in
+    for i, pick_ref in enumerate(feed_refs):
+        pick_ref[...] = columns_of(feed_ref, place_ref, i, pick_ref.shape[1])
+    one = functools.partial(lax.dot_general, preferred_element_type=F32)
+    gate = one(gateup_ref[0], feed_in, NT)
+    up = one(gateup_ref[1], feed_in, NT)
+    grad_hidden = one(down_ref[...], whole_ref[rows + 2 * EDGE :, :], NT)
+    sigma = jax.nn.sigmoid(gate)
+    active = (gate * sigma * up).astype(BF)
+    grad_gate = (grad_hidden * up * sigma * (1.0 + gate * (1.0 - sigma))).astype(BF)
+    grad_up = (grad_hidden * gate * sigma).astype(BF)
+    right_ref[:hidden, :] = grad_gate
+    right_ref[hidden : 2 * hidden, :] = grad_up
+    right_ref[2 * hidden :, :] = active
+    back = one(grad_gate, gateup_ref[0], TN) + one(grad_up, gateup_ref[1], TN)
+    back_ref[...] = back
+    back_half_ref[...] = back.astype(BF)
+    out = one(active, down_ref[...], TN).astype(BF)
+    local = out.shape[1] // sides
+    for side in range(sides):
+        sent_ref[side] = out[:, side * local : (side + 1) * local]
+
+
+def resid_back_kernel(
+    others, whole_ref, resid_ref, merge_ref, out_ref, gate_ref, gain_ref, score_ref, q_ref, w_ref,
+    cols_ref, back_ref, *refs,
 ):
-    heads, _, dim = q_ref.shape
+    (
+        grad_ref, half_ref, dfeed_ref, dout_ref, dupd_ref, dstate_ref, dgate_ref, dgain_ref,
+    ) = refs[others:]
+    heads, length, dim = q_ref.shape
+    rows = length + EDGE
+    back = back_ref[...]
+    for other_ref in refs[:others]:
+        back = back + other_ref[...].astype(F32)
+    resid = resid_ref[...]
+    scale = rms_scale(resid)
+    dfeed_ref[...] = jnp.sum(back * resid * scale, axis=0, keepdims=True)
+    weighted = back * whole_ref[rows + EDGE : rows + EDGE + 1, :].astype(F32)
+    grad = whole_ref[rows + 2 * EDGE :, :].astype(F32) + scale * weighted
+    grad = grad - resid * (scale * scale * scale) * jnp.mean(
+        weighted * resid, axis=1, keepdims=True
+    )
+    grad_ref[...] = grad
+    half = grad.astype(BF)
+    half_ref[...] = half
+    grad_mixed = lax.dot_general(half, merge_ref[...], NT, preferred_element_type=F32)
     for h in range(heads):
-        grad = grad_ref[:, h * dim : (h + 1) * dim]
+        grad = grad_mixed[:, h * dim : (h + 1) * dim]
         out = out_ref[h]
         scale = lax.rsqrt(jnp.mean(out * out, axis=1, keepdims=True) + EPSILON)
         normed = out * scale
@@ -326,19 +409,20 @@
     return left_ref[:, pl.ds(pl.multiple_of(place_ref[z] * share, share), share)]
 
 
-def feature_minor_kernel(parts, lefts, which, place_ref, *refs):
+def blocks_kernel(parts, lefts, which, dims, place_ref, *refs):
     outer = place_ref.shape[0]
     rights = (len(refs) - outer) // parts - lefts
     for z in range(outer):
         out_ref = refs[len(refs) - outer + z]
         share = out_ref.shape[1]
         at = 0
-        for a, b, i in which:
+        for a, b in which:
             total = None
             for p in range(parts):
                 left = columns_of(refs[p * (lefts + rights) + a], place_ref, z, share)
-                right = refs[p * (lefts + rights) + lefts + b][i]
-                one = lax.dot_general(right, left, TN, preferred_element_type=F32)
+                right_ref = refs[p * (lefts + rights) + lefts + b[0]]
+                right = right_ref[b[1] : b[2], :] if len(b) > 1 else right_ref[...]
+                one = lax.dot_general(right, left, dims, preferred_element_type=F32)
                 total = one if total is None else total + one
             out_ref[at : at + total.shape[0], :] = total.astype(BF)
             at += total.shape[0]
@@ -369,16 +453,20 @@
         sent_ref[side, :, local:] = stats.astype(BF)
 
 
-def compose_kernel(early_ref, late_ref, both_ref):
+def compose_kernel(early_ref, late_ref, both_ref, alone_ref, offset_ref):
     for h in range(early_ref.shape[1]):
         later = late_ref[0, h]
-        both_ref[0, h] = dot(early_ref[0, h], later)
-        both_ref[1, h] = dot(early_ref[1, h], later) + late_ref[1, h]
-
-
-def carry_kernel(first_ref, map_ref, second_ref, sum_ref):
+        alone = dot(early_ref[0, h], later)
+        offset = dot(early_ref[1, h], later) + late_ref[1, h]
+        both_ref[0, h] = alone
+        both_ref[1, h] = offset
+        alone_ref[h] = alone
+        offset_ref[h] = offset
+
+
+def carry_kernel(first_ref, pair_ref, sum_ref):
     for h in range(first_ref.shape[0]):
-        sum_ref[h] = dot(first_ref[h], map_ref[h]) + second_ref[h]
+        sum_ref[h] = dot(first_ref[h], pair_ref[0, h]) + pair_ref[1, h]
 
 
 def carry_back_kernel(first_ref, map_ref, second_ref, sum_ref):
@@ -403,15 +491,15 @@
     )(*args)
 
 
-def scan_states(pair, ranks, extras):
+def scan_states(pair, alone, offset, ranks, extras):
     heads = pair.shape[1]
-    shape = pair.shape[1:]
+    shape = (pair.shape[1:], F32)
     maps = []
     done = []
     span = 1
     while 2 * span < ranks:
         early = shifted(pair, "seq", span)
-        joined = shifted(pair[0], "seq", 1 - span) if span > 1 else pair[0]
+        joined = shifted(alone, "seq", 1 - span) if span > 1 else alone
         if extras:
             early, joined, ready = lax.optimization_barrier((early, joined, extras[0]))
             extras = extras[1:]
@@ -419,26 +507,25 @@
         else:
             early, joined = lax.optimization_barrier((early, joined))
         maps.append(joined)
-        (pair,) = kernel_call(compose_kernel, [(pair.shape, F32)], (early, pair), 4 * heads)
+        pair, alone, offset = kernel_call(
+            compose_kernel, [(pair.shape, F32), shape, shape], (early, pair), 4 * heads
+        )
         span *= 2
     near = shifted(pair, "seq", 1)
     if span + 1 >= ranks:
-        return near[1], maps + [pair[0]], done + list(extras)
-    far = shifted(pair[1], "seq", span + 1)
-    joined = shifted(pair[0], "seq", -span)
-    near, far, joined = lax.optimization_barrier((near, far, joined))
-    (incoming,) = kernel_call(carry_kernel, [(shape, F32)], (far, near[0], near[1]), 2 * heads)
+        return near[1], maps + [alone], done + list(extras)
+    far = shifted(offset, "seq", span + 1)
+    joined = shifted(alone, "seq", -span)
+    (incoming,) = kernel_call(carry_kernel, [shape], (far, near), 2 * heads)
     return incoming, maps + [joined], done + list(extras)
 
 
-def scan_back(local, maps, ranks, extra):
+def scan_back(local, maps, ranks):
     heads = local.shape[0]
     total = local
     span = 1
     for level in range(len(maps) - 1):
         later = shifted(total, "seq", -span)
-        if level == len(maps) - 2:
-            later, extra = lax.optimization_barrier((later, extra))
         (total,) = kernel_call(
             carry_back_kernel, [(local.shape, F32)], (later, maps[level], total), 2 * heads
         )
@@ -449,7 +536,7 @@
         (near,) = kernel_call(
             carry_back_kernel, [(local.shape, F32)], (far, maps[-1], near), 2 * heads
         )
-    return near, extra
+    return near
 
 
 def layer(
@@ -481,17 +568,19 @@
 
     edge = shifted(block_input[length - EDGE :], "seq", 1)
     gains = [jnp.broadcast_to(gain[None], (EDGE, local_width)) for gain in (mixer_gain, feed_gain)]
-    packed = jnp.concatenate([edge, block_input, *gains, output_grad], axis=0)
+    (packed,) = kernel_call(
+        pack_kernel,
+        [((rows + 2 * EDGE + length, local_width), BF)],
+        (edge, block_input, jnp.concatenate(gains, axis=0), output_grad),
+        1,
+    )
     whole = lax.all_gather(packed, "head", axis=1, tiled=True)
-    whole, merge_sent = lax.optimization_barrier((whole, merge_weight))
+    whole, merge_sent, proj_late = lax.optimization_barrier((whole, merge_weight, proj_weight))
     inputs_ext = whole[:rows].astype(F32)
-    inputs = inputs_ext[EDGE:]
     gain_one = whole[rows].astype(F32)
-    gain_two = whole[rows + EDGE].astype(F32)
     grads_full = whole[rows + 2 * EDGE :]
-    all_weight = jnp.concatenate(
-        [merge_weight] + [turned(merge_sent, "head", i, sides) for i in range(1, sides)], axis=0
-    )
+    merge_parts = [merge_weight]
+    merge_parts += [turned(merge_sent, "head", i, sides) for i in range(1, sides)]
 
     scale_ext = rms_scale(inputs_ext)
     normed_ext = (inputs_ext * scale_ext * gain_one).astype(BF)
@@ -503,12 +592,12 @@
 
     cube = (heads, length, dim)
     square = (heads, length, length)
-    pre, q, k, inverse, weights, values, scores, inner, cols, pair = kernel_call(
+    pre, q, k, inverse, weights, values, scores, inner, cols, pair, alone, offset = kernel_call(
         setup_kernel,
         [
             ((heads, length, 3 * dim), F32), (cube, F32), (cube, F32), (square, F32), (cube, F32),
             (cube, F32), (square, F32), (square, F32), ((heads, length, 8), F32),
-            ((2, heads, dim, dim), F32),
+            ((2, heads, dim, dim), F32), ((heads, dim, dim), F32), ((heads, dim, dim), F32),
         ],
         (projected, rates, conv_weight, params),
         18 * heads,
@@ -517,73 +606,75 @@
     rate_columns = jnp.moveaxis(rate_weight, 0, 2).reshape(2 * heads, model_width).T
     wide_weight = jnp.concatenate(
         [
-            proj_weight.reshape(model_width, heads * width),
+            proj_late.reshape(model_width, heads * width),
             jnp.pad(rate_columns, ((0, 0), (0, 128 - 2 * heads))),
         ],
         axis=1,
     )
-    incoming, maps, (wide_weight, all_weight) = scan_states(pair, ranks, [wide_weight, all_weight])
+    share = model_width // ranks
+    outer, group = plane(ranks)
+    places = (rank // group + jnp.arange(outer)) % outer * group + rank % group
+    around = (rank // group + jnp.arange(outer)) % outer
+    normed_parts = in_group(normed_ext, ranks)
+    grad_parts = []
+    for steps in range(outer):
+        piece = lax.dynamic_slice_in_dim(
+            grads_full, around[steps] * (group * share), group * share, 1
+        )
+        grad_parts.append(outward(piece, ranks, steps) if steps else piece)
+    incoming, maps, extras = scan_states(
+        pair, alone, offset, ranks,
+        [(wide_weight, normed_parts, grad_parts), merge_parts],
+    )
+    (wide_weight, normed_parts, grad_parts), merge_parts = extras
     mixed_rows, updates, outs = kernel_call(
         outputs_kernel,
         [((length, heads * dim), BF), (cube, F32), (cube, F32)],
         (q, weights, values, scores, cols, incoming, projected, output_gain),
         3 * heads,
     )
-    all_rows = jnp.concatenate(
-        [mixed_rows] + [turned(mixed_rows, "head", i, sides) for i in range(1, sides)], axis=1
-    )
-    mixer_out = jnp.dot(all_rows, all_weight, preferred_element_type=F32)
-    resid = inputs + mixer_out
-    scale_two = rms_scale(resid)
-    feed_in = (resid * scale_two * gain_two).astype(BF)
-    gateup = jnp.einsum("td,dcf->tcf", feed_in, gateup_weight, preferred_element_type=F32)
-    gate_part = gateup[:, 0]
-    up_part = gateup[:, 1]
-    sigma = jax.nn.sigmoid(gate_part)
-    hidden = (gate_part * sigma * up_part).astype(BF)
-    feed_part = jnp.dot(hidden, down_weight, preferred_element_type=F32)
-    grad_hidden = jnp.einsum("td,fd->tf", grads_full, down_weight, preferred_element_type=F32)
-    grad_gate = grad_hidden * up_part * sigma * (1.0 + gate_part * (1.0 - sigma))
-    grad_up = grad_hidden * gate_part * sigma
-    grad_gateup_rows = jnp.stack([grad_gate, grad_up], axis=0).astype(BF)
-    grad_feed_part = jnp.einsum(
-        "ctf,dcf->td", grad_gateup_rows, gateup_weight, preferred_element_type=F32
-    )
-
-    def by_side(value):
-        return jnp.moveaxis(value.reshape(value.shape[0], sides, local_width), 1, 0)
-
-    def by_part(values):
-        return list(zip(*[in_group(value, ranks) for value in values]))
-
-    feed_parts = by_part(
-        [feed_in, grads_full, jnp.concatenate([grad_gateup_rows, hidden[None]], axis=0)]
-    )
-    got = lax.all_to_all(by_side(grad_feed_part.astype(BF)), "head", 0, 0, tiled=True)
-    mine_feed_grad = jnp.sum(got.astype(F32), axis=0)
-    got = lax.all_to_all(by_side(feed_part.astype(BF)), "head", 0, 0, tiled=True)
-    feed_out = jnp.sum(got.astype(F32), axis=0)
+    rows_parts = [mixed_rows] + [turned(mixed_rows, "head", i, sides) for i in range(1, sides)]
+    full = (length, model_width)
+    resid, feed_right, feed_sent, back, back_half, *feed_picks = kernel_call(
+        functools.partial(feed_kernel, sides),
+        [
+            (full, F32), ((3 * hidden_width, length), BF),
+            ((sides, length, local_width), BF), (full, F32), (full, BF),
+        ]
+        + [((length, group * share), BF)] * outer,
+        [around, whole, jnp.moveaxis(gateup_weight, 0, 2), down_weight] + rows_parts + merge_parts,
+        512,
+        [pltpu.VMEM(full, BF)],
+        scalars=1,
+    )
+    others = [turned(back_half, "head", i, sides) for i in range(1, sides)]
+    feed_parts = {0: (feed_right, feed_picks[0])}
+    for steps in range(1, outer):
+        feed_parts[steps] = (
+            outward(feed_right, ranks, steps), outward(feed_picks[steps], ranks, steps)
+        )
+    cube32 = (cube, F32)
+    (
+        grad_resid, grad_resid_half, grad_gain_two, douts, dupdates, dstate, dgate,
+        grad_output_gain,
+    ) = kernel_call(
+        functools.partial(resid_back_kernel, len(others)),
+        [
+            (full, F32), (full, BF), ((1, model_width), F32), cube32, cube32,
+            ((heads, dim, dim), F32), cube32, ((heads, dim), F32),
+        ],
+        [
+            whole, resid, merge_weight, outs, projected, output_gain, scores, q, weights, cols,
+            back, *others,
+        ],
+        100,
+    )
+    feed_out = lax.all_to_all(feed_sent, "head", 0, 0, tiled=True)
     mine_resid = lax.dynamic_slice_in_dim(resid, part * local_width, local_width, 1)
-    block_output = mine_resid + feed_out
-    grad_feed_in = lax.all_gather(mine_feed_grad.astype(BF), "head", axis=1, tiled=True)
-    grad_feed_in, feed_parts = lax.optimization_barrier((grad_feed_in, feed_parts))
-    grad_feed_in = grad_feed_in.astype(F32)
-    grad_gain_two = jnp.sum(mine_feed_grad * mine_resid * scale_two, axis=0)
-    weighted = grad_feed_in * gain_two
-    grad_resid = (
-        grads_full.astype(F32)
-        + scale_two * weighted
-        - resid * scale_two**3 * jnp.mean(weighted * resid, axis=-1, keepdims=True)
-    )
-    grad_resid_half = grad_resid.astype(BF)
-    grad_mixed = jnp.einsum("td,kd->tk", grad_resid_half, merge_weight, preferred_element_type=F32)
-
-    douts, dupdates, dstate, dgate, grad_output_gain = kernel_call(
-        local_back_kernel,
-        [(cube, F32), (cube, F32), ((heads, dim, dim), F32), (cube, F32), ((heads, dim), F32)],
-        (grad_mixed, outs, projected, output_gain, scores, q, weights, cols),
-        3 * heads,
-    )
+    block_output = mine_resid + jnp.sum(feed_out.astype(F32), axis=0)
+    grad_gain_two = lax.dynamic_slice_in_dim(grad_gain_two, part * local_width, local_width, 1)
+    half_parts = in_group(grad_resid_half, ranks)
+    mixed_parts = in_group(mixed_rows, ranks)
     dq, dk, dcum = kernel_call(
         score_back_kernel,
         [(cube, F32), (cube, F32), ((heads, length, 8), F32)],
@@ -591,34 +682,35 @@
         4 * heads,
     )
 
-    share = model_width // ranks
-    outer, group = plane(ranks)
-    places = (rank // group + jnp.arange(outer)) % outer * group + rank % group
-
-    merge_parts = by_part([grad_resid_half, mixed_rows[None]])
-    parts = [
-        [picked(left, places, share) for left in (feed[0], feed[1], merge[0])] + [feed[2], merge[1]]
-        for feed, merge in zip(feed_parts, merge_parts)
+    def local_blocks(places, lefts, rights, which, dims, height):
+        parts = [
+            [picked(left[p], places, share) for left in lefts] + [right[p] for right in rights]
+            for p in range(len(lefts[0]))
+        ]
+        return kernel_call(
+            functools.partial(blocks_kernel, len(parts), len(lefts), which, dims),
+            [((height, share), BF)] * places.shape[0],
+            [places] + [ref for part_refs in parts for ref in part_refs],
+            256,
+            scalars=1,
+        )
+
+    feed_rows = 3 * hidden_width
+    halfway = 2 * hidden_width
+    grad_end = scan_back(dstate, maps, ranks)
+    feed_blocks = local_blocks(
+        (rank + jnp.arange(group)) % group,
+        [[feed_parts[i][1] for i in range(outer)], grad_parts],
+        [[feed_parts[i][0] for i in range(outer)]],
+        ((0, (0, 0, halfway)), (1, (0, halfway, feed_rows))),
+        NN,
+        feed_rows,
+    )
+    feed_sum = inner_sum(feed_blocks, ranks)
+    merge_blocks = local_blocks(places, [half_parts], [mixed_parts], ((0, (0,)),), TN, heads * dim)
+    merge_blocks = [merge_blocks[0]] + [
+        outward(merge_blocks[steps], ranks, steps) for steps in range(1, outer)
     ]
-    feed_rows = 3 * hidden_width
-    late_blocks = kernel_call(
-        functools.partial(
-            feature_minor_kernel, len(parts), 3, ((0, 0, 0), (0, 0, 1), (1, 0, 2), (2, 1, 0))
-        ),
-        [((feed_rows + heads * dim, share), BF)] * outer,
-        [places] + [ref for part_refs in parts for ref in part_refs],
-        256,
-        scalars=1,
-    )
-    grad_end, late_blocks = scan_back(dstate, maps, ranks, late_blocks)
-    late_sum = outer_sum(late_blocks, ranks)
-    feed_sum = late_sum[:feed_rows]
-    grad_merge = late_sum[feed_rows:]
-    grad_gateup = jnp.moveaxis(
-        feed_sum[: 2 * hidden_width].reshape(2, hidden_width, share), 2, 0
-    )
-    grad_down = feed_sum[2 * hidden_width :]
-
     span_width = heads * width + 128
     grad_rows, grad_conv, grad_params = kernel_call(
         final_back_kernel,
@@ -631,7 +723,7 @@
         [pltpu.VMEM((rows, 3 * dim), F32), pltpu.VMEM((rows + EDGE, 3 * dim), F32)],
     )
     right_parts = in_group(grad_rows, ranks)
-    left_parts = [picked(left, places, share) for left in in_group(normed_ext, ranks)]
+    left_parts = [picked(left, places, share) for left in normed_parts]
     parts = list(zip(left_parts, right_parts))
     blocks = kernel_call(
         functools.partial(feature_major_kernel, len(parts)),
@@ -640,7 +732,8 @@
         100,
         scalars=1,
     )
-    summed_rows = outer_sum(blocks, ranks)
+    last_blocks = [blocks[0]]
+    last_blocks += [outward(blocks[steps], ranks, steps) for steps in range(1, outer)]
     (sent,) = kernel_call(
         input_back_kernel,
         [((sides, rows, local_width + 128), BF)],
@@ -675,7 +768,13 @@
     ends = [0]
     for piece in small:
         ends.append(ends[-1] + piece.shape[0])
-    total = summed_over(jnp.concatenate(small, axis=0), "seq")
+    small_parts = shared_sum(jnp.concatenate(small, axis=0), ranks)
+    last_blocks, merge_blocks, small_parts, input_grad, block_output, feed_sum = (
+        lax.optimization_barrier(
+            (last_blocks, merge_blocks, small_parts, input_grad, block_output, feed_sum)
+        )
+    )
+    total = ordered_sum(small_parts, rank // group)
     small = [total[start:end] for start, end in zip(ends, ends[1:])]
     conv_split = 3 * dim // ranks
     gain_split = dim // ranks
@@ -688,6 +787,10 @@
     grad_params = small[2]
     grad_gain_two = small[3].reshape(-1)
     grad_gain_one = small[4].reshape(-1)
+    grad_merge = sum(block.astype(F32) for block in merge_blocks)
+    grad_gateup = jnp.moveaxis(feed_sum[:halfway].reshape(2, hidden_width, share), 2, 0)
+    grad_down = feed_sum[halfway:]
+    summed_rows = sum(block.astype(F32) for block in last_blocks)
     grad_proj_mine = summed_rows[:, : heads * width].reshape(share, heads, width)
     grad_rate_mine = summed_rows[:, heads * width : heads * (width + 2)].reshape(share, heads, 2)
     return (

time: 282 us -> 298 us (1.057)
  waiting for transfers between devices: 55.9 us -> 104 us
  other arithmetic: 26.5 us -> 12.2 us
  Pallas kernels: 42.3 us -> 54.5 us
  local copies, waits for them, and re-layouts: 30.3 us -> 18.5 us
  matrix products: 13.7 us -> 2.17 us
  blocking collectives: 13.9 us -> 7.66 us
    ppermute x12, waiting for transfers between devices: 16.2 us -> 50.4 us  [shifted(): return lax.ppermute(value, axis, pairs)]
    ppermute x13 -> x14, waiting for transfers between devices: 9.19 us -> 30.1 us  [turned(): return lax.ppermute(value, axis, pairs)]
    pallas_call x14 -> x17, Pallas kernels: 42.3 us -> 54.5 us  [kernel_call(): pl.pallas_call(body, out_shape=shapes, in_specs=[smem] * scalars + [vmem]...]
    dot_general x6 -> x0, matrix products: 9.82 us -> none  [the longest x1 2.16 us: layer(): mixer_out = jnp.dot(all_rows, all_weight, preferred_element_type=F32)]
    all_gather x1 -> x0, blocking collectives: 6.39 us -> none  [layer(): lax.all_gather(mine_feed_grad.astype(BF), 'head', axis=1, tiled=True)]
    concatenate x3 -> x2, other arithmetic: 8.48 us -> 2.27 us  [the longest x1 1.67 us: layer(): jnp.concatenate([proj_late.reshape(model_width, heads * width), jnp.pad(r...]
    squeeze x4 -> x0, local copies, waits for them, and re-layouts: 4.93 us -> none  [the longest x1 1.68 us: scan_states(): near[1]]
    convert_element_type x3 -> x1, other arithmetic: 4.83 us -> 0.01 us  [layer(): gain_one = whole[rows].astype(F32)]
  transfers between devices with their start and end apart: 37 -> 47, of which waited for: 16 -> 17; matrix products, arithmetic and copies ran while one was open for 20% -> 5% of each run, Pallas kernels for 9% -> 12%
where the time goes in v2:
time: 298 us; the launch traced here: 297 us
  waiting for transfers between devices  104 us (35%)
  starting transfers between devices  93.5 us (31%)
  Pallas kernels  54.5 us (18%)
  local copies, waits for them, and re-layouts  18.5 us (6%)
  other arithmetic  12.2 us (4%)
  blocking collectives  7.66 us (3%)
  between operations  4.01 us (1%)
    pallas_call x17, Pallas kernels, kernel_call(): pl.pallas_call(body, out_shape=shapes, in_specs=[smem] * scalars + [vmem]...  54.5 us
    ppermute x12, waiting for transfers between devices, shifted(): return lax.ppermute(value, axis, pairs)  50.4 us
    ppermute x18, starting transfers between devices, outward(): return lax.ppermute(value, 'seq', pairs)  40.9 us
    ppermute x14, waiting for transfers between devices, turned(): return lax.ppermute(value, axis, pairs)  30.1 us
    ppermute x12, starting transfers between devices, shifted(): return lax.ppermute(value, axis, pairs)  26.8 us
    ppermute x18, waiting for transfers between devices, outward(): return lax.ppermute(value, 'seq', pairs)  21.6 us
    ppermute x14, starting transfers between devices, turned(): return lax.ppermute(value, axis, pairs)  17.5 us
    all_gather x1, blocking collectives, layer(): whole = lax.all_gather(packed, 'head', axis=1, tiled=True)  7.66 us
  transfers between devices with their start and end apart: 47, of which 17 were waited for; matrix products, arithmetic and copies ran while one was open for 5% of the time, Pallas kernels for 12%

profile of v2, /device:TPU:0, one launch (start us, length us, event | category | flops | bytes accessed | tf_op | source)
XLA Modules:
  0.0 297.1 jit_solution(1346556634001381389)
XLA Ops:
  1.5 4.9 %collective-permute-start = (bf16[8,256]{1,0:T(8,128)(2,1)S(1)}, bf16[8,256]{1,0:T(8,128)(2,1)S(1)}, u32[]{:S(2)}, u32[]{:S(2)}) collective-permute-start(bf16[8,256]{1,0:T(8,128)(2,1)S(1)} %slice.89), channel_id=1, source_target_pairs={{0,4},{4,8},{8,12},{12,16},{16,20},{20,24},{24,28},{1,5},{5,9},{9,... | collective-permute-start | bytes 12296 | tf_op jit(solution)/shard_map/ppermute | solution.py:23
  15.9 7.7 %all_gather.3.whole_ref = bf16[280,1024]{1,0:T(8,128)(2,1)S(1)} all-gather(bf16[280,256]{1,0:T(8,128)(2,1)} %shard_map.245), channel_id=1, replica_groups=mesh['seq'=8,'head'=4] {'head'}, dimensions={1}, use_global_device_ids=true | all-gather | bytes 716800 | tf_op jit(solution)/shard_map/all_gather | solution.py:577
  27.5 2.6 collective-permute-start.4
  34.9 7.4 %shard_map.246 = (f32[2,128,384]{2,1,0:T(8,128)}, f32[2,128,128]{2,1,0:T(8,128)}, f32[2,128,128]{2,1,0:T(8,128)}, f32[2,128,128]{2,1,0:T(8,128)}, f32[2,128,128]...) custom-call(f32[2,136,512]{2,1,0:T(8,128)} %fusion.4.proj_ref.gate_r, ...), custom_call_target="tpu_custom_call" | custom-call | flops 452984832 | bytes 571416 | tf_op jit(solution)/shard_map/pallas_call | solution.py:482
  44.7 2.4 collective-permute-start.1
  48.7 3.9 %collective-permute-done.1.early_ref = f32[2,2,128,128]{3,2,1,0:T(8,128)S(1)} collective-permute-done((f32[2,2,128,128]{3,2,1,0:T(8,128)}, f32[2,2,128,128]{3,2,1,0:T(8,128)S(1)}, u32[]{:S(2)}, u32[]{:S(2)}) %collective-permute-start.1) | collective-permute-done | bytes 262176 | tf_op jit(solution)/shard_map/ppermute | solution.py:23
  53.4 2.1 shard_map.247
  55.5 4.0 %collective-permute-start.6 = (f32[2,2,128,128]{3,2,1,0:T(8,128)}, f32[2,2,128,128]{3,2,1,0:T(8,128)S(1)}, u32[]{:S(2)}, u32[]{:S(2)}) collective-permute-start(f32[2,2,128,128]{3,2,1,0:T(8,128)} %get-tuple-element.110.late_ref), channel_id=1, source_target_pairs={{0,8},{4,12},{8,16},{12,20},{16,24},{20,28},{1,9},{5,13},{9,17},{1... | collective-permute-start | bytes 786440 | tf_op jit(solution)/shard_map/ppermute | solution.py:23
  60.8 5.8 %collective-permute-done.7.map_ref = f32[2,128,128]{2,1,0:T(8,128)S(1)} collective-permute-done((f32[2,128,128]{2,1,0:T(8,128)}, f32[2,128,128]{2,1,0:T(8,128)S(1)}, u32[]{:S(2)}, u32[]{:S(2)}) %collective-permute-start.7) | collective-permute-done | bytes 131104 | tf_op jit(solution)/shard_map/ppermute | solution.py:23
  67.3 2.1 shard_map.248
  69.4 3.8 %collective-permute-start.12 = (f32[2,2,128,128]{3,2,1,0:T(8,128)}, f32[2,2,128,128]{3,2,1,0:T(8,128)S(1)}, u32[]{:S(2)}, u32[]{:S(2)}) collective-permute-start(f32[2,2,128,128]{3,2,1,0:T(8,128)} %get-tuple-element.115), channel_id=1, source_target_pairs={{0,4},{4,8},{8,12},{12,16},{16,20},{20,24},{24,28},{1,5},{5,9},{9,... | collective-permute-start | bytes 786440 | tf_op jit(solution)/shard_map/ppermute | solution.py:23
  73.1 2.7 collective-permute-start.11
  75.8 2.8 collective-permute-done.11.first_ref
  80.0 1.9 shard_map.249.state_ref
  81.8 2.7 shard_map.250
  86.4 2.2 collective-permute-done.13.refs_1_
  90.3 7.2 %shard_map.251 = (f32[128,1024]{1,0:T(8,128)}, bf16[2112,128]{1,0:T(8,128)(2,1)}, bf16[4,128,256]{2,1,0:T(8,128)(2,1)}, f32[128,1024]{1,0:T(8,128)}, bf16[128,10...) custom-call(s32[4]{0:T(128)} %copy-done.21, ...), custom_call_target="tpu_custom_call" | custom-call | flops 6442450944 | bytes 7258128 | tf_op jit(solution)/shard_map/pallas_call | solution.py:482
  99.7 5.6 %collective-permute-done.16.refs_0_ = bf16[128,1024]{1,0:T(8,128)(2,1)S(1)} collective-permute-done((bf16[128,1024]{1,0:T(8,128)(2,1)}, bf16[128,1024]{1,0:T(8,128)(2,1)S(1)}, u32[]{:S(2)}, u32[]{:S(2)}) %collective-permute-start.16) | collective-permute-done | bytes 262176 | tf_op jit(solution)/shard_map/ppermute | solution.py:36
  105.2 2.4 collective-permute-done.17.refs_1_
  107.6 2.6 collective-permute-done.18.refs_2_
  110.9 4.3 %shard_map.252 = (f32[128,1024]{1,0:T(8,128)}, bf16[128,1024]{1,0:T(8,128)(2,1)}, f32[1,1024]{1,0:T(1,128)}, f32[2,128,128]{2,1,0:T(8,128)}, f32[2,128,128]{2,1,...) custom-call(bf16[280,1024]{1,0:T(8,128)(2,1)} %copy-done, ...), custom_call_target="tpu_custom_call" | custom-call | flops 1258291200 | bytes 4023296 | tf_op jit(solution)/shard_map/pallas_call | solution.py:482
  117.7 3.4 %all-to-all-start.1 = ((bf16[4,128,256]{2,1,0:T(8,128)(2,1)}), bf16[4,128,256]{2,1,0:T(8,128)(2,1)S(1)}, u32[]{:S(2)}, u32[]{:S(2)}) async-start(bf16[4,128,256]{2,1,0:T(8,128)(2,1)} %get-tuple-element.157), calls=%async_computation.1 | async-start | bytes 524288 | tf_op jit(solution)/shard_map/all_to_all | solution.py:672
  121.1 1.8 collective-permute-done.19.first_ref
  123.6 1.9 shard_map.253.second_ref
  126.8 1.9 slice_convert_fusion.inputs_ref
  130.0 3.7 %collective-permute-done.20.first_ref = f32[2,128,128]{2,1,0:T(8,128)S(1)} collective-permute-done((f32[2,128,128]{2,1,0:T(8,128)}, f32[2,128,128]{2,1,0:T(8,128)S(1)}, u32[]{:S(2)}, u32[]{:S(2)}) %collective-permute-start.20) | collective-permute-done | bytes 131104 | tf_op jit(solution)/shard_map/ppermute | solution.py:23
  134.3 1.9 shard_map.254
  137.6 2.3 collective-permute-start.39
  139.9 5.2 %collective-permute-start.41 = (bf16[2112,128]{1,0:T(8,128)(2,1)S(1)}, bf16[2112,128]{1,0:T(8,128)(2,1)}, u32[]{:S(2)}, u32[]{:S(2)}) collective-permute-start(bf16[2112,128]{1,0:T(8,128)(2,1)S(1)} %copy-done.25), channel_id=1, source_target_pairs={{0,16},{4,20},{8,24},{12,28},{16,0},{20,4},{24,8},{28,12},{1,17},{... | collective-permute-start | bytes 1622024 | tf_op jit(solution)/shard_map/ppermute | solution.py:66
  146.5 26.8 %collective-permute-done.21.first_ref = f32[2,128,128]{2,1,0:T(8,128)S(1)} collective-permute-done((f32[2,128,128]{2,1,0:T(8,128)}, f32[2,128,128]{2,1,0:T(8,128)S(1)}, u32[]{:S(2)}, u32[]{:S(2)}) %collective-permute-start.21) | collective-permute-done | bytes 131104 | tf_op jit(solution)/shard_map/ppermute | solution.py:23
  176.2 4.2 %collective-permute-done.23.second_ref = f32[2,128,128]{2,1,0:T(8,128)S(1)} collective-permute-done((f32[2,128,128]{2,1,0:T(8,128)}, f32[2,128,128]{2,1,0:T(8,128)S(1)}, u32[]{:S(2)}, u32[]{:S(2)}) %collective-permute-start.23) | collective-permute-done | bytes 131104 | tf_op jit(solution)/shard_map/ppermute | solution.py:23
  180.4 6.4 %collective-permute-start.29 = (bf16[128,256]{1,0:T(8,128)(2,1)S(1)}, bf16[128,256]{1,0:T(8,128)(2,1)S(1)}, u32[]{:S(2)}, u32[]{:S(2)}) collective-permute-start(bf16[128,256]{1,0:T(8,128)(2,1)S(1)} %copy-done.36), channel_id=1, source_target_pairs={{0,4},{4,0},{8,12},{12,8},{16,20},{20,16},{24,28},{28,24},{1,5},{5... | collective-permute-start | bytes 196616 | tf_op jit(solution)/shard_map/ppermute | solution.py:36
  187.5 2.7 shard_map.256
  190.2 1.9 shard_map.255.dend_ref
  192.1 4.5 %shard_map.257 = (bf16[136,1152]{1,0:T(8,128)(2,1)}, f32[4,2,384]{2,1,0:T(2,128)}, f32[2,128]{1,0:T(2,128)}) custom-call(f32[2,128,128]{2,1,0:T(8,128)} %shard_map.255.dend_ref, f32[2,128,128]{2,1,0:T(8,128)} %get-tuple-element.129.dupd_ref, f32[2,128,128]{2,1,0:T(8,128)} %shard_map.249.state_ref, f32[2,128,128]{2,1,0:T(8,128)} %get-tuple-element.130.upd_ref, ...), custom_call_target="tpu_custom_call" | custom-call | flops 176160768 | bytes 2420760 | tf_op jit(solution)/shard_map/pallas_call | solution.py:482
  196.6 12.3 %collective-permute-start.38 = (bf16[128,256]{1,0:T(8,128)(2,1)S(1)}, bf16[128,256]{1,0:T(8,128)(2,1)S(1)}, u32[]{:S(2)}, u32[]{:S(2)}) collective-permute-start(bf16[128,256]{1,0:T(8,128)(2,1)S(1)} %copy-done.39), channel_id=1, source_target_pairs={{0,8},{4,12},{8,16},{12,20},{16,24},{20,28},{24,0},{28,4},{1,9},{5... | collective-permute-start | bytes 196616 | tf_op jit(solution)/shard_map/ppermute | solution.py:66
  208.9 3.6 %shard_map.260 = bf16[4,136,384]{2,1,0:T(8,128)(2,1)} custom-call(bf16[136,1152]{1,0:T(8,128)(2,1)} %get-tuple-element.140.refs_1_.rows_ref, bf16[1024,1152]{1,0:T(8,128)(2,1)} %fusion.1.weight_ref, f32[136,1024]{1,0:T(8,128)} %slice_convert_fusion.inputs_ref, f32[1,1024]{1,0:T(1,128)} %copy-done.18), custom_call_target="tpu_custom_call" | custom-call | flops 805306368 | bytes 3233792 | tf_op jit(solution)/shard_map/pallas_call | solution.py:482
  212.6 3.5 %all-to-all-start = ((bf16[4,136,384]{2,1,0:T(8,128)(2,1)}), bf16[4,136,384]{2,1,0:T(8,128)(2,1)S(1)}, u32[]{:S(2)}, u32[]{:S(2)}) async-start(bf16[4,136,384]{2,1,0:T(8,128)(2,1)} %shard_map.260), calls=%async_computation | async-start | bytes 835584 | tf_op jit(solution)/shard_map/all_to_all | solution.py:743
  216.2 2.4 collective-permute-start.42
  218.6 2.1 shard_map.259
  223.4 3.3 %collective-permute-start.32 = (bf16[256,128]{1,0:T(8,128)(2,1)}, bf16[256,128]{1,0:T(8,128)(2,1)S(1)}, u32[]{:S(2)}, u32[]{:S(2)}) collective-permute-start(bf16[256,128]{1,0:T(8,128)(2,1)} %get-tuple-element.150), channel_id=1, source_target_pairs={{0,24},{4,28},{8,0},{12,4},{16,8},{20,12},{24,16},{28,20},{1,25},{... | collective-permute-start | bytes 196616 | tf_op jit(solution)/shard_map/ppermute | solution.py:66
  226.8 3.9 %shard_map.261 = (bf16[2112,128]{1,0:T(8,128)(2,1)}, bf16[2112,128]{1,0:T(8,128)(2,1)}) custom-call(s32[2]{0:T(128)} %and_select_fusion.place_ref, bf16[128,256]{1,0:T(8,128)(2,1)} %get-tuple-element.158.refs_0_, bf16[128,256]{1,0:T(8,128)(2,1)} %get-tuple-element.159.refs_1_, bf16[2112,128]{1,0:T(8,128)(2,1)} %get-tuple-element.160.refs_2_, ...), custom_call_target="tpu_custom_call" | custom-call | flops 3221225472 | bytes 2686984 | tf_op jit(solution)/shard_map/pallas_call | solution.py:482
  230.8 1.8 collective-permute-start.24
  235.0 16.3 %collective-permute-done.24.refs_3_ = bf16[136,1152]{1,0:T(8,128)(2,1)S(1)} collective-permute-done((bf16[136,1152]{1,0:T(8,128)(2,1)S(1)}, bf16[136,1152]{1,0:T(8,128)(2,1)S(1)}, u32[]{:S(2)}, u32[]{:S(2)}) %collective-permute-start.24) | collective-permute-done | bytes 313376 | tf_op jit(solution)/shard_map/ppermute | solution.py:36
  252.5 2.8 shard_map.258
  258.2 2.3 collective-permute-done.33
  263.1 2.5 collective-permute-start.26
  270.1 19.8 %collective-permute-done.35 = f32[32,128]{1,0:T(8,128)S(1)} collective-permute-done((f32[32,128]{1,0:T(8,128)S(1)}, f32[32,128]{1,0:T(8,128)S(1)}, u32[]{:S(2)}, u32[]{:S(2)}) %collective-permute-start.35) | collective-permute-done | bytes 16416 | tf_op jit(solution)/shard_map/ppermute | solution.py:66
  (213 shorter events, 66.9 us)
Async XLA Ops:
  1.5 12.2 %collective-permute-start = (bf16[8,256]{1,0:T(8,128)(2,1)S(1)}, bf16[8,256]{1,0:T(8,128)(2,1)S(1)}, u32[]{:S(2)}, u32[]{:S(2)}) collective-permute-start(bf16[8,256]{1,0:T(8,128)(2,1)S(1)} %slice.89), channel_id=1, source_target_pairs={{0,4},{4,8},{8,12},{12,16},{16,20},{20,24},{24,28},{1,5},{5,9},{9,... | collective-permute-start | bytes 12296 | tf_op jit(solution)/shard_map/ppermute | solution.py:23
  23.6 114.0 %copy-start.18 = (f32[1,1024]{1,0:T(1,128)}, f32[1,1024]{1,0:T(1,128)S(1)}, u32[]{:S(2)}) copy-start(f32[1,1024]{1,0:T(1,128)S(1)} %slice_convert_fusion.1.gain_ref) | copy-start | bytes 12292
  25.9 16.4 %collective-permute-start.3 = (bf16[128,256]{1,0:T(8,128)(2,1)S(1)}, bf16[128,256]{1,0:T(8,128)(2,1)S(1)}, u32[]{:S(2)}, u32[]{:S(2)}) collective-permute-start(bf16[128,256]{1,0:T(8,128)(2,1)S(1)} %get-tuple-element.205), channel_id=1, source_target_pairs={{0,8},{4,12},{8,16},{12,20},{16,24},{20,28},{24,0},{28,4},{1,9},{5... | collective-permute-start | bytes 196616 | tf_op jit(solution)/shard_map/ppermute | solution.py:66
  27.5 15.7 %collective-permute-start.4 = (bf16[128,256]{1,0:T(8,128)(2,1)S(1)}, bf16[128,256]{1,0:T(8,128)(2,1)}, u32[]{:S(2)}, u32[]{:S(2)}) collective-permute-start(bf16[128,256]{1,0:T(8,128)(2,1)S(1)} %get-tuple-element.204), channel_id=1, source_target_pairs={{0,16},{4,20},{8,24},{12,28},{16,0},{20,4},{24,8},{28,12},{1,17},{... | collective-permute-start | bytes 196616 | tf_op jit(solution)/shard_map/ppermute | solution.py:66
  30.1 14.6 %collective-permute-start.5 = (bf16[128,256]{1,0:T(8,128)(2,1)S(1)}, bf16[128,256]{1,0:T(8,128)(2,1)}, u32[]{:S(2)}, u32[]{:S(2)}) collective-permute-start(bf16[128,256]{1,0:T(8,128)(2,1)S(1)} %get-tuple-element.203), channel_id=1, source_target_pairs={{0,24},{4,28},{8,0},{12,4},{16,8},{20,12},{24,16},{28,20},{1,25},{... | collective-permute-start | bytes 196616 | tf_op jit(solution)/shard_map/ppermute | solution.py:66
  32.3 20.4 %collective-permute-start.2 = (bf16[136,1024]{1,0:T(8,128)(2,1)S(1)}, bf16[136,1024]{1,0:T(8,128)(2,1)}, u32[]{:S(2)}, u32[]{:S(2)}) collective-permute-start(bf16[136,1024]{1,0:T(8,128)(2,1)S(1)} %multiply_convert_fusion.refs_0_), channel_id=1, source_target_pairs={{0,4},{4,0},{8,12},{12,8},{16,20},{20,16},{24,28},{28,24},{1,5},{5... | collective-permute-start | bytes 835592 | tf_op jit(solution)/shard_map/ppermute | solution.py:36
  34.9 31.6 %collective-permute-start.8 = (bf16[256,1024]{1,0:T(8,128)(2,1)S(1)}, bf16[256,1024]{1,0:T(8,128)(2,1)}, u32[]{:S(2)}, u32[]{:S(2)}) collective-permute-start(bf16[256,1024]{1,0:T(8,128)(2,1)S(1)} %copy-done.27), channel_id=1, source_target_pairs={{0,1},{1,2},{2,3},{3,0},{4,5},{5,6},{6,7},{7,4},{8,9},{9,10},{10,1... | collective-permute-start | bytes 1572872 | tf_op jit(solution)/shard_map/ppermute | solution.py:36
  42.3 24.2 %collective-permute-start.9 = (bf16[256,1024]{1,0:T(8,128)(2,1)S(1)}, bf16[256,1024]{1,0:T(8,128)(2,1)}, u32[]{:S(2)}, u32[]{:S(2)}) collective-permute-start(bf16[256,1024]{1,0:T(8,128)(2,1)S(1)} %copy-done.27), channel_id=1, source_target_pairs={{0,2},{1,3},{2,0},{3,1},{4,6},{5,7},{6,4},{7,5},{8,10},{9,11},{10,... | collective-permute-start | bytes 1572872 | tf_op jit(solution)/shard_map/ppermute | solution.py:36
  43.2 23.4 %collective-permute-start.10 = (bf16[256,1024]{1,0:T(8,128)(2,1)S(1)}, bf16[256,1024]{1,0:T(8,128)(2,1)}, u32[]{:S(2)}, u32[]{:S(2)}) collective-permute-start(bf16[256,1024]{1,0:T(8,128)(2,1)S(1)} %copy-done.27), channel_id=1, source_target_pairs={{0,3},{1,0},{2,1},{3,2},{4,7},{5,4},{6,5},{7,6},{8,11},{9,8},{10,9... | collective-permute-start | bytes 1572872 | tf_op jit(solution)/shard_map/ppermute | solution.py:36
  44.7 8.0 %collective-permute-start.1 = (f32[2,2,128,128]{3,2,1,0:T(8,128)}, f32[2,2,128,128]{3,2,1,0:T(8,128)S(1)}, u32[]{:S(2)}, u32[]{:S(2)}) collective-permute-start(f32[2,2,128,128]{3,2,1,0:T(8,128)} %get-tuple-element.100.late_ref), channel_id=1, source_target_pairs={{0,4},{4,8},{8,12},{12,16},{16,20},{20,24},{24,28},{1,5},{5,9},{9,... | collective-permute-start | bytes 786440 | tf_op jit(solution)/shard_map/ppermute | solution.py:23
  55.5 11.1 %collective-permute-start.6 = (f32[2,2,128,128]{3,2,1,0:T(8,128)}, f32[2,2,128,128]{3,2,1,0:T(8,128)S(1)}, u32[]{:S(2)}, u32[]{:S(2)}) collective-permute-start(f32[2,2,128,128]{3,2,1,0:T(8,128)} %get-tuple-element.110.late_ref), channel_id=1, source_target_pairs={{0,8},{4,12},{8,16},{12,20},{16,24},{20,28},{1,9},{5,13},{9,17},{1... | collective-permute-start | bytes 786440 | tf_op jit(solution)/shard_map/ppermute | solution.py:23
  59.5 7.1 %collective-permute-start.7 = (f32[2,128,128]{2,1,0:T(8,128)}, f32[2,128,128]{2,1,0:T(8,128)S(1)}, u32[]{:S(2)}, u32[]{:S(2)}) collective-permute-start(f32[2,128,128]{2,1,0:T(8,128)} %get-tuple-element.111), channel_id=1, source_target_pairs={{4,0},{8,4},{12,8},{16,12},{20,16},{24,20},{28,24},{5,1},{9,5},{13... | collective-permute-start | bytes 393224 | tf_op jit(solution)/shard_map/ppermute | solution.py:23
  69.4 9.3 %collective-permute-start.12 = (f32[2,2,128,128]{3,2,1,0:T(8,128)}, f32[2,2,128,128]{3,2,1,0:T(8,128)S(1)}, u32[]{:S(2)}, u32[]{:S(2)}) collective-permute-start(f32[2,2,128,128]{3,2,1,0:T(8,128)} %get-tuple-element.115), channel_id=1, source_target_pairs={{0,4},{4,8},{8,12},{12,16},{16,20},{20,24},{24,28},{1,5},{5,9},{9,... | collective-permute-start | bytes 786440 | tf_op jit(solution)/shard_map/ppermute | solution.py:23
  73.1 5.5 %collective-permute-start.11 = (f32[2,128,128]{2,1,0:T(8,128)}, f32[2,128,128]{2,1,0:T(8,128)S(1)}, u32[]{:S(2)}, u32[]{:S(2)}) collective-permute-start(f32[2,128,128]{2,1,0:T(8,128)} %get-tuple-element.114), channel_id=1, source_target_pairs={{0,20},{4,24},{8,28},{1,21},{5,25},{9,29},{2,22},{6,26},{10,30},{3... | collective-permute-start | bytes 393224 | tf_op jit(solution)/shard_map/ppermute | solution.py:23
  84.5 4.0 %collective-permute-start.13 = (bf16[128,256]{1,0:T(8,128)(2,1)}, bf16[128,256]{1,0:T(8,128)(2,1)S(1)}, u32[]{:S(2)}, u32[]{:S(2)}) collective-permute-start(bf16[128,256]{1,0:T(8,128)(2,1)} %get-tuple-element.116.refs_0_.refs_1_), channel_id=1, source_target_pairs={{0,1},{1,2},{2,3},{3,0},{4,5},{5,6},{6,7},{7,4},{8,9},{9,10},{10,1... | collective-permute-start | bytes 196616 | tf_op jit(solution)/shard_map/ppermute | solution.py:36
  84.5 5.2 %collective-permute-start.14 = (bf16[128,256]{1,0:T(8,128)(2,1)}, bf16[128,256]{1,0:T(8,128)(2,1)S(1)}, u32[]{:S(2)}, u32[]{:S(2)}) collective-permute-start(bf16[128,256]{1,0:T(8,128)(2,1)} %get-tuple-element.116.refs_0_.refs_1_), channel_id=1, source_target_pairs={{0,2},{1,3},{2,0},{3,1},{4,6},{5,7},{6,4},{7,5},{8,10},{9,11},{10,... | collective-permute-start | bytes 196616 | tf_op jit(solution)/shard_map/ppermute | solution.py:36
  84.9 4.8 %collective-permute-start.15 = (bf16[128,256]{1,0:T(8,128)(2,1)}, bf16[128,256]{1,0:T(8,128)(2,1)S(1)}, u32[]{:S(2)}, u32[]{:S(2)}) collective-permute-start(bf16[128,256]{1,0:T(8,128)(2,1)} %get-tuple-element.116.refs_0_.refs_1_), channel_id=1, source_target_pairs={{0,3},{1,0},{2,1},{3,2},{4,7},{5,4},{6,5},{7,6},{8,11},{9,8},{10,9... | collective-permute-start | bytes 196616 | tf_op jit(solution)/shard_map/ppermute | solution.py:36
  97.6 7.7 %collective-permute-start.16 = (bf16[128,1024]{1,0:T(8,128)(2,1)}, bf16[128,1024]{1,0:T(8,128)(2,1)S(1)}, u32[]{:S(2)}, u32[]{:S(2)}) collective-permute-start(bf16[128,1024]{1,0:T(8,128)(2,1)} %get-tuple-element.124), channel_id=1, source_target_pairs={{0,1},{1,2},{2,3},{3,0},{4,5},{5,6},{6,7},{7,4},{8,9},{9,10},{10,1... | collective-permute-start | bytes 786440 | tf_op jit(solution)/shard_map/ppermute | solution.py:36
  98.2 9.4 %collective-permute-start.17 = (bf16[128,1024]{1,0:T(8,128)(2,1)}, bf16[128,1024]{1,0:T(8,128)(2,1)S(1)}, u32[]{:S(2)}, u32[]{:S(2)}) collective-permute-start(bf16[128,1024]{1,0:T(8,128)(2,1)} %get-tuple-element.124), channel_id=1, source_target_pairs={{0,2},{1,3},{2,0},{3,1},{4,6},{5,7},{6,4},{7,5},{8,10},{9,11},{10,... | collective-permute-start | bytes 786440 | tf_op jit(solution)/shard_map/ppermute | solution.py:36
  98.6 11.6 %collective-permute-start.18 = (bf16[128,1024]{1,0:T(8,128)(2,1)}, bf16[128,1024]{1,0:T(8,128)(2,1)S(1)}, u32[]{:S(2)}, u32[]{:S(2)}) collective-permute-start(bf16[128,1024]{1,0:T(8,128)(2,1)} %get-tuple-element.124), channel_id=1, source_target_pairs={{0,3},{1,0},{2,1},{3,2},{4,7},{5,4},{6,5},{7,6},{8,11},{9,8},{10,9... | collective-permute-start | bytes 786440 | tf_op jit(solution)/shard_map/ppermute | solution.py:36
  115.2 7.7 %collective-permute-start.19 = (f32[2,128,128]{2,1,0:T(8,128)}, f32[2,128,128]{2,1,0:T(8,128)S(1)}, u32[]{:S(2)}, u32[]{:S(2)}) collective-permute-start(f32[2,128,128]{2,1,0:T(8,128)} %get-tuple-element.125.second_ref), channel_id=1, source_target_pairs={{4,0},{8,4},{12,8},{16,12},{20,16},{24,20},{28,24},{5,1},{9,5},{13... | collective-permute-start | bytes 393224 | tf_op jit(solution)/shard_map/ppermute | solution.py:23
  117.7 27.5 %all-to-all-start.1 = ((bf16[4,128,256]{2,1,0:T(8,128)(2,1)}), bf16[4,128,256]{2,1,0:T(8,128)(2,1)S(1)}, u32[]{:S(2)}, u32[]{:S(2)}) async-start(bf16[4,128,256]{2,1,0:T(8,128)(2,1)} %get-tuple-element.157), calls=%async_computation.1 | async-start | bytes 524288 | tf_op jit(solution)/shard_map/all_to_all | solution.py:672
  125.5 8.1 %collective-permute-start.20 = (f32[2,128,128]{2,1,0:T(8,128)}, f32[2,128,128]{2,1,0:T(8,128)S(1)}, u32[]{:S(2)}, u32[]{:S(2)}) collective-permute-start(f32[2,128,128]{2,1,0:T(8,128)} %shard_map.253.second_ref), channel_id=1, source_target_pairs={{8,0},{12,4},{16,8},{20,12},{24,16},{28,20},{9,1},{13,5},{17,9},{2... | collective-permute-start | bytes 393224 | tf_op jit(solution)/shard_map/ppermute | solution.py:23
  128.7 16.5 %collective-permute-start.22 = (f32[2,128,128]{2,1,0:T(8,128)S(1)}, f32[2,128,128]{2,1,0:T(8,128)S(1)}, u32[]{:S(2)}, u32[]{:S(2)}) collective-permute-start(f32[2,128,128]{2,1,0:T(8,128)S(1)} %copy-done.34), channel_id=1, source_target_pairs={{16,0},{20,4},{24,8},{28,12},{17,1},{21,5},{25,9},{29,13},{18,2},{... | collective-permute-start | bytes 393224 | tf_op jit(solution)/shard_map/ppermute | solution.py:23
  136.3 37.1 %collective-permute-start.21 = (f32[2,128,128]{2,1,0:T(8,128)}, f32[2,128,128]{2,1,0:T(8,128)S(1)}, u32[]{:S(2)}, u32[]{:S(2)}) collective-permute-start(f32[2,128,128]{2,1,0:T(8,128)} %shard_map.254), channel_id=1, source_target_pairs={{20,0},{24,4},{28,8},{21,1},{25,5},{29,9},{22,2},{26,6},{30,10},{2... | collective-permute-start | bytes 393224 | tf_op jit(solution)/shard_map/ppermute | solution.py:23
  137.6 85.8 %collective-permute-start.39 = (bf16[2112,128]{1,0:T(8,128)(2,1)S(1)}, bf16[2112,128]{1,0:T(8,128)(2,1)S(1)}, u32[]{:S(2)}, u32[]{:S(2)}) collective-permute-start(bf16[2112,128]{1,0:T(8,128)(2,1)S(1)} %copy-done.25), channel_id=1, source_target_pairs={{0,8},{4,12},{8,16},{12,20},{16,24},{20,28},{24,0},{28,4},{1,9},{5... | collective-permute-start | bytes 1622024 | tf_op jit(solution)/shard_map/ppermute | solution.py:66
  139.9 86.8 %collective-permute-start.41 = (bf16[2112,128]{1,0:T(8,128)(2,1)S(1)}, bf16[2112,128]{1,0:T(8,128)(2,1)}, u32[]{:S(2)}, u32[]{:S(2)}) collective-permute-start(bf16[2112,128]{1,0:T(8,128)(2,1)S(1)} %copy-done.25), channel_id=1, source_target_pairs={{0,16},{4,20},{8,24},{12,28},{16,0},{20,4},{24,8},{28,12},{1,17},{... | collective-permute-start | bytes 1622024 | tf_op jit(solution)/shard_map/ppermute | solution.py:66
  145.2 81.5 %collective-permute-start.43 = (bf16[2112,128]{1,0:T(8,128)(2,1)S(1)}, bf16[2112,128]{1,0:T(8,128)(2,1)}, u32[]{:S(2)}, u32[]{:S(2)}) collective-permute-start(bf16[2112,128]{1,0:T(8,128)(2,1)S(1)} %copy-done.25), channel_id=1, source_target_pairs={{0,24},{4,28},{8,0},{12,4},{16,8},{20,12},{24,16},{28,20},{1,25},{... | collective-permute-start | bytes 1622024 | tf_op jit(solution)/shard_map/ppermute | solution.py:66
  145.3 70.9 %collective-permute-start.28 = (bf16[128,1024]{1,0:T(8,128)(2,1)S(1)}, bf16[128,1024]{1,0:T(8,128)(2,1)S(1)}, u32[]{:S(2)}, u32[]{:S(2)}) collective-permute-start(bf16[128,1024]{1,0:T(8,128)(2,1)S(1)} %copy-done.29), channel_id=1, source_target_pairs={{0,4},{4,0},{8,12},{12,8},{16,20},{20,16},{24,28},{28,24},{1,5},{5... | collective-permute-start | bytes 786440 | tf_op jit(solution)/shard_map/ppermute | solution.py:36
  173.4 7.1 %collective-permute-start.23 = (f32[2,128,128]{2,1,0:T(8,128)}, f32[2,128,128]{2,1,0:T(8,128)S(1)}, u32[]{:S(2)}, u32[]{:S(2)}) collective-permute-start(f32[2,128,128]{2,1,0:T(8,128)} %shard_map.254), channel_id=1, source_target_pairs={{4,0},{8,4},{12,8},{16,12},{20,16},{24,20},{28,24},{5,1},{9,5},{13... | collective-permute-start | bytes 393224 | tf_op jit(solution)/shard_map/ppermute | solution.py:23
  180.4 16.2 %collective-permute-start.29 = (bf16[128,256]{1,0:T(8,128)(2,1)S(1)}, bf16[128,256]{1,0:T(8,128)(2,1)S(1)}, u32[]{:S(2)}, u32[]{:S(2)}) collective-permute-start(bf16[128,256]{1,0:T(8,128)(2,1)S(1)} %copy-done.36), channel_id=1, source_target_pairs={{0,4},{4,0},{8,12},{12,8},{16,20},{20,16},{24,28},{28,24},{1,5},{5... | collective-permute-start | bytes 196616 | tf_op jit(solution)/shard_map/ppermute | solution.py:36
  196.6 19.4 %collective-permute-start.38 = (bf16[128,256]{1,0:T(8,128)(2,1)S(1)}, bf16[128,256]{1,0:T(8,128)(2,1)S(1)}, u32[]{:S(2)}, u32[]{:S(2)}) collective-permute-start(bf16[128,256]{1,0:T(8,128)(2,1)S(1)} %copy-done.39), channel_id=1, source_target_pairs={{0,8},{4,12},{8,16},{12,20},{16,24},{20,28},{24,0},{28,4},{1,9},{5... | collective-permute-start | bytes 196616 | tf_op jit(solution)/shard_map/ppermute | solution.py:66
  212.6 20.1 %all-to-all-start = ((bf16[4,136,384]{2,1,0:T(8,128)(2,1)}), bf16[4,136,384]{2,1,0:T(8,128)(2,1)S(1)}, u32[]{:S(2)}, u32[]{:S(2)}) async-start(bf16[4,136,384]{2,1,0:T(8,128)(2,1)} %shard_map.260), calls=%async_computation | async-start | bytes 835584 | tf_op jit(solution)/shard_map/all_to_all | solution.py:743
  216.1 6.3 %collective-permute-start.40 = (bf16[128,256]{1,0:T(8,128)(2,1)S(1)}, bf16[128,256]{1,0:T(8,128)(2,1)S(1)}, u32[]{:S(2)}, u32[]{:S(2)}) collective-permute-start(bf16[128,256]{1,0:T(8,128)(2,1)S(1)} %copy-done.38), channel_id=1, source_target_pairs={{0,16},{4,20},{8,24},{12,28},{16,0},{20,4},{24,8},{28,12},{1,17},{... | collective-permute-start | bytes 196616 | tf_op jit(solution)/shard_map/ppermute | solution.py:66
  216.2 6.2 %collective-permute-start.42 = (bf16[128,256]{1,0:T(8,128)(2,1)S(1)}, bf16[128,256]{1,0:T(8,128)(2,1)S(1)}, u32[]{:S(2)}, u32[]{:S(2)}) collective-permute-start(bf16[128,256]{1,0:T(8,128)(2,1)S(1)} %copy-done.37), channel_id=1, source_target_pairs={{0,24},{4,28},{8,0},{12,4},{16,8},{20,12},{24,16},{28,20},{1,25},{... | collective-permute-start | bytes 196616 | tf_op jit(solution)/shard_map/ppermute | solution.py:66
  222.4 39.9 %collective-permute-start.30 = (bf16[256,128]{1,0:T(8,128)(2,1)}, bf16[256,128]{1,0:T(8,128)(2,1)S(1)}, u32[]{:S(2)}, u32[]{:S(2)}) collective-permute-start(bf16[256,128]{1,0:T(8,128)(2,1)} %get-tuple-element.148), channel_id=1, source_target_pairs={{0,8},{4,12},{8,16},{12,20},{16,24},{20,28},{24,0},{28,4},{1,9},{5... | collective-permute-start | bytes 196616 | tf_op jit(solution)/shard_map/ppermute | solution.py:66
  222.4 40.7 %collective-permute-start.31 = (bf16[256,128]{1,0:T(8,128)(2,1)}, bf16[256,128]{1,0:T(8,128)(2,1)S(1)}, u32[]{:S(2)}, u32[]{:S(2)}) collective-permute-start(bf16[256,128]{1,0:T(8,128)(2,1)} %get-tuple-element.149), channel_id=1, source_target_pairs={{0,16},{4,20},{8,24},{12,28},{16,0},{20,4},{24,8},{28,12},{1,17},{... | collective-permute-start | bytes 196616 | tf_op jit(solution)/shard_map/ppermute | solution.py:66
  223.4 42.2 %collective-permute-start.32 = (bf16[256,128]{1,0:T(8,128)(2,1)}, bf16[256,128]{1,0:T(8,128)(2,1)S(1)}, u32[]{:S(2)}, u32[]{:S(2)}) collective-permute-start(bf16[256,128]{1,0:T(8,128)(2,1)} %get-tuple-element.150), channel_id=1, source_target_pairs={{0,24},{4,28},{8,0},{12,4},{16,8},{20,12},{24,16},{28,20},{1,25},{... | collective-permute-start | bytes 196616 | tf_op jit(solution)/shard_map/ppermute | solution.py:66
  230.6 37.5 %collective-permute-start.44 = (bf16[2112,128]{1,0:T(8,128)(2,1)}, bf16[2112,128]{1,0:T(8,128)(2,1)S(1)}, u32[]{:S(2)}, u32[]{:S(2)}) collective-permute-start(bf16[2112,128]{1,0:T(8,128)(2,1)} %get-tuple-element.168), channel_id=1, source_target_pairs={{0,4},{4,0},{8,12},{12,8},{16,20},{20,16},{24,28},{28,24},{1,5},{5... | collective-permute-start | bytes 1622024 | tf_op jit(solution)/shard_map/ppermute | solution.py:36
  230.8 20.4 %collective-permute-start.24 = (bf16[136,1152]{1,0:T(8,128)(2,1)S(1)}, bf16[136,1152]{1,0:T(8,128)(2,1)S(1)}, u32[]{:S(2)}, u32[]{:S(2)}) collective-permute-start(bf16[136,1152]{1,0:T(8,128)(2,1)S(1)} %copy-done.4), channel_id=1, source_target_pairs={{0,4},{4,0},{8,12},{12,8},{16,20},{20,16},{24,28},{28,24},{1,5},{5... | collective-permute-start | bytes 940040 | tf_op jit(solution)/shard_map/ppermute | solution.py:36
  251.2 5.5 %collective-permute-start.37 = (f32[8,256]{1,0:T(8,128)S(1)}, f32[8,256]{1,0:T(8,128)S(1)}, u32[]{:S(2)}, u32[]{:S(2)}) collective-permute-start(f32[8,256]{1,0:T(8,128)S(1)} %slice.123), channel_id=1, source_target_pairs={{4,0},{8,4},{12,8},{16,12},{20,16},{24,20},{28,24},{5,1},{9,5},{13... | collective-permute-start | bytes 24584 | tf_op jit(solution)/shard_map/ppermute | solution.py:23
  256.8 3.7 %collective-permute-start.33 = (f32[32,128]{1,0:T(8,128)S(1)}, f32[32,128]{1,0:T(8,128)S(1)}, u32[]{:S(2)}, u32[]{:S(2)}) collective-permute-start(f32[32,128]{1,0:T(8,128)S(1)} %concatenate.14), channel_id=1, source_target_pairs={{0,4},{4,0},{8,12},{12,8},{16,20},{20,16},{24,28},{28,24},{1,5},{5... | collective-permute-start | bytes 49160 | tf_op jit(solution)/shard_map/ppermute | solution.py:48
  260.5 6.0 %collective-permute-start.34 = (f32[32,128]{1,0:T(8,128)S(1)}, f32[32,128]{1,0:T(8,128)S(1)}, u32[]{:S(2)}, u32[]{:S(2)}) collective-permute-start(f32[32,128]{1,0:T(8,128)S(1)} %add.171), channel_id=1, source_target_pairs={{0,8},{4,12},{8,16},{12,20},{16,24},{20,28},{24,0},{28,4},{1,9},{5... | collective-permute-start | bytes 49160 | tf_op jit(solution)/shard_map/ppermute | solution.py:66
  262.3 27.6 %collective-permute-start.25 = (bf16[128,1152]{1,0:T(8,128)(2,1)}, bf16[128,1152]{1,0:T(8,128)(2,1)S(1)}, u32[]{:S(2)}, u32[]{:S(2)}) collective-permute-start(bf16[128,1152]{1,0:T(8,128)(2,1)} %get-tuple-element.143), channel_id=1, source_target_pairs={{0,8},{4,12},{8,16},{12,20},{16,24},{20,28},{24,0},{28,4},{1,9},{5... | collective-permute-start | bytes 884744 | tf_op jit(solution)/shard_map/ppermute | solution.py:66
  263.1 26.8 %collective-permute-start.26 = (bf16[128,1152]{1,0:T(8,128)(2,1)}, bf16[128,1152]{1,0:T(8,128)(2,1)S(1)}, u32[]{:S(2)}, u32[]{:S(2)}) collective-permute-start(bf16[128,1152]{1,0:T(8,128)(2,1)} %get-tuple-element.144), channel_id=1, source_target_pairs={{0,16},{4,20},{8,24},{12,28},{16,0},{20,4},{24,8},{28,12},{1,17},{... | collective-permute-start | bytes 884744 | tf_op jit(solution)/shard_map/ppermute | solution.py:66
  265.6 24.3 %collective-permute-start.27 = (bf16[128,1152]{1,0:T(8,128)(2,1)}, bf16[128,1152]{1,0:T(8,128)(2,1)S(1)}, u32[]{:S(2)}, u32[]{:S(2)}) collective-permute-start(bf16[128,1152]{1,0:T(8,128)(2,1)} %get-tuple-element.145), channel_id=1, source_target_pairs={{0,24},{4,28},{8,0},{12,4},{16,8},{20,12},{24,16},{28,20},{1,25},{... | collective-permute-start | bytes 884744 | tf_op jit(solution)/shard_map/ppermute | solution.py:66
  266.5 23.4 %collective-permute-start.35 = (f32[32,128]{1,0:T(8,128)S(1)}, f32[32,128]{1,0:T(8,128)S(1)}, u32[]{:S(2)}, u32[]{:S(2)}) collective-permute-start(f32[32,128]{1,0:T(8,128)S(1)} %add.171), channel_id=1, source_target_pairs={{0,16},{4,20},{8,24},{12,28},{16,0},{20,4},{24,8},{28,12},{1,17},{... | collective-permute-start | bytes 49160 | tf_op jit(solution)/shard_map/ppermute | solution.py:66
  268.2 21.7 %collective-permute-start.36 = (f32[32,128]{1,0:T(8,128)S(1)}, f32[32,128]{1,0:T(8,128)S(1)}, u32[]{:S(2)}, u32[]{:S(2)}) collective-permute-start(f32[32,128]{1,0:T(8,128)S(1)} %add.171), channel_id=1, source_target_pairs={{0,24},{4,28},{8,0},{12,4},{16,8},{20,12},{24,16},{28,20},{1,25},{... | collective-permute-start | bytes 49160 | tf_op jit(solution)/shard_map/ppermute | solution.py:66
  (46 other events, 536.4 us)

commit v3 on v2

--- a/solution.py
+++ b/solution.py
@@ -175,7 +175,7 @@
         offset = dot(values, kept, TN)
         map_ref[0, h] = alone
         map_ref[1, h] = offset
-        alone_ref[h] = alone
+        alone_ref[h] = alone.astype(BF)
         offset_ref[h] = offset
         q_ref[h] = q
         k_ref[h] = k
@@ -221,7 +221,10 @@
     feed_in = (resid * rms_scale(resid) * gain).astype(BF)
     feed_ref[...] = feed_in
     for i, pick_ref in enumerate(feed_refs):
-        pick_ref[...] = columns_of(feed_ref, place_ref, i, pick_ref.shape[1])
+        size = pick_ref.shape[1] // 2
+        pick_ref[:, :size] = columns_of(feed_ref, place_ref, i, size)
+        columns = pl.ds(pl.multiple_of(place_ref[i] * size, size), size)
+        pick_ref[:, size:] = whole_ref[rows + 2 * EDGE :, columns]
     one = functools.partial(lax.dot_general, preferred_element_type=F32)
     gate = one(gateup_ref[0], feed_in, NT)
     up = one(gateup_ref[1], feed_in, NT)
@@ -247,7 +250,7 @@
     cols_ref, back_ref, *refs,
 ):
     (
-        grad_ref, half_ref, dfeed_ref, dout_ref, dupd_ref, dstate_ref, dgate_ref, dgain_ref,
+        grad_ref, half_ref, dfeed_ref, dout_ref, dupd_ref, dstate_ref, dgate_ref, dgain_ref, sent_ref,
     ) = refs[others:]
     heads, length, dim = q_ref.shape
     rows = length + EDGE
@@ -281,7 +284,9 @@
         dout = scale * (inside - normed * jnp.mean(inside * normed, axis=1, keepdims=True))
         dupd = dot(score_ref[h], dout, TN)
         grown = jnp.exp(cols_ref[h, :, 0:1]) * dout
-        dstate_ref[h] = dot(grown, q_ref[h], TN) - dot(dupd, w_ref[h], TN)
+        dstate = dot(grown, q_ref[h], TN) - dot(dupd, w_ref[h], TN)
+        dstate_ref[h] = dstate
+        sent_ref[h] = dstate.astype(BF)
         dout_ref[h] = dout
         dupd_ref[h] = dupd
 
@@ -396,21 +401,22 @@
         rows_ref[EDGE:, h * width + 3 * dim : (h + 1) * width] = dgate_ref[h].astype(BF)
 
 
-def picked(left, places, share):
+def picked(left, places, share, base=0):
     if share % 128 == 0:
         return left
-    starts = [places[z] * share for z in range(places.shape[0])]
+    starts = [base + places[z] * share for z in range(places.shape[0])]
     return jnp.stack([lax.dynamic_slice_in_dim(left, start, share, 1) for start in starts])
 
 
-def columns_of(left_ref, place_ref, z, share):
+def columns_of(left_ref, place_ref, z, share, base=0):
     if len(left_ref.shape) == 3:
         return left_ref[z]
-    return left_ref[:, pl.ds(pl.multiple_of(place_ref[z] * share, share), share)]
-
-
-def blocks_kernel(parts, lefts, which, dims, place_ref, *refs):
+    return left_ref[:, pl.ds(pl.multiple_of(base + place_ref[z] * share, share), share)]
+
+
+def blocks_kernel(parts, bases, which, dims, place_ref, *refs):
     outer = place_ref.shape[0]
+    lefts = len(bases)
     rights = (len(refs) - outer) // parts - lefts
     for z in range(outer):
         out_ref = refs[len(refs) - outer + z]
@@ -419,7 +425,9 @@
         for a, b in which:
             total = None
             for p in range(parts):
-                left = columns_of(refs[p * (lefts + rights) + a], place_ref, z, share)
+                left = columns_of(
+                    refs[p * (lefts + rights) + a], place_ref, z, share, bases[a]
+                )
                 right_ref = refs[p * (lefts + rights) + lefts + b[0]]
                 right = right_ref[b[1] : b[2], :] if len(b) > 1 else right_ref[...]
                 one = lax.dot_general(right, left, dims, preferred_element_type=F32)
@@ -460,7 +468,7 @@
         offset = dot(early_ref[1, h], later) + late_ref[1, h]
         both_ref[0, h] = alone
         both_ref[1, h] = offset
-        alone_ref[h] = alone
+        alone_ref[h] = alone.astype(BF)
         offset_ref[h] = offset
 
 
@@ -469,9 +477,12 @@
         sum_ref[h] = dot(first_ref[h], pair_ref[0, h]) + pair_ref[1, h]
 
 
-def carry_back_kernel(first_ref, map_ref, second_ref, sum_ref):
+def carry_back_kernel(first_ref, map_ref, second_ref, sum_ref, sent_ref):
     for h in range(first_ref.shape[0]):
-        sum_ref[h] = dot(first_ref[h], map_ref[h], NT) + second_ref[h]
+        one = lax.dot_general(first_ref[h], map_ref[h], NT, preferred_element_type=F32)
+        total = one + second_ref[h].astype(F32)
+        sum_ref[h] = total
+        sent_ref[h] = total.astype(BF)
 
 
 def kernel_call(body, outs, args, dots, scratch=(), scalars=0):
@@ -494,6 +505,7 @@
 def scan_states(pair, alone, offset, ranks, extras):
     heads = pair.shape[1]
     shape = (pair.shape[1:], F32)
+    half = (pair.shape[1:], BF)
     maps = []
     done = []
     span = 1
@@ -501,14 +513,12 @@
         early = shifted(pair, "seq", span)
         joined = shifted(alone, "seq", 1 - span) if span > 1 else alone
         if extras:
-            early, joined, ready = lax.optimization_barrier((early, joined, extras[0]))
+            early, ready = lax.optimization_barrier((early, extras[0]))
             extras = extras[1:]
             done.append(ready)
-        else:
-            early, joined = lax.optimization_barrier((early, joined))
         maps.append(joined)
         pair, alone, offset = kernel_call(
-            compose_kernel, [(pair.shape, F32), shape, shape], (early, pair), 4 * heads
+            compose_kernel, [(pair.shape, F32), half, shape], (early, pair), 4 * heads
         )
         span *= 2
     near = shifted(pair, "seq", 1)
@@ -520,23 +530,21 @@
     return incoming, maps + [joined], done + list(extras)
 
 
-def scan_back(local, maps, ranks):
-    heads = local.shape[0]
-    total = local
+def scan_back(total, sent, maps, ranks):
+    heads = total.shape[0]
+    kinds = [(total.shape, F32), (total.shape, BF)]
     span = 1
     for level in range(len(maps) - 1):
-        later = shifted(total, "seq", -span)
-        (total,) = kernel_call(
-            carry_back_kernel, [(local.shape, F32)], (later, maps[level], total), 2 * heads
+        later = shifted(sent, "seq", -span)
+        total, sent = kernel_call(
+            carry_back_kernel, kinds, (later, maps[level], total), 2 * heads
         )
         span *= 2
-    near = shifted(total, "seq", -1)
+    near = shifted(sent, "seq", -1)
     if span + 1 < ranks:
-        far = shifted(total, "seq", -(span + 1))
-        (near,) = kernel_call(
-            carry_back_kernel, [(local.shape, F32)], (far, maps[-1], near), 2 * heads
-        )
-    return near
+        far = shifted(sent, "seq", -(span + 1))
+        near, _ = kernel_call(carry_back_kernel, kinds, (far, maps[-1], near), 2 * heads)
+    return near.astype(F32)
 
 
 def layer(
@@ -578,7 +586,6 @@
     whole, merge_sent, proj_late = lax.optimization_barrier((whole, merge_weight, proj_weight))
     inputs_ext = whole[:rows].astype(F32)
     gain_one = whole[rows].astype(F32)
-    grads_full = whole[rows + 2 * EDGE :]
     merge_parts = [merge_weight]
     merge_parts += [turned(merge_sent, "head", i, sides) for i in range(1, sides)]
 
@@ -597,7 +604,7 @@
         [
             ((heads, length, 3 * dim), F32), (cube, F32), (cube, F32), (square, F32), (cube, F32),
             (cube, F32), (square, F32), (square, F32), ((heads, length, 8), F32),
-            ((2, heads, dim, dim), F32), ((heads, dim, dim), F32), ((heads, dim, dim), F32),
+            ((2, heads, dim, dim), F32), ((heads, dim, dim), BF), ((heads, dim, dim), F32),
         ],
         (projected, rates, conv_weight, params),
         18 * heads,
@@ -616,17 +623,9 @@
     places = (rank // group + jnp.arange(outer)) % outer * group + rank % group
     around = (rank // group + jnp.arange(outer)) % outer
     normed_parts = in_group(normed_ext, ranks)
-    grad_parts = []
-    for steps in range(outer):
-        piece = lax.dynamic_slice_in_dim(
-            grads_full, around[steps] * (group * share), group * share, 1
-        )
-        grad_parts.append(outward(piece, ranks, steps) if steps else piece)
-    incoming, maps, extras = scan_states(
-        pair, alone, offset, ranks,
-        [(wide_weight, normed_parts, grad_parts), merge_parts],
-    )
-    (wide_weight, normed_parts, grad_parts), merge_parts = extras
+    incoming, maps, (wide_weight, merge_parts) = scan_states(
+        pair, alone, offset, ranks, [wide_weight, merge_parts]
+    )
     mixed_rows, updates, outs = kernel_call(
         outputs_kernel,
         [((length, heads * dim), BF), (cube, F32), (cube, F32)],
@@ -641,27 +640,26 @@
             (full, F32), ((3 * hidden_width, length), BF),
             ((sides, length, local_width), BF), (full, F32), (full, BF),
         ]
-        + [((length, group * share), BF)] * outer,
+        + [((length, 2 * group * share), BF)] * outer,
         [around, whole, jnp.moveaxis(gateup_weight, 0, 2), down_weight] + rows_parts + merge_parts,
         512,
         [pltpu.VMEM(full, BF)],
         scalars=1,
     )
     others = [turned(back_half, "head", i, sides) for i in range(1, sides)]
-    feed_parts = {0: (feed_right, feed_picks[0])}
-    for steps in range(1, outer):
-        feed_parts[steps] = (
-            outward(feed_right, ranks, steps), outward(feed_picks[steps], ranks, steps)
-        )
+    right_parts, left_parts = [feed_right], [feed_picks[0]]
+    for i in range(1, outer):
+        right_parts.append(outward(feed_right, ranks, i))
+        left_parts.append(outward(feed_picks[i], ranks, i))
     cube32 = (cube, F32)
     (
         grad_resid, grad_resid_half, grad_gain_two, douts, dupdates, dstate, dgate,
-        grad_output_gain,
+        grad_output_gain, dstate_sent,
     ) = kernel_call(
         functools.partial(resid_back_kernel, len(others)),
         [
             (full, F32), (full, BF), ((1, model_width), F32), cube32, cube32,
-            ((heads, dim, dim), F32), cube32, ((heads, dim), F32),
+            ((heads, dim, dim), F32), cube32, ((heads, dim), F32), ((heads, dim, dim), BF),
         ],
         [
             whole, resid, merge_weight, outs, projected, output_gain, scores, q, weights, cols,
@@ -682,13 +680,14 @@
         4 * heads,
     )
 
-    def local_blocks(places, lefts, rights, which, dims, height):
+    def local_blocks(places, lefts, bases, rights, which, dims, height):
         parts = [
-            [picked(left[p], places, share) for left in lefts] + [right[p] for right in rights]
+            [picked(left[p], places, share, base) for left, base in zip(lefts, bases)]
+            + [right[p] for right in rights]
             for p in range(len(lefts[0]))
         ]
         return kernel_call(
-            functools.partial(blocks_kernel, len(parts), len(lefts), which, dims),
+            functools.partial(blocks_kernel, len(parts), bases, which, dims),
             [((height, share), BF)] * places.shape[0],
             [places] + [ref for part_refs in parts for ref in part_refs],
             256,
@@ -697,17 +696,20 @@
 
     feed_rows = 3 * hidden_width
     halfway = 2 * hidden_width
-    grad_end = scan_back(dstate, maps, ranks)
+    grad_end = scan_back(dstate, dstate_sent, maps, ranks)
     feed_blocks = local_blocks(
         (rank + jnp.arange(group)) % group,
-        [[feed_parts[i][1] for i in range(outer)], grad_parts],
-        [[feed_parts[i][0] for i in range(outer)]],
+        [left_parts, left_parts],
+        (0, group * share),
+        [right_parts],
         ((0, (0, 0, halfway)), (1, (0, halfway, feed_rows))),
         NN,
         feed_rows,
     )
     feed_sum = inner_sum(feed_blocks, ranks)
-    merge_blocks = local_blocks(places, [half_parts], [mixed_parts], ((0, (0,)),), TN, heads * dim)
+    merge_blocks = local_blocks(
+        places, [half_parts], (0,), [mixed_parts], ((0, (0,)),), TN, heads * dim
+    )
     merge_blocks = [merge_blocks[0]] + [
         outward(merge_blocks[steps], ranks, steps) for steps in range(1, outer)
     ]
@@ -722,9 +724,8 @@
         7 * heads,
         [pltpu.VMEM((rows, 3 * dim), F32), pltpu.VMEM((rows + EDGE, 3 * dim), F32)],
     )
-    right_parts = in_group(grad_rows, ranks)
-    left_parts = [picked(left, places, share) for left in normed_parts]
-    parts = list(zip(left_parts, right_parts))
+    row_parts = in_group(grad_rows, ranks)
+    parts = list(zip([picked(left, places, share) for left in normed_parts], row_parts))
     blocks = kernel_call(
         functools.partial(feature_major_kernel, len(parts)),
         [((share, span_width), BF)] * outer,

time: 298 us -> 277 us (0.930)
  starting transfers between devices: 93.5 us -> 84.7 us
  waiting for transfers between devices: 104 us -> 95.4 us
    ppermute x14, waiting for transfers between devices: 30.1 us -> 11.8 us  [turned(): return lax.ppermute(value, axis, pairs)]
    ppermute x18 -> x15, starting transfers between devices: 40.9 us -> 29.7 us  [outward(): return lax.ppermute(value, 'seq', pairs)]
    ppermute x12, waiting for transfers between devices: 50.4 us -> 57.4 us  [shifted(): return lax.ppermute(value, axis, pairs)]
    ppermute x12, starting transfers between devices: 26.8 us -> 32.3 us  [shifted(): return lax.ppermute(value, axis, pairs)]
    ppermute x18 -> x15, waiting for transfers between devices: 21.6 us -> 22.4 us  [outward(): return lax.ppermute(value, 'seq', pairs)]
    unnamed x95 -> x87, local copies, waits for them, and re-layouts: 7.2 us -> 6.62 us
  transfers between devices with their start and end apart: 47 -> 44, of which waited for: 17 -> 17; matrix products, arithmetic and copies ran while one was open for 5% -> 6% of each run, Pallas kernels for 12% -> 14%
where the time goes in v3:
time: 277 us; the launch traced here: 276 us
  waiting for transfers between devices  95.4 us (34%)
  starting transfers between devices  84.7 us (31%)
  Pallas kernels  54.4 us (20%)
  local copies, waits for them, and re-layouts  17.4 us (6%)
  other arithmetic  12.6 us (5%)
  blocking collectives  7.66 us (3%)
    ppermute x12, waiting for transfers between devices, shifted(): return lax.ppermute(value, axis, pairs)  57.4 us
    pallas_call x17, Pallas kernels, kernel_call(): pl.pallas_call(body, out_shape=shapes, in_specs=[smem] * scalars + [vmem]...  54.4 us
    ppermute x12, starting transfers between devices, shifted(): return lax.ppermute(value, axis, pairs)  32.3 us
    ppermute x15, starting transfers between devices, outward(): return lax.ppermute(value, 'seq', pairs)  29.7 us
    ppermute x15, waiting for transfers between devices, outward(): return lax.ppermute(value, 'seq', pairs)  22.4 us
    ppermute x14, starting transfers between devices, turned(): return lax.ppermute(value, axis, pairs)  15.8 us
    ppermute x14, waiting for transfers between devices, turned(): return lax.ppermute(value, axis, pairs)  11.8 us
    all_gather x1, blocking collectives, layer(): whole = lax.all_gather(packed, 'head', axis=1, tiled=True)  7.66 us
  transfers between devices with their start and end apart: 44, of which 17 were waited for; matrix products, arithmetic and copies ran while one was open for 6% of the time, Pallas kernels for 14%

profile of v3, /device:TPU:0, one launch (start us, length us, event | category | flops | bytes accessed | tf_op | source)
XLA Modules:
  0.0 275.5 jit_solution(645581469069597804)
XLA Ops:
  1.5 4.9 %collective-permute-start = (bf16[8,256]{1,0:T(8,128)(2,1)S(1)}, bf16[8,256]{1,0:T(8,128)(2,1)S(1)}, u32[]{:S(2)}, u32[]{:S(2)}) collective-permute-start(bf16[8,256]{1,0:T(8,128)(2,1)S(1)} %slice.74), channel_id=1, source_target_pairs={{0,4},{4,8},{8,12},{12,16},{16,20},{20,24},{24,28},{1,5},{5,9},{9,... | collective-permute-start | bytes 12296 | tf_op jit(solution)/shard_map/ppermute | solution.py:23
  12.7 7.7 %all_gather.3.whole_ref = bf16[280,1024]{1,0:T(8,128)(2,1)S(1)} all-gather(bf16[280,256]{1,0:T(8,128)(2,1)} %shard_map.245), channel_id=1, replica_groups=mesh['seq'=8,'head'=4] {'head'}, dimensions={1}, use_global_device_ids=true | all-gather | bytes 716800 | tf_op jit(solution)/shard_map/all_gather | solution.py:585
  25.1 7.4 %shard_map.246 = (f32[2,128,384]{2,1,0:T(8,128)}, f32[2,128,128]{2,1,0:T(8,128)}, f32[2,128,128]{2,1,0:T(8,128)}, f32[2,128,128]{2,1,0:T(8,128)}, f32[2,128,128]...) custom-call(f32[2,136,512]{2,1,0:T(8,128)} %fusion.4.proj_ref.gate_r, ...), custom_call_target="tpu_custom_call" | custom-call | flops 452984832 | bytes 571416 | tf_op jit(solution)/shard_map/pallas_call | solution.py:493
  32.5 3.5 %collective-permute-start.1 = (f32[2,2,128,128]{3,2,1,0:T(8,128)}, f32[2,2,128,128]{3,2,1,0:T(8,128)S(1)}, u32[]{:S(2)}, u32[]{:S(2)}) collective-permute-start(f32[2,2,128,128]{3,2,1,0:T(8,128)} %get-tuple-element.102.late_ref), channel_id=1, source_target_pairs={{0,4},{4,8},{8,12},{12,16},{16,20},{20,24},{24,28},{1,5},{5,9},{9,... | collective-permute-start | bytes 786440 | tf_op jit(solution)/shard_map/ppermute | solution.py:23
  38.1 3.4 %collective-permute-done.1.early_ref = f32[2,2,128,128]{3,2,1,0:T(8,128)S(1)} collective-permute-done((f32[2,2,128,128]{3,2,1,0:T(8,128)}, f32[2,2,128,128]{3,2,1,0:T(8,128)S(1)}, u32[]{:S(2)}, u32[]{:S(2)}) %collective-permute-start.1) | collective-permute-done | bytes 262176 | tf_op jit(solution)/shard_map/ppermute | solution.py:23
  42.3 2.1 shard_map.247
  44.3 5.2 %collective-permute-start.2 = (f32[2,2,128,128]{3,2,1,0:T(8,128)}, f32[2,2,128,128]{3,2,1,0:T(8,128)S(1)}, u32[]{:S(2)}, u32[]{:S(2)}) collective-permute-start(f32[2,2,128,128]{3,2,1,0:T(8,128)} %get-tuple-element.105.late_ref), channel_id=1, source_target_pairs={{0,8},{4,12},{8,16},{12,20},{16,24},{20,28},{1,9},{5,13},{9,17},{1... | collective-permute-start | bytes 786440 | tf_op jit(solution)/shard_map/ppermute | solution.py:23
  49.5 4.7 %collective-permute-done.2.early_ref = f32[2,2,128,128]{3,2,1,0:T(8,128)S(1)} collective-permute-done((f32[2,2,128,128]{3,2,1,0:T(8,128)}, f32[2,2,128,128]{3,2,1,0:T(8,128)S(1)}, u32[]{:S(2)}, u32[]{:S(2)}) %collective-permute-start.2) | collective-permute-done | bytes 262176 | tf_op jit(solution)/shard_map/ppermute | solution.py:23
  55.0 2.1 shard_map.248
  57.0 2.5 collective-permute-start.7
  59.6 7.1 %collective-permute-start.6 = (f32[2,128,128]{2,1,0:T(8,128)}, f32[2,128,128]{2,1,0:T(8,128)S(1)}, u32[]{:S(2)}, u32[]{:S(2)}) collective-permute-start(f32[2,128,128]{2,1,0:T(8,128)} %get-tuple-element.108), channel_id=1, source_target_pairs={{0,20},{4,24},{8,28},{1,21},{5,25},{9,29},{2,22},{6,26},{10,30},{3... | collective-permute-start | bytes 393224 | tf_op jit(solution)/shard_map/ppermute | solution.py:23
  66.7 2.8 %collective-permute-done.6.first_ref = f32[2,128,128]{2,1,0:T(8,128)S(1)} collective-permute-done((f32[2,128,128]{2,1,0:T(8,128)}, f32[2,128,128]{2,1,0:T(8,128)S(1)}, u32[]{:S(2)}, u32[]{:S(2)}) %collective-permute-start.6) | collective-permute-done | bytes 131104 | tf_op jit(solution)/shard_map/ppermute | solution.py:23
  70.9 1.9 shard_map.249.state_ref
  72.8 2.7 shard_map.250
  81.3 7.4 %shard_map.251 = (f32[128,1024]{1,0:T(8,128)}, bf16[2112,128]{1,0:T(8,128)(2,1)}, bf16[4,128,256]{2,1,0:T(8,128)(2,1)}, f32[128,1024]{1,0:T(8,128)}, bf16[128,10...) custom-call(s32[4]{0:T(128)} %and_select_fusion.1.place_ref, ...), custom_call_target="tpu_custom_call" | custom-call | flops 6442450944 | bytes 7258128 | tf_op jit(solution)/shard_map/pallas_call | solution.py:493
  91.9 3.4 %all-to-all-start.1 = ((bf16[4,128,256]{2,1,0:T(8,128)(2,1)}), bf16[4,128,256]{2,1,0:T(8,128)(2,1)S(1)}, u32[]{:S(2)}, u32[]{:S(2)}) async-start(bf16[4,128,256]{2,1,0:T(8,128)(2,1)} %get-tuple-element.155), calls=%async_computation.1 | async-start | bytes 524288 | tf_op jit(solution)/shard_map/all_to_all | solution.py:670
  96.3 2.4 collective-permute-done.12.refs_1_
  98.7 4.0 %collective-permute-done.13.refs_2_ = bf16[128,1024]{1,0:T(8,128)(2,1)S(1)} collective-permute-done((bf16[128,1024]{1,0:T(8,128)(2,1)}, bf16[128,1024]{1,0:T(8,128)(2,1)S(1)}, u32[]{:S(2)}, u32[]{:S(2)}) %collective-permute-start.13) | collective-permute-done | bytes 262176 | tf_op jit(solution)/shard_map/ppermute | solution.py:36
  103.5 4.3 %shard_map.252 = (f32[128,1024]{1,0:T(8,128)}, bf16[128,1024]{1,0:T(8,128)(2,1)}, f32[1,1024]{1,0:T(1,128)}, f32[2,128,128]{2,1,0:T(8,128)}, f32[2,128,128]{2,1,...) custom-call(bf16[280,1024]{1,0:T(8,128)(2,1)} %copy-done, ...), custom_call_target="tpu_custom_call" | custom-call | flops 1258291200 | bytes 4023296 | tf_op jit(solution)/shard_map/pallas_call | solution.py:493
  109.2 1.8 slice_convert_fusion.inputs_ref
  112.3 2.2 collective-permute-done.14.first_ref
  115.2 1.8 shard_map.253
  121.0 2.6 collective-permute-start.36
  123.6 4.3 %collective-permute-start.38 = (bf16[2112,128]{1,0:T(8,128)(2,1)S(1)}, bf16[2112,128]{1,0:T(8,128)(2,1)}, u32[]{:S(2)}, u32[]{:S(2)}) collective-permute-start(bf16[2112,128]{1,0:T(8,128)(2,1)S(1)} %copy-done.22), channel_id=1, source_target_pairs={{0,16},{4,20},{8,24},{12,28},{16,0},{20,4},{24,8},{28,12},{1,17},{... | collective-permute-start | bytes 1622024 | tf_op jit(solution)/shard_map/ppermute | solution.py:66
  128.6 1.8 shard_map.254
  131.7 21.4 %collective-permute-done.18.map_ref = bf16[2,128,128]{2,1,0:T(8,128)(2,1)S(1)} collective-permute-done((bf16[2,128,128]{2,1,0:T(8,128)(2,1)S(1)}, bf16[2,128,128]{2,1,0:T(8,128)(2,1)S(1)}, u32[]{:S(2)}, u32[]{:S(2)}) %collective-permute-start.18) | collective-permute-done | bytes 65568 | tf_op jit(solution)/shard_map/ppermute | solution.py:23
  154.7 12.5 %collective-permute-done.17.first_ref = bf16[2,128,128]{2,1,0:T(8,128)(2,1)S(1)} collective-permute-done((bf16[2,128,128]{2,1,0:T(8,128)(2,1)}, bf16[2,128,128]{2,1,0:T(8,128)(2,1)S(1)}, u32[]{:S(2)}, u32[]{:S(2)}) %collective-permute-start.17) | collective-permute-done | bytes 65568 | tf_op jit(solution)/shard_map/ppermute | solution.py:23
  170.1 3.5 %collective-permute-done.19.second_ref = bf16[2,128,128]{2,1,0:T(8,128)(2,1)S(1)} collective-permute-done((bf16[2,128,128]{2,1,0:T(8,128)(2,1)}, bf16[2,128,128]{2,1,0:T(8,128)(2,1)S(1)}, u32[]{:S(2)}, u32[]{:S(2)}) %collective-permute-start.19) | collective-permute-done | bytes 65568 | tf_op jit(solution)/shard_map/ppermute | solution.py:23
  174.3 2.7 shard_map.256
  178.7 4.5 %shard_map.257 = (bf16[136,1152]{1,0:T(8,128)(2,1)}, f32[4,2,384]{2,1,0:T(2,128)}, f32[2,128]{1,0:T(2,128)}) custom-call(f32[2,128,128]{2,1,0:T(8,128)} %get-tuple-element.127.dend_ref, f32[2,128,128]{2,1,0:T(8,128)} %get-tuple-element.128.dupd_ref, f32[2,128,128]{2,1,0:T(8,128)} %shard_map.249.state_ref, f32[2,128,128]{2,1,0:T(8,128)} %get-tuple-element.129.upd_ref, ...), custom_call_target="tpu_custom_call" | custom-call | flops 176160768 | bytes 2420760 | tf_op jit(solution)/shard_map/pallas_call | solution.py:493
  184.0 3.6 %shard_map.260 = bf16[4,136,384]{2,1,0:T(8,128)(2,1)} custom-call(bf16[136,1152]{1,0:T(8,128)(2,1)} %get-tuple-element.139.refs_1_.rows_ref, bf16[1024,1152]{1,0:T(8,128)(2,1)} %fusion.1.weight_ref, f32[136,1024]{1,0:T(8,128)} %slice_convert_fusion.inputs_ref, f32[1,1024]{1,0:T(1,128)} %copy-done.17), custom_call_target="tpu_custom_call" | custom-call | flops 805306368 | bytes 3233792 | tf_op jit(solution)/shard_map/pallas_call | solution.py:493
  187.6 3.5 %all-to-all-start = ((bf16[4,136,384]{2,1,0:T(8,128)(2,1)}), bf16[4,136,384]{2,1,0:T(8,128)(2,1)S(1)}, u32[]{:S(2)}, u32[]{:S(2)}) async-start(bf16[4,136,384]{2,1,0:T(8,128)(2,1)} %shard_map.260), calls=%async_computation | async-start | bytes 835584 | tf_op jit(solution)/shard_map/all_to_all | solution.py:744
  191.1 6.9 %collective-permute-start.37 = (bf16[128,512]{1,0:T(8,128)(2,1)S(1)}, bf16[128,512]{1,0:T(8,128)(2,1)S(1)}, u32[]{:S(2)}, u32[]{:S(2)}) collective-permute-start(bf16[128,512]{1,0:T(8,128)(2,1)S(1)} %copy-done.30), channel_id=1, source_target_pairs={{0,16},{4,20},{8,24},{12,28},{16,0},{20,4},{24,8},{28,12},{1,17},{... | collective-permute-start | bytes 393224 | tf_op jit(solution)/shard_map/ppermute | solution.py:66
  198.0 2.9 %collective-permute-start.39 = (bf16[128,512]{1,0:T(8,128)(2,1)S(1)}, bf16[128,512]{1,0:T(8,128)(2,1)S(1)}, u32[]{:S(2)}, u32[]{:S(2)}) collective-permute-start(bf16[128,512]{1,0:T(8,128)(2,1)S(1)} %copy-done.29), channel_id=1, source_target_pairs={{0,24},{4,28},{8,0},{12,4},{16,8},{20,12},{24,16},{28,20},{1,25},{... | collective-permute-start | bytes 393224 | tf_op jit(solution)/shard_map/ppermute | solution.py:66
  201.0 2.1 shard_map.259
  203.1 2.0 collective-permute-done.37.refs_6_.refs_7_
  205.0 4.4 %collective-permute-start.20 = (bf16[136,1024]{1,0:T(8,128)(2,1)S(1)}, bf16[136,1024]{1,0:T(8,128)(2,1)}, u32[]{:S(2)}, u32[]{:S(2)}) collective-permute-start(bf16[136,1024]{1,0:T(8,128)(2,1)S(1)} %multiply_convert_fusion.refs_0_), channel_id=1, source_target_pairs={{0,4},{4,0},{8,12},{12,8},{16,20},{20,16},{24,28},{28,24},{1,5},{5... | collective-permute-start | bytes 835592 | tf_op jit(solution)/shard_map/ppermute | solution.py:36
  209.5 3.2 %collective-permute-start.27 = (bf16[256,128]{1,0:T(8,128)(2,1)}, bf16[256,128]{1,0:T(8,128)(2,1)S(1)}, u32[]{:S(2)}, u32[]{:S(2)}) collective-permute-start(bf16[256,128]{1,0:T(8,128)(2,1)} %get-tuple-element.146), channel_id=1, source_target_pairs={{0,8},{4,12},{8,16},{12,20},{16,24},{20,28},{24,0},{28,4},{1,9},{5... | collective-permute-start | bytes 196616 | tf_op jit(solution)/shard_map/ppermute | solution.py:66
  213.3 4.0 %shard_map.261 = (bf16[2112,128]{1,0:T(8,128)(2,1)}, bf16[2112,128]{1,0:T(8,128)(2,1)}) custom-call(s32[2]{0:T(128)} %and_select_fusion.place_ref, bf16[128,512]{1,0:T(8,128)(2,1)} %get-tuple-element.156.refs_0_.refs_1_, bf16[128,512]{1,0:T(8,128)(2,1)} %get-tuple-element.156.refs_0_.refs_1_, bf16[2112,128]{1,0:T(8,128)(2,1)} %get-tuple-element.157.refs_2_, ...), custom_call_target="tpu_custom_call" | custom-call | flops 3221225472 | bytes 3211272 | tf_op jit(solution)/shard_map/pallas_call | solution.py:493
  217.4 1.8 collective-permute-start.41
  221.8 2.0 collective-permute-done.21.refs_3_
  225.0 2.8 %shard_map.258 = (bf16[128,1152]{1,0:T(8,128)(2,1)}, bf16[128,1152]{1,0:T(8,128)(2,1)}, bf16[128,1152]{1,0:T(8,128)(2,1)}, bf16[128,1152]{1,0:T(8,128)(2,1)}) custom-call(s32[4]{0:T(128)} %multiply_add_fusion.place_ref, bf16[136,1024]{1,0:T(8,128)(2,1)} %copy-done.5, bf16[136,1152]{1,0:T(8,128)(2,1)} %get-tuple-element.139.refs_1_.rows_ref, ...), custom_call_target="tpu_custom_call" | custom-call | flops 1258291200 | bytes 1183760 | tf_op jit(solution)/shard_map/pallas_call | solution.py:493
  227.9 6.8 %collective-permute-done.34 = f32[8,256]{1,0:T(8,128)S(1)} collective-permute-done((f32[8,256]{1,0:T(8,128)S(1)}, f32[8,256]{1,0:T(8,128)S(1)}, u32[]{:S(2)}, u32[]{:S(2)}) %collective-permute-start.34) | collective-permute-done | bytes 8224 | tf_op jit(solution)/shard_map/ppermute | solution.py:23
  234.7 3.7 %collective-permute-done.30 = f32[32,128]{1,0:T(8,128)S(1)} collective-permute-done((f32[32,128]{1,0:T(8,128)S(1)}, f32[32,128]{1,0:T(8,128)S(1)}, u32[]{:S(2)}, u32[]{:S(2)}) %collective-permute-start.30) | collective-permute-done | bytes 16416 | tf_op jit(solution)/shard_map/ppermute | solution.py:48
  239.2 4.3 %collective-permute-start.23 = (bf16[128,1152]{1,0:T(8,128)(2,1)}, bf16[128,1152]{1,0:T(8,128)(2,1)S(1)}, u32[]{:S(2)}, u32[]{:S(2)}) collective-permute-start(bf16[128,1152]{1,0:T(8,128)(2,1)} %get-tuple-element.142), channel_id=1, source_target_pairs={{0,16},{4,20},{8,24},{12,28},{16,0},{20,4},{24,8},{28,12},{1,17},{... | collective-permute-start | bytes 884744 | tf_op jit(solution)/shard_map/ppermute | solution.py:66
  243.5 2.0 collective-permute-start.24
  245.5 2.4 collective-permute-start.33
  248.0 20.3 %collective-permute-done.32 = f32[32,128]{1,0:T(8,128)S(1)} collective-permute-done((f32[32,128]{1,0:T(8,128)S(1)}, f32[32,128]{1,0:T(8,128)S(1)}, u32[]{:S(2)}, u32[]{:S(2)}) %collective-permute-start.32) | collective-permute-done | bytes 16416 | tf_op jit(solution)/shard_map/ppermute | solution.py:66
  (196 shorter events, 56.9 us)
Async XLA Ops:
  1.5 9.0 %collective-permute-start = (bf16[8,256]{1,0:T(8,128)(2,1)S(1)}, bf16[8,256]{1,0:T(8,128)(2,1)S(1)}, u32[]{:S(2)}, u32[]{:S(2)}) collective-permute-start(bf16[8,256]{1,0:T(8,128)(2,1)S(1)} %slice.74), channel_id=1, source_target_pairs={{0,4},{4,8},{8,12},{12,16},{16,20},{20,24},{24,28},{1,5},{5,9},{9,... | collective-permute-start | bytes 12296 | tf_op jit(solution)/shard_map/ppermute | solution.py:23
  20.3 98.0 %copy-start.17 = (f32[1,1024]{1,0:T(1,128)}, f32[1,1024]{1,0:T(1,128)S(1)}, u32[]{:S(2)}) copy-start(f32[1,1024]{1,0:T(1,128)S(1)} %slice_convert_fusion.1.gain_ref) | copy-start | bytes 12292
  20.6 184.4 %copy-start.5 = (bf16[136,1024]{1,0:T(8,128)(2,1)}, bf16[136,1024]{1,0:T(8,128)(2,1)S(1)}, u32[]{:S(2)}) copy-start(bf16[136,1024]{1,0:T(8,128)(2,1)S(1)} %multiply_convert_fusion.refs_0_) | copy-start | bytes 835588
  22.8 31.5 %collective-permute-start.3 = (bf16[256,1024]{1,0:T(8,128)(2,1)S(1)}, bf16[256,1024]{1,0:T(8,128)(2,1)}, u32[]{:S(2)}, u32[]{:S(2)}) collective-permute-start(bf16[256,1024]{1,0:T(8,128)(2,1)S(1)} %copy-done.24), channel_id=1, source_target_pairs={{0,1},{1,2},{2,3},{3,0},{4,5},{5,6},{6,7},{7,4},{8,9},{9,10},{10,1... | collective-permute-start | bytes 1572872 | tf_op jit(solution)/shard_map/ppermute | solution.py:36
  23.2 31.1 %collective-permute-start.4 = (bf16[256,1024]{1,0:T(8,128)(2,1)S(1)}, bf16[256,1024]{1,0:T(8,128)(2,1)}, u32[]{:S(2)}, u32[]{:S(2)}) collective-permute-start(bf16[256,1024]{1,0:T(8,128)(2,1)S(1)} %copy-done.24), channel_id=1, source_target_pairs={{0,2},{1,3},{2,0},{3,1},{4,6},{5,7},{6,4},{7,5},{8,10},{9,11},{10,... | collective-permute-start | bytes 1572872 | tf_op jit(solution)/shard_map/ppermute | solution.py:36
  24.0 30.3 %collective-permute-start.5 = (bf16[256,1024]{1,0:T(8,128)(2,1)S(1)}, bf16[256,1024]{1,0:T(8,128)(2,1)}, u32[]{:S(2)}, u32[]{:S(2)}) collective-permute-start(bf16[256,1024]{1,0:T(8,128)(2,1)S(1)} %copy-done.24), channel_id=1, source_target_pairs={{0,3},{1,0},{2,1},{3,2},{4,7},{5,4},{6,5},{7,6},{8,11},{9,8},{10,9... | collective-permute-start | bytes 1572872 | tf_op jit(solution)/shard_map/ppermute | solution.py:36
  32.5 9.1 %collective-permute-start.1 = (f32[2,2,128,128]{3,2,1,0:T(8,128)}, f32[2,2,128,128]{3,2,1,0:T(8,128)S(1)}, u32[]{:S(2)}, u32[]{:S(2)}) collective-permute-start(f32[2,2,128,128]{3,2,1,0:T(8,128)} %get-tuple-element.102.late_ref), channel_id=1, source_target_pairs={{0,4},{4,8},{8,12},{12,16},{16,20},{20,24},{24,28},{1,5},{5,9},{9,... | collective-permute-start | bytes 786440 | tf_op jit(solution)/shard_map/ppermute | solution.py:23
  44.3 10.0 %collective-permute-start.2 = (f32[2,2,128,128]{3,2,1,0:T(8,128)}, f32[2,2,128,128]{3,2,1,0:T(8,128)S(1)}, u32[]{:S(2)}, u32[]{:S(2)}) collective-permute-start(f32[2,2,128,128]{3,2,1,0:T(8,128)} %get-tuple-element.105.late_ref), channel_id=1, source_target_pairs={{0,8},{4,12},{8,16},{12,20},{16,24},{20,28},{1,9},{5,13},{9,17},{1... | collective-permute-start | bytes 786440 | tf_op jit(solution)/shard_map/ppermute | solution.py:23
  57.0 12.5 %collective-permute-start.7 = (f32[2,2,128,128]{3,2,1,0:T(8,128)}, f32[2,2,128,128]{3,2,1,0:T(8,128)S(1)}, u32[]{:S(2)}, u32[]{:S(2)}) collective-permute-start(f32[2,2,128,128]{3,2,1,0:T(8,128)} %get-tuple-element.109), channel_id=1, source_target_pairs={{0,4},{4,8},{8,12},{12,16},{16,20},{20,24},{24,28},{1,5},{5,9},{9,... | collective-permute-start | bytes 786440 | tf_op jit(solution)/shard_map/ppermute | solution.py:23
  59.6 10.0 %collective-permute-start.6 = (f32[2,128,128]{2,1,0:T(8,128)}, f32[2,128,128]{2,1,0:T(8,128)S(1)}, u32[]{:S(2)}, u32[]{:S(2)}) collective-permute-start(f32[2,128,128]{2,1,0:T(8,128)} %get-tuple-element.108), channel_id=1, source_target_pairs={{0,20},{4,24},{8,28},{1,21},{5,25},{9,29},{2,22},{6,26},{10,30},{3... | collective-permute-start | bytes 393224 | tf_op jit(solution)/shard_map/ppermute | solution.py:23
  75.5 4.0 %collective-permute-start.8 = (bf16[128,256]{1,0:T(8,128)(2,1)}, bf16[128,256]{1,0:T(8,128)(2,1)S(1)}, u32[]{:S(2)}, u32[]{:S(2)}) collective-permute-start(bf16[128,256]{1,0:T(8,128)(2,1)} %get-tuple-element.110.refs_0_.refs_1_), channel_id=1, source_target_pairs={{0,1},{1,2},{2,3},{3,0},{4,5},{5,6},{6,7},{7,4},{8,9},{9,10},{10,1... | collective-permute-start | bytes 196616 | tf_op jit(solution)/shard_map/ppermute | solution.py:36
  75.5 5.2 %collective-permute-start.9 = (bf16[128,256]{1,0:T(8,128)(2,1)}, bf16[128,256]{1,0:T(8,128)(2,1)S(1)}, u32[]{:S(2)}, u32[]{:S(2)}) collective-permute-start(bf16[128,256]{1,0:T(8,128)(2,1)} %get-tuple-element.110.refs_0_.refs_1_), channel_id=1, source_target_pairs={{0,2},{1,3},{2,0},{3,1},{4,6},{5,7},{6,4},{7,5},{8,10},{9,11},{10,... | collective-permute-start | bytes 196616 | tf_op jit(solution)/shard_map/ppermute | solution.py:36
  76.3 4.4 %collective-permute-start.10 = (bf16[128,256]{1,0:T(8,128)(2,1)}, bf16[128,256]{1,0:T(8,128)(2,1)S(1)}, u32[]{:S(2)}, u32[]{:S(2)}) collective-permute-start(bf16[128,256]{1,0:T(8,128)(2,1)} %get-tuple-element.110.refs_0_.refs_1_), channel_id=1, source_target_pairs={{0,3},{1,0},{2,1},{3,2},{4,7},{5,4},{6,5},{7,6},{8,11},{9,8},{10,9... | collective-permute-start | bytes 196616 | tf_op jit(solution)/shard_map/ppermute | solution.py:36
  88.6 7.7 %collective-permute-start.11 = (bf16[128,1024]{1,0:T(8,128)(2,1)}, bf16[128,1024]{1,0:T(8,128)(2,1)S(1)}, u32[]{:S(2)}, u32[]{:S(2)}) collective-permute-start(bf16[128,1024]{1,0:T(8,128)(2,1)} %get-tuple-element.118), channel_id=1, source_target_pairs={{0,1},{1,2},{2,3},{3,0},{4,5},{5,6},{6,7},{7,4},{8,9},{9,10},{10,1... | collective-permute-start | bytes 786440 | tf_op jit(solution)/shard_map/ppermute | solution.py:36
  89.3 9.4 %collective-permute-start.12 = (bf16[128,1024]{1,0:T(8,128)(2,1)}, bf16[128,1024]{1,0:T(8,128)(2,1)S(1)}, u32[]{:S(2)}, u32[]{:S(2)}) collective-permute-start(bf16[128,1024]{1,0:T(8,128)(2,1)} %get-tuple-element.118), channel_id=1, source_target_pairs={{0,2},{1,3},{2,0},{3,1},{4,6},{5,7},{6,4},{7,5},{8,10},{9,11},{10,... | collective-permute-start | bytes 786440 | tf_op jit(solution)/shard_map/ppermute | solution.py:36
  90.1 12.6 %collective-permute-start.13 = (bf16[128,1024]{1,0:T(8,128)(2,1)}, bf16[128,1024]{1,0:T(8,128)(2,1)S(1)}, u32[]{:S(2)}, u32[]{:S(2)}) collective-permute-start(bf16[128,1024]{1,0:T(8,128)(2,1)} %get-tuple-element.118), channel_id=1, source_target_pairs={{0,3},{1,0},{2,1},{3,2},{4,7},{5,4},{6,5},{7,6},{8,11},{9,8},{10,9... | collective-permute-start | bytes 786440 | tf_op jit(solution)/shard_map/ppermute | solution.py:36
  91.9 39.8 %all-to-all-start.1 = ((bf16[4,128,256]{2,1,0:T(8,128)(2,1)}), bf16[4,128,256]{2,1,0:T(8,128)(2,1)S(1)}, u32[]{:S(2)}, u32[]{:S(2)}) async-start(bf16[4,128,256]{2,1,0:T(8,128)(2,1)} %get-tuple-element.155), calls=%async_computation.1 | async-start | bytes 524288 | tf_op jit(solution)/shard_map/all_to_all | solution.py:670
  107.8 65.8 %copy-start.31 = (bf16[128,512]{1,0:T(8,128)(2,1)S(1)}, bf16[128,512]{1,0:T(8,128)(2,1)}, u32[]{:S(2)}) copy-start(bf16[128,512]{1,0:T(8,128)(2,1)} %get-tuple-element.158) | copy-start | bytes 393220
  107.8 6.8 %collective-permute-start.14 = (bf16[2,128,128]{2,1,0:T(8,128)(2,1)}, bf16[2,128,128]{2,1,0:T(8,128)(2,1)S(1)}, u32[]{:S(2)}, u32[]{:S(2)}) collective-permute-start(bf16[2,128,128]{2,1,0:T(8,128)(2,1)} %get-tuple-element.119), channel_id=1, source_target_pairs={{4,0},{8,4},{12,8},{16,12},{20,16},{24,20},{28,24},{5,1},{9,5},{13... | collective-permute-start | bytes 196616 | tf_op jit(solution)/shard_map/ppermute | solution.py:23
  111.0 12.6 %collective-permute-start.16 = (bf16[2,128,128]{2,1,0:T(8,128)(2,1)S(1)}, bf16[2,128,128]{2,1,0:T(8,128)(2,1)S(1)}, u32[]{:S(2)}, u32[]{:S(2)}) collective-permute-start(bf16[2,128,128]{2,1,0:T(8,128)(2,1)S(1)} %copy-done.37), channel_id=1, source_target_pairs={{4,0},{8,4},{12,8},{16,12},{20,16},{24,20},{28,24},{5,1},{9,5},{13... | collective-permute-start | bytes 196616 | tf_op jit(solution)/shard_map/ppermute | solution.py:23
  117.0 11.0 %collective-permute-start.15 = (bf16[2,128,128]{2,1,0:T(8,128)(2,1)}, bf16[2,128,128]{2,1,0:T(8,128)(2,1)S(1)}, u32[]{:S(2)}, u32[]{:S(2)}) collective-permute-start(bf16[2,128,128]{2,1,0:T(8,128)(2,1)} %get-tuple-element.122), channel_id=1, source_target_pairs={{8,0},{12,4},{16,8},{20,12},{24,16},{28,20},{9,1},{13,5},{17,9},{2... | collective-permute-start | bytes 196616 | tf_op jit(solution)/shard_map/ppermute | solution.py:23
  118.3 34.8 %collective-permute-start.18 = (bf16[2,128,128]{2,1,0:T(8,128)(2,1)S(1)}, bf16[2,128,128]{2,1,0:T(8,128)(2,1)S(1)}, u32[]{:S(2)}, u32[]{:S(2)}) collective-permute-start(bf16[2,128,128]{2,1,0:T(8,128)(2,1)S(1)} %copy-done.36), channel_id=1, source_target_pairs={{16,0},{20,4},{24,8},{28,12},{17,1},{21,5},{25,9},{29,13},{18,2},{... | collective-permute-start | bytes 196616 | tf_op jit(solution)/shard_map/ppermute | solution.py:23
  119.6 33.5 %collective-permute-start.26 = (bf16[128,256]{1,0:T(8,128)(2,1)S(1)}, bf16[128,256]{1,0:T(8,128)(2,1)S(1)}, u32[]{:S(2)}, u32[]{:S(2)}) collective-permute-start(bf16[128,256]{1,0:T(8,128)(2,1)S(1)} %copy-done.35), channel_id=1, source_target_pairs={{0,4},{4,0},{8,12},{12,8},{16,20},{20,16},{24,28},{28,24},{1,5},{5... | collective-permute-start | bytes 196616 | tf_op jit(solution)/shard_map/ppermute | solution.py:36
  121.0 88.5 %collective-permute-start.36 = (bf16[2112,128]{1,0:T(8,128)(2,1)S(1)}, bf16[2112,128]{1,0:T(8,128)(2,1)S(1)}, u32[]{:S(2)}, u32[]{:S(2)}) collective-permute-start(bf16[2112,128]{1,0:T(8,128)(2,1)S(1)} %copy-done.22), channel_id=1, source_target_pairs={{0,8},{4,12},{8,16},{12,20},{16,24},{20,28},{24,0},{28,4},{1,9},{5... | collective-permute-start | bytes 1622024 | tf_op jit(solution)/shard_map/ppermute | solution.py:66
  123.6 89.1 %collective-permute-start.38 = (bf16[2112,128]{1,0:T(8,128)(2,1)S(1)}, bf16[2112,128]{1,0:T(8,128)(2,1)}, u32[]{:S(2)}, u32[]{:S(2)}) collective-permute-start(bf16[2112,128]{1,0:T(8,128)(2,1)S(1)} %copy-done.22), channel_id=1, source_target_pairs={{0,16},{4,20},{8,24},{12,28},{16,0},{20,4},{24,8},{28,12},{1,17},{... | collective-permute-start | bytes 1622024 | tf_op jit(solution)/shard_map/ppermute | solution.py:66
  130.4 36.8 %collective-permute-start.17 = (bf16[2,128,128]{2,1,0:T(8,128)(2,1)}, bf16[2,128,128]{2,1,0:T(8,128)(2,1)S(1)}, u32[]{:S(2)}, u32[]{:S(2)}) collective-permute-start(bf16[2,128,128]{2,1,0:T(8,128)(2,1)} %get-tuple-element.125), channel_id=1, source_target_pairs={{20,0},{24,4},{28,8},{21,1},{25,5},{29,9},{22,2},{26,6},{30,10},{2... | collective-permute-start | bytes 196616 | tf_op jit(solution)/shard_map/ppermute | solution.py:23
  153.2 60.1 %collective-permute-start.40 = (bf16[2112,128]{1,0:T(8,128)(2,1)S(1)}, bf16[2112,128]{1,0:T(8,128)(2,1)}, u32[]{:S(2)}, u32[]{:S(2)}) collective-permute-start(bf16[2112,128]{1,0:T(8,128)(2,1)S(1)} %copy-done.22), channel_id=1, source_target_pairs={{0,24},{4,28},{8,0},{12,4},{16,8},{20,12},{24,16},{28,20},{1,25},{... | collective-permute-start | bytes 1622024 | tf_op jit(solution)/shard_map/ppermute | solution.py:66
  153.2 44.8 %collective-permute-start.25 = (bf16[128,1024]{1,0:T(8,128)(2,1)}, bf16[128,1024]{1,0:T(8,128)(2,1)S(1)}, u32[]{:S(2)}, u32[]{:S(2)}) collective-permute-start(bf16[128,1024]{1,0:T(8,128)(2,1)} %get-tuple-element.144.refs_0_), channel_id=1, source_target_pairs={{0,4},{4,0},{8,12},{12,8},{16,20},{20,16},{24,28},{28,24},{1,5},{5... | collective-permute-start | bytes 786440 | tf_op jit(solution)/shard_map/ppermute | solution.py:36
  167.2 6.4 %collective-permute-start.19 = (bf16[2,128,128]{2,1,0:T(8,128)(2,1)}, bf16[2,128,128]{2,1,0:T(8,128)(2,1)S(1)}, u32[]{:S(2)}, u32[]{:S(2)}) collective-permute-start(bf16[2,128,128]{2,1,0:T(8,128)(2,1)} %get-tuple-element.125), channel_id=1, source_target_pairs={{4,0},{8,4},{12,8},{16,12},{20,16},{24,20},{28,24},{5,1},{9,5},{13... | collective-permute-start | bytes 196616 | tf_op jit(solution)/shard_map/ppermute | solution.py:23
  173.6 17.5 %collective-permute-start.35 = (bf16[128,512]{1,0:T(8,128)(2,1)S(1)}, bf16[128,512]{1,0:T(8,128)(2,1)S(1)}, u32[]{:S(2)}, u32[]{:S(2)}) collective-permute-start(bf16[128,512]{1,0:T(8,128)(2,1)S(1)} %copy-done.31), channel_id=1, source_target_pairs={{0,8},{4,12},{8,16},{12,20},{16,24},{20,28},{24,0},{28,4},{1,9},{5... | collective-permute-start | bytes 393224 | tf_op jit(solution)/shard_map/ppermute | solution.py:66
  187.6 31.6 %all-to-all-start = ((bf16[4,136,384]{2,1,0:T(8,128)(2,1)}), bf16[4,136,384]{2,1,0:T(8,128)(2,1)S(1)}, u32[]{:S(2)}, u32[]{:S(2)}) async-start(bf16[4,136,384]{2,1,0:T(8,128)(2,1)} %shard_map.260), calls=%async_computation | async-start | bytes 835584 | tf_op jit(solution)/shard_map/all_to_all | solution.py:744
  191.1 13.9 %collective-permute-start.37 = (bf16[128,512]{1,0:T(8,128)(2,1)S(1)}, bf16[128,512]{1,0:T(8,128)(2,1)S(1)}, u32[]{:S(2)}, u32[]{:S(2)}) collective-permute-start(bf16[128,512]{1,0:T(8,128)(2,1)S(1)} %copy-done.30), channel_id=1, source_target_pairs={{0,16},{4,20},{8,24},{12,28},{16,0},{20,4},{24,8},{28,12},{1,17},{... | collective-permute-start | bytes 393224 | tf_op jit(solution)/shard_map/ppermute | solution.py:66
  198.0 11.4 %collective-permute-start.39 = (bf16[128,512]{1,0:T(8,128)(2,1)S(1)}, bf16[128,512]{1,0:T(8,128)(2,1)S(1)}, u32[]{:S(2)}, u32[]{:S(2)}) collective-permute-start(bf16[128,512]{1,0:T(8,128)(2,1)S(1)} %copy-done.29), channel_id=1, source_target_pairs={{0,24},{4,28},{8,0},{12,4},{16,8},{20,12},{24,16},{28,20},{1,25},{... | collective-permute-start | bytes 393224 | tf_op jit(solution)/shard_map/ppermute | solution.py:66
  205.0 16.4 %collective-permute-start.20 = (bf16[136,1024]{1,0:T(8,128)(2,1)S(1)}, bf16[136,1024]{1,0:T(8,128)(2,1)}, u32[]{:S(2)}, u32[]{:S(2)}) collective-permute-start(bf16[136,1024]{1,0:T(8,128)(2,1)S(1)} %multiply_convert_fusion.refs_0_), channel_id=1, source_target_pairs={{0,4},{4,0},{8,12},{12,8},{16,20},{20,16},{24,28},{28,24},{1,5},{5... | collective-permute-start | bytes 835592 | tf_op jit(solution)/shard_map/ppermute | solution.py:36
  209.4 14.3 %collective-permute-start.21 = (bf16[136,1152]{1,0:T(8,128)(2,1)S(1)}, bf16[136,1152]{1,0:T(8,128)(2,1)}, u32[]{:S(2)}, u32[]{:S(2)}) collective-permute-start(bf16[136,1152]{1,0:T(8,128)(2,1)S(1)} %copy-done.3), channel_id=1, source_target_pairs={{0,4},{4,0},{8,12},{12,8},{16,20},{20,16},{24,28},{28,24},{1,5},{5... | collective-permute-start | bytes 940040 | tf_op jit(solution)/shard_map/ppermute | solution.py:36
  209.5 29.7 %collective-permute-start.27 = (bf16[256,128]{1,0:T(8,128)(2,1)}, bf16[256,128]{1,0:T(8,128)(2,1)S(1)}, u32[]{:S(2)}, u32[]{:S(2)}) collective-permute-start(bf16[256,128]{1,0:T(8,128)(2,1)} %get-tuple-element.146), channel_id=1, source_target_pairs={{0,8},{4,12},{8,16},{12,20},{16,24},{20,28},{24,0},{28,4},{1,9},{5... | collective-permute-start | bytes 196616 | tf_op jit(solution)/shard_map/ppermute | solution.py:66
  212.7 26.5 %collective-permute-start.28 = (bf16[256,128]{1,0:T(8,128)(2,1)}, bf16[256,128]{1,0:T(8,128)(2,1)S(1)}, u32[]{:S(2)}, u32[]{:S(2)}) collective-permute-start(bf16[256,128]{1,0:T(8,128)(2,1)} %get-tuple-element.147), channel_id=1, source_target_pairs={{0,16},{4,20},{8,24},{12,28},{16,0},{20,4},{24,8},{28,12},{1,17},{... | collective-permute-start | bytes 196616 | tf_op jit(solution)/shard_map/ppermute | solution.py:66
  217.4 28.2 %collective-permute-start.41 = (bf16[2112,128]{1,0:T(8,128)(2,1)}, bf16[2112,128]{1,0:T(8,128)(2,1)S(1)}, u32[]{:S(2)}, u32[]{:S(2)}) collective-permute-start(bf16[2112,128]{1,0:T(8,128)(2,1)} %get-tuple-element.162), channel_id=1, source_target_pairs={{0,4},{4,0},{8,12},{12,8},{16,20},{20,16},{24,28},{28,24},{1,5},{5... | collective-permute-start | bytes 1622024 | tf_op jit(solution)/shard_map/ppermute | solution.py:36
  221.5 22.1 %collective-permute-start.29 = (bf16[256,128]{1,0:T(8,128)(2,1)S(1)}, bf16[256,128]{1,0:T(8,128)(2,1)S(1)}, u32[]{:S(2)}, u32[]{:S(2)}) collective-permute-start(bf16[256,128]{1,0:T(8,128)(2,1)S(1)} %copy-done.38), channel_id=1, source_target_pairs={{0,24},{4,28},{8,0},{12,4},{16,8},{20,12},{24,16},{28,20},{1,25},{... | collective-permute-start | bytes 196616 | tf_op jit(solution)/shard_map/ppermute | solution.py:66
  223.7 11.0 %collective-permute-start.34 = (f32[8,256]{1,0:T(8,128)S(1)}, f32[8,256]{1,0:T(8,128)S(1)}, u32[]{:S(2)}, u32[]{:S(2)}) collective-permute-start(f32[8,256]{1,0:T(8,128)S(1)} %slice.103), channel_id=1, source_target_pairs={{4,0},{8,4},{12,8},{16,12},{20,16},{24,20},{28,24},{5,1},{9,5},{13... | collective-permute-start | bytes 24584 | tf_op jit(solution)/shard_map/ppermute | solution.py:23
  227.9 40.5 %copy-start.4 = (bf16[128,1152]{1,0:T(8,128)(2,1)S(1)}, bf16[128,1152]{1,0:T(8,128)(2,1)}, u32[]{:S(2)}) copy-start(bf16[128,1152]{1,0:T(8,128)(2,1)} %get-tuple-element.169) | copy-start | bytes 884740
  234.7 3.7 %collective-permute-start.30 = (f32[32,128]{1,0:T(8,128)S(1)}, f32[32,128]{1,0:T(8,128)S(1)}, u32[]{:S(2)}, u32[]{:S(2)}) collective-permute-start(f32[32,128]{1,0:T(8,128)S(1)} %concatenate.14), channel_id=1, source_target_pairs={{0,4},{4,0},{8,12},{12,8},{16,20},{20,16},{24,28},{28,24},{1,5},{5... | collective-permute-start | bytes 49160 | tf_op jit(solution)/shard_map/ppermute | solution.py:48
  238.5 7.1 %collective-permute-start.31 = (f32[32,128]{1,0:T(8,128)S(1)}, f32[32,128]{1,0:T(8,128)S(1)}, u32[]{:S(2)}, u32[]{:S(2)}) collective-permute-start(f32[32,128]{1,0:T(8,128)S(1)} %add.155), channel_id=1, source_target_pairs={{0,8},{4,12},{8,16},{12,20},{16,24},{20,28},{24,0},{28,4},{1,9},{5... | collective-permute-start | bytes 49160 | tf_op jit(solution)/shard_map/ppermute | solution.py:66
  239.2 29.2 %collective-permute-start.22 = (bf16[128,1152]{1,0:T(8,128)(2,1)}, bf16[128,1152]{1,0:T(8,128)(2,1)S(1)}, u32[]{:S(2)}, u32[]{:S(2)}) collective-permute-start(bf16[128,1152]{1,0:T(8,128)(2,1)} %get-tuple-element.141), channel_id=1, source_target_pairs={{0,8},{4,12},{8,16},{12,20},{16,24},{20,28},{24,0},{28,4},{1,9},{5... | collective-permute-start | bytes 884744 | tf_op jit(solution)/shard_map/ppermute | solution.py:66
  239.2 29.1 %collective-permute-start.23 = (bf16[128,1152]{1,0:T(8,128)(2,1)}, bf16[128,1152]{1,0:T(8,128)(2,1)S(1)}, u32[]{:S(2)}, u32[]{:S(2)}) collective-permute-start(bf16[128,1152]{1,0:T(8,128)(2,1)} %get-tuple-element.142), channel_id=1, source_target_pairs={{0,16},{4,20},{8,24},{12,28},{16,0},{20,4},{24,8},{28,12},{1,17},{... | collective-permute-start | bytes 884744 | tf_op jit(solution)/shard_map/ppermute | solution.py:66
  243.5 24.9 %collective-permute-start.24 = (bf16[128,1152]{1,0:T(8,128)(2,1)}, bf16[128,1152]{1,0:T(8,128)(2,1)S(1)}, u32[]{:S(2)}, u32[]{:S(2)}) collective-permute-start(bf16[128,1152]{1,0:T(8,128)(2,1)} %get-tuple-element.143), channel_id=1, source_target_pairs={{0,24},{4,28},{8,0},{12,4},{16,8},{20,12},{24,16},{28,20},{1,25},{... | collective-permute-start | bytes 884744 | tf_op jit(solution)/shard_map/ppermute | solution.py:66
  245.5 22.8 %collective-permute-start.32 = (f32[32,128]{1,0:T(8,128)S(1)}, f32[32,128]{1,0:T(8,128)S(1)}, u32[]{:S(2)}, u32[]{:S(2)}) collective-permute-start(f32[32,128]{1,0:T(8,128)S(1)} %add.155), channel_id=1, source_target_pairs={{0,16},{4,20},{8,24},{12,28},{16,0},{20,4},{24,8},{28,12},{1,17},{... | collective-permute-start | bytes 49160 | tf_op jit(solution)/shard_map/ppermute | solution.py:66
  245.5 22.8 %collective-permute-start.33 = (f32[32,128]{1,0:T(8,128)S(1)}, f32[32,128]{1,0:T(8,128)S(1)}, u32[]{:S(2)}, u32[]{:S(2)}) collective-permute-start(f32[32,128]{1,0:T(8,128)S(1)} %add.155), channel_id=1, source_target_pairs={{0,24},{4,28},{8,0},{12,4},{16,8},{20,12},{24,16},{28,20},{1,25},{... | collective-permute-start | bytes 49160 | tf_op jit(solution)/shard_map/ppermute | solution.py:66
  (39 other events, 299.7 us)
